TPU v7x, 128 devices: a whole 4x4x4 slice. The times are simulated.
128 devices in a mesh: col: 8 (over x, z_lo), row: 16 (over y, z_hi, core).
Axes of the slice: x: 4, y: 4, z: 4 (z_hi: 2, z_lo: 2; z = z_hi * 2 + z_lo), core: 2. Of those that a mesh axis runs over, the one named last changes fastest.
Arguments:
- covariance: float32 [12288, 12288], P('row', 'col'), may hold values from -2 to 2, as said below
- wfs_map: int32 [12288], P('row'), may hold values from 0 to 5
- noise_var: float32 [6], replicated, may hold values from 0.5 to 2
- targets: float32 [12288, 2048], P('row', 'col'), may hold values from -0.6 to 0.6
- target_pos: float32 [2, 2048], replicated, may hold values from -1 to 1
- layer_strength: float32 [35], replicated, may hold values from 0.005 to 0.05
- layer_scale: float32 [35], replicated, may hold values from 0.2 to 2
- tile_layer: int32 [16], replicated, may hold values from 0 to 34
Outputs:
- updated: float32 [12288, 12288], P('row', 'col')
- panel_factor: float32 [12288, 256], P('row')
- reconstructor: float32 [12288, 2048], P('row', 'col')
- error_cov: float32 [2048, 2048], P('row', 'col')
Inputs may be any that keep to these rules, and one draw needn't show every extreme that they name: `covariance`: symmetric and positive semidefinite; its diagonal lies between 0.5 and 2.
All inputs are finite; a program needn't handle non-finite values.
Results may differ from a plain program's by a relative error of at most 0.0003.
Values sent between devices are 32-bit elements; how exact they have to be, the bound alone decides.
No kernel may reach another device: no remote copies, remote signals or barrier semaphores. Data moves between devices by JAX's collectives and lax.ppermute only.
A program may use at most 64 MiB of HBM per device.

v0:
```python
import jax
import jax.numpy as jnp
from jax import lax
from jax.sharding import PartitionSpec as P

PB = 256
TILE = 128


precise = lax.Precision.HIGHEST


def broadcast(shard, axis, root):
    mine = lax.axis_index(axis) == root
    return lax.psum(jnp.where(mine, shard, jnp.zeros_like(shard)), axis)


def lookup(values, indices, entries):
    one_hot = (indices[:, None] == jnp.arange(entries, dtype=jnp.int32)[None, :]).astype(
        jnp.float32
    )
    return jnp.dot(one_hot, values, precision=precise)


def target_covariance(pos_rows, pos_cols, layer_rows, layer_cols, layer_strength, layer_scale):
    distance = (pos_rows[0][:, None] - pos_cols[0][None, :]) ** 2 + (
        pos_rows[1][:, None] - pos_cols[1][None, :]
    ) ** 2
    lowest = jnp.minimum(layer_rows[:, None], layer_cols[None, :])
    levels = jnp.arange(layer_strength.shape[0], dtype=jnp.int32)
    weights = layer_strength[:, None, None] / (
        1.0 + distance[None] / (layer_scale * layer_scale)[:, None, None]
    )
    return jnp.sum(jnp.where(levels[:, None, None] <= lowest[None], weights, 0.0), axis=0)


def local(
    covariance, wfs_map, noise_var, targets, target_pos, layer_strength, layer_scale, tile_layer
):
    row_count, col_count = covariance.shape
    target_width = targets.shape[1]
    row_index = lax.axis_index("row")
    col_index = lax.axis_index("col")
    row_ids = row_index * row_count + jnp.arange(row_count, dtype=jnp.int32)
    col_ids = col_index * col_count + jnp.arange(col_count, dtype=jnp.int32)
    noise_rows = lookup(noise_var, wfs_map, noise_var.shape[0])
    on_diagonal = row_ids[:, None] == col_ids[None, :]
    matrix = covariance + jnp.where(on_diagonal, noise_rows[:, None], 0.0)
    diag_block = broadcast(matrix[:PB, :PB], ("col", "row"), 0)
    factor = jnp.linalg.cholesky(diag_block)
    solved = jax.scipy.linalg.solve_triangular(factor, matrix[:, :PB].T, lower=True).T
    top_rows = jnp.concatenate([factor, jnp.zeros((row_count - PB, PB), jnp.float32)], axis=0)
    own_rows = jnp.where(row_ids[:, None] < PB, top_rows, solved)
    panel_rows = broadcast(own_rows, "col", 0)
    head_rows = jax.scipy.linalg.solve_triangular(factor, targets[:PB], lower=True)
    upper_rows = jax.scipy.linalg.solve_triangular(factor, matrix[:PB, :], lower=True)
    lead_cols = jnp.concatenate([factor.T, jnp.zeros((PB, col_count - PB), jnp.float32)], axis=1)
    upper_rows = jnp.where(col_ids[None, :] < PB, lead_cols, upper_rows)
    upper_rows, head_cols = (broadcast(upper_rows, "row", 0), broadcast(head_rows, "row", 0))
    product = jnp.dot(panel_rows, upper_rows, precision=precise)
    fill_cols = jnp.concatenate(
        [panel_rows, jnp.zeros((row_count, col_count - PB), jnp.float32)], axis=1
    )
    trailing = (row_ids[:, None] >= PB) & (col_ids[None, :] >= PB)
    updated = jnp.where(
        trailing, matrix - product, jnp.where(col_ids[None, :] < PB, fill_cols, 0.0)
    )
    head_top = jnp.concatenate(
        [head_cols, jnp.zeros((row_count - PB, target_width), jnp.float32)], axis=0
    )
    reduced = targets - jnp.dot(panel_rows, head_cols, precision=precise)
    reconstructor = jnp.where(row_ids[:, None] < PB, head_top, reduced)
    error_rows = target_width * lax.axis_size("col") // lax.axis_size("row")
    row_start = row_index * error_rows
    gathered = lax.all_gather(head_cols, "col", axis=1, tiled=True)
    head_needed = lax.dynamic_slice_in_dim(gathered, row_start, error_rows, 1)
    layer_all = jnp.repeat(tile_layer, TILE)
    col_start = col_index * target_width
    pos_rows = lax.dynamic_slice_in_dim(target_pos, row_start, error_rows, 1)
    pos_cols = lax.dynamic_slice_in_dim(target_pos, col_start, target_width, 1)
    layer_rows = lax.dynamic_slice_in_dim(layer_all, row_start, error_rows, 0)
    layer_cols = lax.dynamic_slice_in_dim(layer_all, col_start, target_width, 0)
    target_cov = target_covariance(
        pos_rows, pos_cols, layer_rows, layer_cols, layer_strength, layer_scale
    )
    error_cov = target_cov - lax.dot_general(
        head_needed,
        head_cols,
        (((0,), (0,)), ((), ())),
        precision=precise,
        preferred_element_type=jnp.float32,
    )
    return (updated, panel_rows, reconstructor, error_cov)


def solution(mesh):
    placed = (P("row", "col"), P("row"), P(), P("row", "col"), P(), P(), P(), P())
    return jax.shard_map(
        local,
        mesh=mesh,
        in_specs=placed,
        out_specs=(P("row", "col"), P("row", None), P("row", "col"), P("row", "col")),
        check_vma=False,
    )
```

profile of v0, /device:TPU:1, one launch (start us, length us, event | category | flops | bytes accessed | tf_op | source)
XLA Modules:
  0.0 517.1 jit_solution(5108484847680421361)
XLA Ops:
  7.2 6.1 %copy.26 = f32[768,1536]{0,1:T(8,128)} copy(f32[768,1536]{1,0:T(8,128)} %param.8) | data formatting | bytes 9437184 | tf_op args[0]
  13.3 0.4 convolution_reduce_fusion
  13.8 2.9 select_add_fusion
  16.6 2.2 copy-done.1
  18.8 0.7 slice_select_fusion
  19.7 144.9 %all-reduce.10.cloned.1.call-done = f32[256,256]{0,1:T(8,128)} async-done(((f32[256,256]{0,1:T(8,128)}), f32[256,256]{0,1:T(8,128)}) %all-reduce.10.cloned.1.call-update) | async-done | bytes 262160 | tf_op jit(solution)/shard_map/psum | solution.py:15
  164.5 1.1 copy.27
  165.6 1.0 fusion.11
  166.6 11.7 %cholesky.49 = f32[128,128]{1,0:T(8,128)S(1)} custom-call(f32[128,128]{1,0:T(8,128)S(1)} %cholesky.115), custom_call_target="Cholesky" | custom-call | tf_op jit(solution)/shard_map/jit(cholesky)/cholesky | solution.py:50
  178.4 0.1 copy.28
  178.5 9.8 %custom-call.21 = f32[1,128,128]{1,2,0:T(8,128)S(1)} custom-call(f32[1,128,128]{2,1,0:T(8,128)S(1)} %get-tuple-element.43), custom_call_target="InvertDiagBlocksLowerTriangular" | custom-call | tf_op jit(solution)/shard_map/jit(cholesky)/cholesky | solution.py:50
  188.3 0.2 fusion.17
  188.6 0.3 convolution_subtract_fusion.5
  188.9 11.7 %cholesky.103 = f32[128,128]{1,0:T(8,128)S(1)} custom-call(f32[128,128]{1,0:T(8,128)S(1)} %convolution_subtract_fusion.5), custom_call_target="Cholesky" | custom-call | tf_op jit(solution)/shard_map/jit(cholesky)/cholesky | solution.py:50
  200.8 0.6 compare_reduce_fusion
  202.9 4.4 while.1
  203.0 0.6 fusion.47
  203.6 1.4 dynamic-slice.11
  205.1 0.6 fusion.47
  205.7 1.4 dynamic-slice.11
  207.2 19.7 %custom-call.22 = f32[2,128,128]{1,2,0:T(8,128)S(1)} custom-call(f32[2,128,128]{2,1,0:T(8,128)S(1)} %get-tuple-element.11), custom_call_target="InvertDiagBlocksLowerTriangular" | custom-call | tf_op jit(solution)/shard_map/jit(_solve_triangular)/triangular_solve | solution.py:51
  226.9 2.0 fusion.5
  228.9 1.2 fusion.15
  230.1 1.2 convolution_subtract_fusion.4
  231.5 2.5 convolution_subtract_fusion
  234.0 0.9 fusion.21
  234.9 0.4 fusion.20
  235.3 0.7 maximum_select_fusion.1
  236.0 1.3 fusion.3
  237.5 1.2 slice_bitcast_fusion
  238.7 0.5 fusion.9
  239.2 0.5 convolution_subtract_fusion.2
  239.8 0.5 fusion.22
  240.3 1.0 fusion.8
  241.3 137.0 %all-reduce.14.cloned.1.call-done = (f32[256,1536]{1,0:T(8,128)}, f32[256,256]{0,1:T(8,128)}) async-done(((f32[256,1536]{1,0:T(8,128)}, f32[256,256]{0,1:T(8,128)}), (f32[256,1536]{1,0:T(8,128)}, f32[256,256]{0,1:T(8,128)})) %all-reduce.14.cloned.1.call-update) | async-done | bytes 1835024 | tf_op jit(solution)/shard_map/psum | solution.py:15
  378.4 0.3 copy.35
  378.9 0.7 constant_dynamic-slice_fusion.2
  379.6 0.8 constant_dynamic-slice_fusion.1
  380.5 0.1 multiply_add_fusion
  380.6 1.2 fusion.2
  381.8 71.5 %all-reduce.12.cloned.1.call-done = f32[768,256]{0,1:T(8,128)} async-done(((f32[768,256]{0,1:T(8,128)}), f32[768,256]{0,1:T(8,128)}) %all-reduce.12.cloned.1.call-update) | async-done | bytes 786448 | tf_op jit(solution)/shard_map/psum | solution.py:15
  453.3 2.3 copy.38
  455.6 9.2 %select_select_fusion = f32[768,1536]{0,1:T(8,128)} fusion(f32[768,256]{0,1:T(8,128)} %all-reduce.12.cloned.1.call-done, f32[768,1536]{0,1:T(8,128)} %copy-done.1, f32[256,1536]{1,0:T(8,128)S(1)} %copy-done.4, pred[1536]{0:T(1024)(128)(4,1)S(1)} %fusion.26, pred[768]{0:T(1024)(128)(4,1)S(1)} %fusion.29, pred[1536]{0:T(1024)(128)(4,1)S(1)} %fusion.27), kind=kOutput, calls=%fused_computation.2 | convolution fusion | flops 3628597248 | bytes 11800320 | tf_op jit(solution)/shard_map/dot_general | solution.py:60
  464.8 6.1 %copy.37 = f32[768,1536]{1,0:T(8,128)} copy(f32[768,1536]{0,1:T(8,128)} %select_select_fusion) | data formatting | bytes 9437184
  470.9 0.9 fusion.4
  471.8 1.1 copy.39
  473.0 35.7 %all-gather.2.cloned.1.call-done = f32[256,2048]{0,1:T(8,128)} async-done(((f32[256,256]{0,1:T(8,128)}), f32[256,2048]{0,1:T(8,128)}) %all-gather.2.cloned.1.call-update) | async-done | bytes 2097168 | tf_op jit(solution)/shard_map/all_gather | solution.py:75
  508.6 2.0 convolution_subtract_fusion.3
  (58 shorter events, 1.3 us)
Async XLA Ops:
  7.2 371.5 %copy-start = (s32[16]{0:T(128)S(1)}, s32[16]{0:T(128)}, u32[]{:S(2)}) copy-start(s32[16]{0:T(128)} %param.15) | copy-start | bytes 196
  7.2 157.4 %all-reduce.10.cloned.1.call-start = ((), (), s32[]{:S(2)}) async-start(), calls=%async_computation | async-start | bytes 524288 | tf_op jit(solution)/shard_map/psum | solution.py:15
  7.2 6.1 %copy-start.7 = (s32[768]{0:T(1024)S(1)}, s32[768]{0:T(1024)}, u32[]{:S(2)}) copy-start(s32[768]{0:T(1024)} %param.9) | copy-start | bytes 9220
  7.2 6.1 %copy-start.8 = (f32[6]{0:T(128)S(1)}, f32[6]{0:T(128)}, u32[]{:S(2)}) copy-start(f32[6]{0:T(128)} %param.10) | copy-start | bytes 76
  16.6 2.2 copy-start.1
  19.6 358.8 %all-reduce.14.cloned.1.call-start = ((), (), s32[]{:S(2)}) async-start(), calls=%async_computation.3 | async-start | bytes 3670016 | tf_op jit(solution)/shard_map/psum | solution.py:15
  237.4 141.0 %copy-start.5 = (f32[768,256]{1,0:T(8,128)S(1)}, f32[768,256]{1,0:T(8,128)}, u32[]{:S(2)}) copy-start(f32[768,256]{1,0:T(8,128)} %param.11) | copy-start | bytes 2359300
  237.4 141.3 %copy-start.9 = (f32[35]{0:T(128)S(1)}, f32[35]{0:T(128)}, u32[]{:S(2)}) copy-start(f32[35]{0:T(128)} %param.14) | copy-start | bytes 424
  237.4 215.9 %all-reduce.12.cloned.1.call-start = ((), (), s32[]{:S(2)}) async-start(), calls=%async_computation.1 | async-start | bytes 1572864 | tf_op jit(solution)/shard_map/psum | solution.py:15
  237.5 143.2 %copy-start.6 = (f32[35]{0:T(128)S(1)}, f32[35]{0:T(128)}, u32[]{:S(2)}) copy-start(f32[35]{0:T(128)} %param.13) | copy-start | bytes 424
  241.3 267.3 %all-gather.2.cloned.1.call-start = ((), (), s32[]{:S(2)}) async-start(), calls=%async_computation.2 | async-start | bytes 2359296 | tf_op jit(solution)/shard_map/all_gather | solution.py:75
  378.3 77.3 %copy-start.4 = (f32[256,1536]{1,0:T(8,128)S(1)}, f32[256,1536]{1,0:T(8,128)}, u32[]{:S(2)}) copy-start(f32[256,1536]{1,0:T(8,128)} %get-tuple-element.36) | copy-start | bytes 4718596
  464.7 6.2 %copy-start.2 = (f32[768,256]{0,1:T(8,128)S(1)}, f32[768,256]{0,1:T(8,128)}, u32[]{:S(2)}) copy-start(f32[768,256]{0,1:T(8,128)} %all-reduce.12.cloned.1.call-done) | copy-start | bytes 2359300
  464.8 6.2 %copy-start.3 = (f32[256,256]{0,1:T(8,128)S(1)}, f32[256,256]{0,1:T(8,128)}, u32[]{:S(2)}) copy-start(f32[256,256]{0,1:T(8,128)} %get-tuple-element.37) | copy-start | bytes 786436
Sparse Core Ops, SparseCore 0:
  19.7 144.8 all-reduce.9
  237.5 140.7 all-reduce.13
  381.6 71.6 all-reduce.11
  454.8 53.7 all-gather.1
where the time goes:
time: 519 us; the launch traced here: 517 us
  waiting for transfers between devices  389 us (75%)
  other arithmetic  62.7 us (12%)
  local copies, waits for them, and re-layouts  26.8 us (5%)
  matrix products  22.7 us (4%)
  between operations  15.5 us (3%)
    psum x3, waiting for transfers between devices, broadcast(): return lax.psum(jnp.where(mine, shard, jnp.zeros_like(shard)), axis)  353 us
    all_gather x1, waiting for transfers between devices, local(): gathered = lax.all_gather(head_cols, 'col', axis=1, tiled=True)  35.7 us
    another operation x6, other arithmetic, local(): factor = jnp.linalg.cholesky(diag_block)  33.9 us
    another operation x3, other arithmetic, local(): jax.scipy.linalg.solve_triangular(factor, matrix[:, :PB].T, lower=True)  19.7 us
    unnamed x25, local copies, waits for them, and re-layouts  18.1 us
  transfers between devices with their start and end apart: 4, of which 4 were waited for; matrix products, arithmetic and copies ran while one was open for 5% of the time, Pallas kernels for 0%

commit v1 on v0

v1 whole, which is shorter than its diff:
```python
import functools

import jax
import jax.numpy as jnp
from jax import lax
from jax.experimental import pallas as pl
from jax.experimental.pallas import tpu as pltpu
from jax.sharding import PartitionSpec as P

PB = 256
HB = 128
TILE = 128
BOTH = ("col", "row")
precise = lax.Precision.HIGHEST
F32 = jnp.float32


def mm(a, b, dims=((1,), (0,))):
    return lax.dot_general(a, b, (dims, ((), ())), precision=precise, preferred_element_type=F32)


def split(x):
    hi = x.astype(jnp.bfloat16)
    return hi, (x - hi.astype(F32)).astype(jnp.bfloat16)


def mm3(a, b, dims=((1,), (0,))):
    dot = lambda x, y: lax.dot_general(x, y, (dims, ((), ())), preferred_element_type=F32)
    return dot(a[0], b[0]) + (dot(a[0], b[1]) + dot(a[1], b[0]))


def inverse_factor(a_ref, w_ref):
    n = a_ref.shape[0]
    rows = lax.broadcasted_iota(jnp.int32, (n, n), 0)
    lanes = lax.broadcasted_iota(jnp.int32, (n, n), 1)
    groups = rows.reshape(n // 8, 8, n)
    w_ref[...] = jnp.where(rows == lanes, 1.0, 0.0).astype(F32)

    def pick(x, index):
        return jnp.take_along_axis(
            x, jnp.full(x.shape, index, jnp.int32), axis=1, mode="promise_in_bounds"
        )

    def step(it, carry):
        k = it * 4
        a = a_ref[...]
        c = [pick(a, k + t).reshape(n // 8, 8, n) for t in range(4)]
        a = a.reshape(n // 8, 8, n)
        w = w_ref[...].reshape(n // 8, 8, n)
        r = [jnp.broadcast_to(a_ref[pl.ds(k + t, 1), :], (8, n)) for t in range(4)]
        v = [jnp.broadcast_to(w_ref[pl.ds(k + t, 1), :], (8, n)) for t in range(4)]
        g = [[pick(r[t], k + s) for s in range(4)] for t in range(4)]
        inv = []
        for t in range(4):
            inv.append(1.0 / g[t][t])
            for s in range(t + 1, 4):
                m = g[t][s] * inv[t]
                for u in range(s, 4):
                    g[s][u] = g[s][u] - m * g[t][u]
                r[s] = r[s] - m * r[t]
                v[s] = v[s] - m * v[t]
        for t in range(4):
            m = c[t] * inv[t]
            for s in range(t + 1, 4):
                c[s] = c[s] - m * g[t][s]
            m = jnp.where(groups >= k + 4, m, 0.0)
            a = a - m * r[t]
            w = w - m * v[t]
        a_ref[...] = a.reshape(n, n)
        w_ref[...] = w.reshape(n, n)
        for t in range(4):
            d = g[t][t]
            y = lax.rsqrt(d)
            y = y * (1.5 - 0.5 * d * y * y)
            w_ref[pl.ds(k + t, 1), :] = (v[t] * y)[:1]
        return carry

    lax.fori_loop(0, n // 4, step, 0)


def factor_kernel(d_ref, out_ref, a_ref, w1_ref, w2_ref):
    a_ref[...] = d_ref[:HB, :HB]
    inverse_factor(a_ref, w1_ref)
    first = w1_ref[...]
    low = mm(d_ref[HB:, :HB], first, ((1,), (1,)))
    a_ref[...] = d_ref[HB:, HB:] - mm(low, low, ((1,), (1,)))
    inverse_factor(a_ref, w2_ref)
    second = w2_ref[...]
    out_ref[:HB, :] = first
    out_ref[HB:PB, :] = -mm(second, mm(low, first))
    out_ref[PB:, :] = second


def inverse_of_factor(block):
    return pl.pallas_call(
        factor_kernel,
        out_shape=jax.ShapeDtypeStruct((3 * HB, HB), F32),
        scratch_shapes=[pltpu.VMEM((HB, HB), F32)] * 3,
        cost_estimate=pl.CostEstimate(
            flops=200_000_000, transcendentals=0, bytes_accessed=80_000_000
        ),
        name="inverse_factor",
    )(block)


def apply_kernel(
    place_ref, noise_ref, wfs_ref, a_ref, t_ref, own_ref, other_ref, inv_ref, ctt_ref,
    upd_ref, pan_ref, rec_ref, err_ref, lt_ref, u_ref, head_ref,
):
    i = pl.program_id(0)
    row, col = place_ref[0], place_ref[1]
    core = lax.rem(row, 2)
    tile, width = upd_ref.shape
    per = a_ref.shape[1] // 2 // HB

    @pl.when(i == 0)
    def _():
        inv = jnp.concatenate(
            [
                jnp.concatenate([inv_ref[:HB, :], jnp.zeros((HB, HB), F32)], axis=1),
                jnp.concatenate([inv_ref[HB:PB, :], inv_ref[PB:, :]], axis=1),
            ],
            axis=0,
        )
        hi, lo = split(inv)
        lt_ref[0], lt_ref[1] = hi, lo
        half = width // 2
        for ref, at, base in ((own_ref, core, 24), (other_ref, 1 - core, 0)):
            stack = ref[:, base : base + 24, :].reshape(2 * half, HB)
            rows = split(jnp.concatenate([stack[:half], stack[half:]], axis=1))
            u = split(mm3((hi, lo), rows, ((1,), (1,))))
            where = pl.ds(pl.multiple_of(at * half, HB), half)
            u_ref[0, :, where] = u[0]
            u_ref[1, :, where] = u[1]
        mine = own_ref[:, 52:56, :].reshape(PB, HB)
        theirs = other_ref[:, 28:32, :].reshape(PB, HB)
        first = jnp.where(core == 0, mine, theirs)
        last = jnp.where(core == 0, theirs, mine)
        head = mm3((hi, lo), split(jnp.concatenate([first, last], axis=1)))
        head_ref[...] = head
        need = mm3((hi, lo), split(own_ref[:, 48:52, :].reshape(PB, HB)))
        err_ref[...] = ctt_ref[...] - mm3(split(need), split(head), ((0,), (0,)))

    inv = (lt_ref[0], lt_ref[1])
    rows = split(
        jnp.concatenate([panel_rows(own_ref, i, tile, 0), panel_rows(own_ref, i, tile, 1)], axis=1)
    )
    panel = mm3(rows, inv, ((1,), (1,)))
    ids = row * (tile * pl.num_programs(0)) + i * tile + lax.broadcasted_iota(jnp.int32, (tile, PB), 0)
    lane = lax.broadcasted_iota(jnp.int32, (tile, PB), 1)
    panel = jnp.where((ids < PB) & (lane > ids), 0.0, panel)
    pan_ref[...] = panel
    pair = split(panel)
    upd_ref[...] = a_ref[...] - mm3(pair, (u_ref[0], u_ref[1]))
    rec_ref[...] = t_ref[...] - mm3(pair, split(head_ref[...]))

    @pl.when(lax.div(row, 2) == col)
    def _():
        at = pl.multiple_of(core * (width // 2) + i * tile, HB)
        noise = jnp.zeros((1, tile), F32)
        for s in range(noise_ref.shape[0]):
            noise = jnp.where(wfs_ref[...] == s, noise_ref[s], noise)
        eye = lax.broadcasted_iota(jnp.int32, (tile, tile), 0) == lax.broadcasted_iota(
            jnp.int32, (tile, tile), 1
        )
        upd_ref[:, pl.ds(at, tile)] = upd_ref[:, pl.ds(at, tile)] + jnp.where(eye, noise, 0.0)

    @pl.when((row == 0) & (i * tile < PB))
    def _():
        upd_ref[...] = jnp.zeros_like(upd_ref)
        rec_ref[...] = head_ref[pl.ds(pl.multiple_of(i * tile, tile), tile), :]

    @pl.when(col == 0)
    def _():
        upd_ref[:, :PB] = panel


def panel_rows(ref, i, tile, half):
    start = half * 6 + i
    groups = tile // 8
    pieces = []
    for g in range(groups):
        tile_id = start * groups + g
        piece = lax.div(tile_id, 3)
        offset = pl.multiple_of(lax.rem(tile_id, 3) * 8, 8)
        pieces.append(ref[piece, pl.ds(offset, 8), :])
    return jnp.concatenate(pieces, axis=0)


def apply(place, noise_var, wfs, covariance, targets, own, other, inv, ctt):
    rows, width = covariance.shape
    tile = 128
    target_width = targets.shape[1]
    whole = lambda x: pl.BlockSpec(x.shape, lambda i: (0,) * x.ndim, pipeline_mode=pl.Buffered(1))
    smem = pl.BlockSpec(memory_space=pltpu.SMEM)
    return pl.pallas_call(
        apply_kernel,
        grid=(rows // tile,),
        in_specs=[
            smem,
            smem,
            pl.BlockSpec((1, tile), lambda i: (0, i)),
            pl.BlockSpec((tile, width), lambda i: (i, 0)),
            pl.BlockSpec((tile, target_width), lambda i: (i, 0)),
            whole(own),
            whole(other),
            whole(inv),
            whole(ctt),
        ],
        out_specs=[
            pl.BlockSpec((tile, width), lambda i: (i, 0)),
            pl.BlockSpec((tile, PB), lambda i: (i, 0)),
            pl.BlockSpec((tile, target_width), lambda i: (i, 0)),
            pl.BlockSpec(ctt.shape, lambda i: (0, 0)),
        ],
        out_shape=[
            jax.ShapeDtypeStruct((rows, width), F32),
            jax.ShapeDtypeStruct((rows, PB), F32),
            jax.ShapeDtypeStruct((rows, target_width), F32),
            jax.ShapeDtypeStruct(ctt.shape, F32),
        ],
        scratch_shapes=[
            pltpu.VMEM((2, PB, PB), jnp.bfloat16),
            pltpu.VMEM((2, PB, width), jnp.bfloat16),
            pltpu.VMEM((PB, target_width), F32),
        ],
        compiler_params=pltpu.CompilerParams(vmem_limit_bytes=48 << 20),
        cost_estimate=pl.CostEstimate(
            flops=3_300_000_000, transcendentals=0, bytes_accessed=15_000_000
        ),
        name="apply",
    )(place, noise_var, wfs[None, :], covariance, targets, own, other, inv, ctt)


def device(x, z_lo, y, z_hi, core):
    return (x * 2 + z_lo) * 16 + y * 4 + z_hi * 2 + core


def spread(value):
    four, two = range(4), range(2)
    index = lax.axis_index("col") * 16 + lax.axis_index("row")
    value = jnp.where(index == 0, value, 0.0)
    rounds = (
        [[(device(0, 0, 0, 0, 0), device(k, 0, 0, 0, 0))] for k in (2, 1, 3)],
        [[(device(x, 0, 0, 0, 0), device(x, 0, k, 0, 0)) for x in four] for k in (2, 1, 3)],
        [
            [(device(x, 0, y, 0, 0), device(x, lo, y, hi, 0)) for x in four for y in four]
            for lo, hi in ((0, 1), (1, 1), (1, 0))
        ],
        [
            [
                (device(x, lo, y, hi, 0), device(x, lo, y, hi, 1))
                for x in four for y in four for lo in two for hi in two
            ]
        ],
    )
    for perms in rounds:
        value = sum([lax.ppermute(value, BOTH, perm) for perm in perms], value)
    return value


def target_covariance(pos_rows, pos_cols, low, strength, scale):
    distance = (pos_rows[0][:, None] - pos_cols[0][None, :]) ** 2 + (
        pos_rows[1][:, None] - pos_cols[1][None, :]
    ) ** 2
    levels = jnp.arange(strength.shape[0], dtype=jnp.int32)
    weights = strength[:, None, None] / (1.0 + distance[None] / (scale * scale)[:, None, None])
    return jnp.sum(jnp.where(levels[:, None, None] <= low[None, None, :], weights, 0.0), axis=0)


def local(covariance, wfs_map, noise_var, targets, target_pos, strength, scale, tile_layer):
    rows, width = covariance.shape
    target_width = targets.shape[1]
    row, col = lax.axis_index("row"), lax.axis_index("col")
    groups = [[c * 16 + 2 * m + k for c in range(8) for m in range(8)] for k in range(2)]
    exchange = lambda x: lax.all_to_all(
        x, BOTH, 0, 0, axis_index_groups=groups, tiled=True
    )

    noise = jnp.sum(
        jnp.where(
            wfs_map[:, None] == jnp.arange(noise_var.shape[0], dtype=jnp.int32)[None, :],
            noise_var[None, :],
            0.0,
        ),
        axis=1,
    )
    row_ids = row * rows + jnp.arange(rows, dtype=jnp.int32)
    col_ids = col * width + jnp.arange(PB, dtype=jnp.int32)
    panel = covariance[:, :PB] + jnp.where(
        row_ids[:, None] == col_ids[None, :], noise[:, None], 0.0
    )
    inv = inverse_of_factor(panel[:PB, :])

    second = lax.ppermute(targets[:PB, HB:], "row", [(0, 1)])
    half = jnp.where(row == 1, second, targets[:PB, :HB])
    pieces = jnp.concatenate([panel[:, :HB], panel[:, HB:]], axis=0).reshape(64, 24, HB)
    half = jnp.pad(half.reshape(64, 4, HB), ((0, 0), (0, 4), (0, 0)))
    held = exchange(jnp.concatenate([pieces, half], axis=1))
    held_panel = held[:8, :24]
    held_head = held.reshape(8, 8, 32, HB)[:, 0, 24:28]

    shape = lambda n: (8, 8, n, HB)
    over_m = lambda x: jnp.broadcast_to(x[None], shape(x.shape[1]))
    over_c = lambda x: jnp.broadcast_to(x[:, None], shape(x.shape[1]))
    wanted = jnp.concatenate(
        [over_m(held_panel), over_c(held_panel), over_m(held_head), over_c(held_head)], axis=2
    )
    own = exchange(wanted.reshape(64, 56, HB))
    other = lax.ppermute(own[:, 24:], "row", [(i, i ^ 1) for i in range(16)])
    inv = spread(inv)

    start = row * TILE
    pos_rows = lax.dynamic_slice_in_dim(target_pos, start, TILE, 1)
    pos_cols = lax.dynamic_slice_in_dim(target_pos, col * target_width, target_width, 1)
    level_cols = lax.dynamic_slice_in_dim(tile_layer, col * (target_width // TILE), target_width // TILE, 0)
    level_row = lax.dynamic_slice_in_dim(tile_layer, row, 1, 0)
    low = jnp.repeat(jnp.minimum(level_row, level_cols), TILE)
    ctt = target_covariance(pos_rows, pos_cols, low, strength, scale)

    place = jnp.stack([row, col]).astype(jnp.int32)
    updated, panel, reconstructor, error = apply(
        place, noise_var, wfs_map, covariance, targets, own, other, inv, ctt
    )
    return updated, panel, reconstructor, error


def solution(mesh):
    placed = (P("row", "col"), P("row"), P(), P("row", "col"), P(), P(), P(), P())
    return jax.shard_map(
        local,
        mesh=mesh,
        in_specs=placed,
        out_specs=(P("row", "col"), P("row", None), P("row", "col"), P("row", "col")),
        check_vma=False,
    )
```

time: 519 us -> 97.1 us (0.19)
  waiting for transfers between devices: 389 us -> 18.1 us
  other arithmetic: 62.7 us -> 8.16 us
  starting transfers between devices: 0.16 us -> 37.4 us
  Pallas kernels: 0 us -> 26.6 us
  matrix products: 22.7 us -> 0 us
  local copies, waits for them, and re-layouts: 26.8 us -> 4.9 us
  between operations: 15.5 us -> 1.04 us
    psum x3 -> x0, waiting for transfers between devices: 353 us -> none  [broadcast(): return lax.psum(jnp.where(mine, shard, jnp.zeros_like(shard)), axis)]
    another operation x9 -> x1, other arithmetic: 53.7 us -> 0.08 us  [local(): place = jnp.stack([row, col]).astype(jnp.int32)]
    all_gather x1 -> x0, waiting for transfers between devices: 35.7 us -> none  [local(): gathered = lax.all_gather(head_cols, 'col', axis=1, tiled=True)]
    pallas_call x0 -> x2, Pallas kernels: none -> 26.6 us  [the longest x1 15.8 us: inverse_of_factor(): pl.pallas_call(factor_kernel, out_shape=jax.ShapeDtypeStruct((3 * HB, HB)...]
    all_to_all x0 -> x2, starting transfers between devices: none -> 21.2 us  [local(): lax.all_to_all(x, BOTH, 0, 0, axis_index_groups=groups, tiled=True)]
    unnamed x25 -> x14, local copies, waits for them, and re-layouts: 18.1 us -> 0.03 us
    all_to_all x0 -> x2, waiting for transfers between devices: none -> 17.1 us  [local(): lax.all_to_all(x, BOTH, 0, 0, axis_index_groups=groups, tiled=True)]
    ppermute x0 -> x12, starting transfers between devices: none -> 16.2 us  [the longest x1 7.59 us: local(): other = lax.ppermute(own[:, 24:], 'row', [(i, i ^ 1) for i in range(16)])]
  transfers between devices with their start and end apart: 4 -> 14, of which waited for: 4 -> 2; matrix products, arithmetic and copies ran while one was open for 5% -> 11% of each run, Pallas kernels for 0% -> 16%
where the time goes in v1:
time: 97.1 us; the launch traced here: 96.2 us
  starting transfers between devices  37.4 us (39%)
  Pallas kernels  26.6 us (27%)
  waiting for transfers between devices  18.1 us (19%)
  other arithmetic  8.16 us (8%)
  local copies, waits for them, and re-layouts  4.9 us (5%)
  between operations  1.04 us (1%)
    all_to_all x2, starting transfers between devices, local(): lax.all_to_all(x, BOTH, 0, 0, axis_index_groups=groups, tiled=True)  21.2 us
    all_to_all x2, waiting for transfers between devices, local(): lax.all_to_all(x, BOTH, 0, 0, axis_index_groups=groups, tiled=True)  17.1 us
    pallas_call x1, Pallas kernels, inverse_of_factor(): pl.pallas_call(factor_kernel, out_shape=jax.ShapeDtypeStruct((3 * HB, HB)...  15.8 us
    pallas_call x1, Pallas kernels, apply(): pl.pallas_call(apply_kernel, grid=(rows // tile,), in_specs=[smem, smem,...  10.7 us
    ppermute x1, starting transfers between devices, local(): other = lax.ppermute(own[:, 24:], 'row', [(i, i ^ 1) for i in range(16)])  7.59 us
    ppermute x10, starting transfers between devices, spread(): value = sum([lax.ppermute(value, BOTH, perm) for perm in perms], value)  7.34 us
  transfers between devices with their start and end apart: 14, of which 2 were waited for; matrix products, arithmetic and copies ran while one was open for 11% of the time, Pallas kernels for 16%

profile of v1, /device:TPU:1, one launch (start us, length us, event | category | flops | bytes accessed | tf_op | source)
XLA Modules:
  0.0 96.2 jit_solution(9953892882288154912)
XLA Ops:
  0.6 1.0 %slice.46 = f32[256,128]{1,0:T(8,128)S(1)} slice(f32[768,256]{1,0:T(8,128)} %t_ref.1), slice={[0:256], [128:256]} | slice | bytes 262144 | tf_op jit(solution)/shard_map/slice | solution.py:295
  1.6 1.3 %collective-permute-start = (f32[256,128]{1,0:T(8,128)S(1)}, f32[256,128]{1,0:T(8,128)S(1)}, u32[]{:S(2)}, u32[]{:S(2)}) collective-permute-start(f32[256,128]{1,0:T(8,128)S(1)} %slice.46), channel_id=1, source_target_pairs={{0,1},{16,17},{32,33},{48,49},{64,65},{80,81},{96,97},{112,113}} | collective-permute-start | bytes 393224 | tf_op jit(solution)/shard_map/ppermute | solution.py:295
  3.0 0.8 select_reduce_fusion
  3.8 1.4 %select_add_fusion = f32[768,256]{1,0:T(8,128)S(1)} fusion(f32[768,1536]{1,0:T(8,128)} %a_ref.1, f32[768]{0:T(1024)S(1)} %select_reduce_fusion, s32[256]{0:T(256)S(1)} %iota_add_fusion.1, s32[768]{0:T(1024)S(1)} %iota_add_fusion), kind=kLoop, calls=%fused_computation.8 | loop fusion | flops 589824 | bytes 1580032 | tf_op jit(solution)/shard_map/add | solution.py:290
  5.2 0.0 copy-start.5
  5.2 0.1 fusion.3
  5.2 0.1 pad_maximum_fusion.1
  5.3 1.1 %select_maximum_fusion = f32[64,32,128]{2,1,0:T(8,128)} fusion(f32[64,4,128]{2,1,0:T(4,128)S(1)} %bitcast.22, f32[64,24,128]{2,1,0:T(8,128)S(1)} %bitcast.20), kind=kLoop, calls=%fused_computation.5 | loop fusion | flops 786432 | bytes 1966080 | tf_op jit(solution)/shard_map/concatenate | solution.py:299
  6.4 11.3 %all-to-all-start = ((f32[64,32,128]{2,1,0:T(8,128)}), f32[64,32,128]{2,1,0:T(8,128)S(1)}, u32[]{:S(2)}, u32[]{:S(2)}) async-start(f32[64,32,128]{2,1,0:T(8,128)} %select_maximum_fusion), calls=%async_computation | async-start | bytes 2097152 | tf_op jit(solution)/shard_map/all_to_all | solution.py:276
  17.8 0.7 slice.63.d_ref
  18.5 15.8 %inverse_factor.1 = f32[384,128]{1,0:T(8,128)} custom-call(f32[256,256]{1,0:T(8,128)} %slice.63.d_ref), custom_call_target="tpu_custom_call" | custom-call | flops 200000000 | bytes 80000000 | tf_op jit(solution)/shard_map/inverse_factor/pallas_call | solution.py:95
  34.3 0.7 broadcast_select_fusion
  35.0 0.7 collective-permute-start.3
  35.7 0.7 collective-permute-start.4
  36.4 0.7 collective-permute-start.2
  37.1 0.6 dynamic_slice.12
  37.7 0.7 constant_dynamic-slice_fusion.1
  38.4 0.0 all-to-all-done
  38.4 0.0 copy-start.6
  38.4 0.0 copy-start.2
  38.5 0.1 broadcast_in_dim.86
  38.5 0.1 broadcast_in_dim.85
  38.6 1.4 %pad_maximum_fusion = f32[8,8,56,128]{3,2,1,0:T(8,128)} fusion(f32[8,8,4,128]{3,2,1,0:T(4,128)S(1)} %broadcast_in_dim.89, f32[8,8,4,128]{3,2,1,0:T(4,128)S(1)} %broadcast_in_dim.88, f32[8,8,24,128]{3,2,1,0:T(8,128)S(1)} %broadcast_in_dim.86, f32[8,8,24,128]{3,2,1,0:T(8,128)S(1)} %broadcast_in_dim.85), kind=kLoop, calls=%fused_computation.4 | loop fusion | flops 1376256 | bytes 3670016 | tf_op jit(solution)/shard_map/concatenate | solution.py:306
  40.0 9.9 %all-to-all-start.1 = ((f32[64,56,128]{2,1,0:T(8,128)}), f32[64,56,128]{2,1,0:T(8,128)S(1)}, u32[]{:S(2)}, u32[]{:S(2)}) async-start(f32[64,56,128]{2,1,0:T(8,128)} %bitcast.19), calls=%async_computation.1 | async-start | bytes 3670016 | tf_op jit(solution)/shard_map/all_to_all | solution.py:276
  49.9 1.2 %dynamic-slice_minimum_fusion = s32[2]{0:T(128)} fusion(s32[16]{0:T(128)S(1)} %copy-done.5, s32[]{:T(128)S(6)} %select_n.47, s32[]{:T(128)} %bitcast.7), kind=kLoop, calls=%fused_computation.24 | loop fusion | flops 2 | bytes 24 | tf_op jit(solution)/shard_map/min | solution.py:318
  51.1 0.8 constant_dynamic-slice_fusion
  52.0 0.1 multiply_add_fusion
  52.1 0.0 collective-permute-done.3
  52.1 0.0 collective-permute-done.2
  52.2 0.7 collective-permute-start.7
  52.8 0.7 collective-permute-start.6
  53.5 0.7 collective-permute-start.5
  54.2 0.7 broadcast_bitcast_fusion
  54.9 0.0 collective-permute-done.7
  54.9 0.0 collective-permute-done.6
  55.0 0.7 collective-permute-start.10
  55.6 0.7 collective-permute-start.9
  56.3 0.7 collective-permute-start.8
  57.0 0.0 collective-permute-done.10
  57.0 0.0 collective-permute-done.9
  57.1 1.3 %collective-permute-start.11 = (f32[384,128]{1,0:T(8,128)S(1)}, f32[384,128]{1,0:T(8,128)S(1)}, u32[]{:S(2)}, u32[]{:S(2)}) collective-permute-start(f32[384,128]{1,0:T(8,128)S(1)} %add_add_fusion), channel_id=1, source_target_pairs={{0,1},{2,3},{16,17},{18,19},{4,5},{6,7},{20,21},{22,23},{8,9},{10,... | collective-permute-start | bytes 589832 | tf_op jit(solution)/shard_map/ppermute | solution.py:258
  58.4 17.1 %all-to-all-done.1.own_ref = f32[64,56,128]{2,1,0:T(8,128)S(1)} async-done(((f32[64,56,128]{2,1,0:T(8,128)}), f32[64,56,128]{2,1,0:T(8,128)S(1)}, u32[]{:S(2)}, u32[]{:S(2)}) %all-to-all-start.1) | async-done | bytes 1835040 | tf_op jit(solution)/shard_map/all_to_all | solution.py:276
  75.5 0.1 slice.62
  75.6 7.6 %collective-permute-start.1 = (f32[64,32,128]{2,1,0:T(8,128)S(1)}, f32[64,32,128]{2,1,0:T(8,128)S(1)}, u32[]{:S(2)}, u32[]{:S(2)}) collective-permute-start(f32[64,32,128]{2,1,0:T(8,128)S(1)} %slice.62), channel_id=1, source_target_pairs={{0,1},{1,0},{2,3},{3,2},{4,5},{5,4},{6,7},{7,6},{8,9},{9,8},{10,11... | collective-permute-start | bytes 3145736 | tf_op jit(solution)/shard_map/ppermute | solution.py:310
  83.2 1.1 %fusion.2.ctt_ref = f32[128,256]{1,0:T(8,128)S(1)} fusion(f32[35]{0:T(128)S(1)} %mul.27, f32[128,256]{1,0:T(8,128)S(1)} %multiply_add_fusion, f32[35]{0:T(128)S(1)} %copy-done.4, pred[35,256]{1,0:T(8,128)(4,1)S(1)} %iota_compare_fusion.1), kind=kLoop, calls=%fused_computation.3 | loop fusion | flops 5701632 | bytes 271384 | tf_op jit(solution)/shard_map/reduce_sum | solution.py:268
  84.3 0.1 pad_add_fusion.place_ref
  84.5 1.0 %collective-permute-done.1.other_ref = f32[64,32,128]{2,1,0:T(8,128)S(1)} collective-permute-done((f32[64,32,128]{2,1,0:T(8,128)S(1)}, f32[64,32,128]{2,1,0:T(8,128)S(1)}, u32[]{:S(2)}, u32[]{:S(2)}) %collective-permute-start.1) | collective-permute-done | bytes 1048608 | tf_op jit(solution)/shard_map/ppermute | solution.py:310
  85.5 10.7 %apply.1 = (f32[768,1536]{1,0:T(8,128)}, f32[768,256]{1,0:T(8,128)}, f32[768,256]{1,0:T(8,128)}, f32[128,256]{1,0:T(8,128)}) custom-call(s32[2]{0:T(128)S(1)} %pad_add_fusion.place_ref, f32[6]{0:T(128)S(1)} %copy-done.1, s32[1,768]{1,0:T(1,128)S(1)} %broadcast_in_dim.80.wfs_ref, f32[768,1536]{1,0:T(8,128)} %a_ref.1, f32[768,256]{1,0:T(8,128)S(1)} %copy-done, ...), custom_call_target="tpu_custom_call" | custom-call | flops 3300000000 | bytes 15000000 | tf_op jit(solution)/shard_map/apply/pallas_call | solution.py:196
  (31 shorter events, 0.3 us)
Async XLA Ops:
  0.6 4.7 %copy-start = (f32[768,256]{1,0:T(8,128)S(1)}, f32[768,256]{1,0:T(8,128)}, u32[]{:S(2)}) copy-start(f32[768,256]{1,0:T(8,128)} %t_ref.1) | copy-start | bytes 2359300
  1.6 3.7 %collective-permute-start = (f32[256,128]{1,0:T(8,128)S(1)}, f32[256,128]{1,0:T(8,128)S(1)}, u32[]{:S(2)}, u32[]{:S(2)}) collective-permute-start(f32[256,128]{1,0:T(8,128)S(1)} %slice.46), channel_id=1, source_target_pairs={{0,1},{16,17},{32,33},{48,49},{64,65},{80,81},{96,97},{112,113}} | collective-permute-start | bytes 393224 | tf_op jit(solution)/shard_map/ppermute | solution.py:295
  5.2 31.9 %copy-start.5 = (s32[16]{0:T(128)S(1)}, s32[16]{0:T(128)}, u32[]{:S(2)}) copy-start(s32[16]{0:T(128)} %param.15) | copy-start | bytes 196
  6.4 31.9 %all-to-all-start = ((f32[64,32,128]{2,1,0:T(8,128)}), f32[64,32,128]{2,1,0:T(8,128)S(1)}, u32[]{:S(2)}, u32[]{:S(2)}) async-start(f32[64,32,128]{2,1,0:T(8,128)} %select_maximum_fusion), calls=%async_computation | async-start | bytes 2097152 | tf_op jit(solution)/shard_map/all_to_all | solution.py:276
  35.0 17.0 %collective-permute-start.3 = (f32[384,128]{1,0:T(8,128)}, f32[384,128]{1,0:T(8,128)S(1)}, u32[]{:S(2)}, u32[]{:S(2)}) collective-permute-start(f32[384,128]{1,0:T(8,128)} %broadcast_select_fusion), channel_id=1, source_target_pairs={{0,32}} | collective-permute-start | bytes 589832 | tf_op jit(solution)/shard_map/ppermute | solution.py:258
  35.7 16.4 %collective-permute-start.4 = (f32[384,128]{1,0:T(8,128)}, f32[384,128]{1,0:T(8,128)S(1)}, u32[]{:S(2)}, u32[]{:S(2)}) collective-permute-start(f32[384,128]{1,0:T(8,128)} %broadcast_select_fusion), channel_id=1, source_target_pairs={{0,96}} | collective-permute-start | bytes 589832 | tf_op jit(solution)/shard_map/ppermute | solution.py:258
  36.4 15.7 %collective-permute-start.2 = (f32[384,128]{1,0:T(8,128)}, f32[384,128]{1,0:T(8,128)S(1)}, u32[]{:S(2)}, u32[]{:S(2)}) collective-permute-start(f32[384,128]{1,0:T(8,128)} %broadcast_select_fusion), channel_id=1, source_target_pairs={{0,64}} | collective-permute-start | bytes 589832 | tf_op jit(solution)/shard_map/ppermute | solution.py:258
  38.4 12.7 %copy-start.6 = (f32[35]{0:T(128)S(1)}, f32[35]{0:T(128)}, u32[]{:S(2)}) copy-start(f32[35]{0:T(128)} %param.14) | copy-start | bytes 424
  38.4 13.6 %copy-start.2 = (f32[384,128]{1,0:T(8,128)S(1)}, f32[384,128]{1,0:T(8,128)}, u32[]{:S(2)}) copy-start(f32[384,128]{1,0:T(8,128)} %inverse_factor.1) | copy-start | bytes 589828
  40.0 43.2 %copy-start.4 = (f32[35]{0:T(128)S(1)}, f32[35]{0:T(128)}, u32[]{:S(2)}) copy-start(f32[35]{0:T(128)} %param.13) | copy-start | bytes 424
  40.0 44.3 %copy-start.3 = (s32[768]{0:T(1024)S(1)}, s32[768]{0:T(1024)}, u32[]{:S(2)}) copy-start(s32[768]{0:T(1024)} %param.9) | copy-start | bytes 9220
  40.0 45.5 %copy-start.1 = (f32[6]{0:T(128)S(1)}, f32[6]{0:T(128)}, u32[]{:S(2)}) copy-start(f32[6]{0:T(128)} %noise_ref.1) | copy-start | bytes 76
  40.0 35.5 %all-to-all-start.1 = ((f32[64,56,128]{2,1,0:T(8,128)}), f32[64,56,128]{2,1,0:T(8,128)S(1)}, u32[]{:S(2)}, u32[]{:S(2)}) async-start(f32[64,56,128]{2,1,0:T(8,128)} %bitcast.19), calls=%async_computation.1 | async-start | bytes 3670016 | tf_op jit(solution)/shard_map/all_to_all | solution.py:276
  52.2 2.8 %collective-permute-start.7 = (f32[384,128]{1,0:T(8,128)S(1)}, f32[384,128]{1,0:T(8,128)S(1)}, u32[]{:S(2)}, u32[]{:S(2)}) collective-permute-start(f32[384,128]{1,0:T(8,128)S(1)} %add_add_fusion.2), channel_id=1, source_target_pairs={{0,12},{32,44},{64,76},{96,108}} | collective-permute-start | bytes 589832 | tf_op jit(solution)/shard_map/ppermute | solution.py:258
  52.8 2.1 %collective-permute-start.6 = (f32[384,128]{1,0:T(8,128)S(1)}, f32[384,128]{1,0:T(8,128)S(1)}, u32[]{:S(2)}, u32[]{:S(2)}) collective-permute-start(f32[384,128]{1,0:T(8,128)S(1)} %add_add_fusion.2), channel_id=1, source_target_pairs={{0,4},{32,36},{64,68},{96,100}} | collective-permute-start | bytes 589832 | tf_op jit(solution)/shard_map/ppermute | solution.py:258
  53.5 1.4 %collective-permute-start.5 = (f32[384,128]{1,0:T(8,128)S(1)}, f32[384,128]{1,0:T(8,128)S(1)}, u32[]{:S(2)}, u32[]{:S(2)}) collective-permute-start(f32[384,128]{1,0:T(8,128)S(1)} %add_add_fusion.2), channel_id=1, source_target_pairs={{0,8},{32,40},{64,72},{96,104}} | collective-permute-start | bytes 589832 | tf_op jit(solution)/shard_map/ppermute | solution.py:258
  55.0 2.1 %collective-permute-start.10 = (f32[384,128]{1,0:T(8,128)S(1)}, f32[384,128]{1,0:T(8,128)S(1)}, u32[]{:S(2)}, u32[]{:S(2)}) collective-permute-start(f32[384,128]{1,0:T(8,128)S(1)} %add_add_fusion.1), channel_id=1, source_target_pairs={{0,16},{4,20},{8,24},{12,28},{32,48},{36,52},{40,56},{44,60},{64,8... | collective-permute-start | bytes 589832 | tf_op jit(solution)/shard_map/ppermute | solution.py:258
  55.6 1.4 %collective-permute-start.9 = (f32[384,128]{1,0:T(8,128)S(1)}, f32[384,128]{1,0:T(8,128)S(1)}, u32[]{:S(2)}, u32[]{:S(2)}) collective-permute-start(f32[384,128]{1,0:T(8,128)S(1)} %add_add_fusion.1), channel_id=1, source_target_pairs={{0,18},{4,22},{8,26},{12,30},{32,50},{36,54},{40,58},{44,62},{64,8... | collective-permute-start | bytes 589832 | tf_op jit(solution)/shard_map/ppermute | solution.py:258
  56.3 0.7 collective-permute-start.8
  57.1 27.3 %collective-permute-start.11 = (f32[384,128]{1,0:T(8,128)S(1)}, f32[384,128]{1,0:T(8,128)S(1)}, u32[]{:S(2)}, u32[]{:S(2)}) collective-permute-start(f32[384,128]{1,0:T(8,128)S(1)} %add_add_fusion), channel_id=1, source_target_pairs={{0,1},{2,3},{16,17},{18,19},{4,5},{6,7},{20,21},{22,23},{8,9},{10,... | collective-permute-start | bytes 589832 | tf_op jit(solution)/shard_map/ppermute | solution.py:258
  75.6 9.9 %collective-permute-start.1 = (f32[64,32,128]{2,1,0:T(8,128)S(1)}, f32[64,32,128]{2,1,0:T(8,128)S(1)}, u32[]{:S(2)}, u32[]{:S(2)}) collective-permute-start(f32[64,32,128]{2,1,0:T(8,128)S(1)} %slice.62), channel_id=1, source_target_pairs={{0,1},{1,0},{2,3},{3,2},{4,5},{5,4},{6,7},{7,6},{8,9},{9,8},{10,11... | collective-permute-start | bytes 3145736 | tf_op jit(solution)/shard_map/ppermute | solution.py:310

commit v2 on v1

v2 whole, which is shorter than its diff:
```python
import functools

import jax
import jax.numpy as jnp
from jax import lax
from jax.experimental import pallas as pl
from jax.experimental.pallas import tpu as pltpu
from jax.sharding import PartitionSpec as P

PB = 256
HB = 128
TILE = 128
BOTH = ("col", "row")
precise = lax.Precision.HIGHEST
F32 = jnp.float32


def mm(a, b, dims=((1,), (0,))):
    return lax.dot_general(a, b, (dims, ((), ())), precision=precise, preferred_element_type=F32)


def split(x):
    hi = x.astype(jnp.bfloat16)
    return hi, (x - hi.astype(F32)).astype(jnp.bfloat16)


def mm3(a, b, dims=((1,), (0,))):
    dot = lambda x, y: lax.dot_general(x, y, (dims, ((), ())), preferred_element_type=F32)
    return dot(a[0], b[0]) + (dot(a[0], b[1]) + dot(a[1], b[0]))


def inverse_factor(a_ref, w_ref):
    n = a_ref.shape[0]
    rows = lax.broadcasted_iota(jnp.int32, (n, n), 0)
    lanes = lax.broadcasted_iota(jnp.int32, (n, n), 1)
    groups = rows.reshape(n // 8, 8, n)
    w_ref[...] = jnp.where(rows == lanes, 1.0, 0.0).astype(F32)

    def pick(x, index):
        return jnp.take_along_axis(
            x, jnp.full(x.shape, index, jnp.int32), axis=1, mode="promise_in_bounds"
        )

    def step(it, carry):
        k = it * 4
        a = a_ref[...]
        c = [pick(a, k + t).reshape(n // 8, 8, n) for t in range(4)]
        a = a.reshape(n // 8, 8, n)
        w = w_ref[...].reshape(n // 8, 8, n)
        r = [jnp.broadcast_to(a_ref[pl.ds(k + t, 1), :], (8, n)) for t in range(4)]
        v = [jnp.broadcast_to(w_ref[pl.ds(k + t, 1), :], (8, n)) for t in range(4)]
        g = [[pick(r[t], k + s) for s in range(4)] for t in range(4)]
        inv = []
        for t in range(4):
            inv.append(1.0 / g[t][t])
            for s in range(t + 1, 4):
                m = g[t][s] * inv[t]
                for u in range(s, 4):
                    g[s][u] = g[s][u] - m * g[t][u]
                r[s] = r[s] - m * r[t]
                v[s] = v[s] - m * v[t]
        for t in range(4):
            m = c[t] * inv[t]
            for s in range(t + 1, 4):
                c[s] = c[s] - m * g[t][s]
            m = jnp.where(groups >= k + 4, m, 0.0)
            a = a - m * r[t]
            w = w - m * v[t]
        a_ref[...] = a.reshape(n, n)
        w_ref[...] = w.reshape(n, n)
        for t in range(4):
            d = g[t][t]
            y = lax.rsqrt(d)
            y = y * (1.5 - 0.5 * d * y * y)
            w_ref[pl.ds(k + t, 1), :] = (v[t] * y)[:1]
        return carry

    lax.fori_loop(0, n // 4, step, 0)


def factor_kernel(d_ref, out_ref, a_ref, w1_ref, w2_ref):
    a_ref[...] = d_ref[:HB, :HB]
    inverse_factor(a_ref, w1_ref)
    first = w1_ref[...]
    low = mm(d_ref[HB:, :HB], first, ((1,), (1,)))
    a_ref[...] = d_ref[HB:, HB:] - mm(low, low, ((1,), (1,)))
    inverse_factor(a_ref, w2_ref)
    second = w2_ref[...]
    out_ref[:HB, :] = first
    out_ref[HB:PB, :] = -mm(second, mm(low, first))
    out_ref[PB:, :] = second


def inverse_of_factor(block):
    return pl.pallas_call(
        factor_kernel,
        out_shape=jax.ShapeDtypeStruct((3 * HB, HB), F32),
        scratch_shapes=[pltpu.VMEM((HB, HB), F32)] * 3,
        cost_estimate=pl.CostEstimate(
            flops=200_000_000, transcendentals=0, bytes_accessed=80_000_000
        ),
        name="inverse_factor",
    )(block)


def inverse_pair(inv_ref):
    return split(
        jnp.concatenate(
            [
                jnp.concatenate([inv_ref[:HB, :], jnp.zeros((HB, HB), F32)], axis=1),
                jnp.concatenate([inv_ref[HB:PB, :], inv_ref[PB:, :]], axis=1),
            ],
            axis=0,
        )
    )


def solve_kernel(
    row_ref, noise_ref, own_ref, head_ref, need_ref, inv_ref, ctt_ref,
    pan_ref, lead_ref, err_ref,
):
    inv = inverse_pair(inv_ref)
    pan_ref[...] = mm3(split(own_ref[...]), inv, ((1,), (1,)))

    @pl.when(row_ref[0] == 0)
    def _():
        sub = lax.broadcasted_iota(jnp.int32, (PB, PB), 0)
        lane = lax.broadcasted_iota(jnp.int32, (PB, PB), 1)
        block = own_ref[:PB] + jnp.where(sub == lane, noise_ref[:, :PB], 0.0)
        lead = mm3(split(block), inv, ((1,), (1,)))
        pan_ref[:PB, :] = jnp.where(lane > sub, 0.0, lead)

    head = mm3(inv, split(head_ref[...]))
    need = mm3(inv, split(need_ref[...]))
    lead_ref[...] = head
    err_ref[...] = ctt_ref[...] - mm3(split(need), split(head), ((0,), (0,)))


def columns_kernel(rows_ref, inv_ref, u_ref):
    u_ref[0], u_ref[1] = split(mm3(inverse_pair(inv_ref), split(rows_ref[...]), ((1,), (1,))))


def update_kernel(
    place_ref, noise_ref, a_ref, t_ref, pan_ref, mine_ref, other_ref, head_ref, inv_ref,
    upd_ref, rec_ref, u_ref, pair_ref,
):
    i = pl.program_id(0)
    row, col = place_ref[0], place_ref[1]
    core = lax.rem(row, 2)
    tile, width = upd_ref.shape
    half = width // 2

    @pl.when(i == 0)
    def _():
        u = split(mm3(inverse_pair(inv_ref), split(other_ref[...]), ((1,), (1,))))
        theirs = pl.ds(pl.multiple_of((1 - core) * half, HB), half)
        ours = pl.ds(pl.multiple_of(core * half, HB), half)
        for part in range(2):
            u_ref[part, :, theirs] = u[part]
            u_ref[part, :, ours] = mine_ref[part]
        pair_ref[0], pair_ref[1] = split(head_ref[...])

    pair = split(pan_ref[...])
    here = pl.ds(pl.multiple_of(i * tile, tile), tile)
    upd_ref[...] = a_ref[...] - mm3(pair, (u_ref[0], u_ref[1]))
    rec_ref[...] = t_ref[...] - mm3(pair, (pair_ref[0], pair_ref[1]))

    @pl.when(lax.div(row, 2) == col)
    def _():
        block = pl.ds(pl.multiple_of(core * half + i * tile, HB), tile)
        eye = lax.broadcasted_iota(jnp.int32, (tile, tile), 0) == lax.broadcasted_iota(
            jnp.int32, (tile, tile), 1
        )
        upd_ref[:, block] = upd_ref[:, block] + jnp.where(eye, noise_ref[...], 0.0)

    @pl.when((row == 0) & (i * tile < PB))
    def _():
        upd_ref[...] = jnp.zeros_like(upd_ref)
        rec_ref[...] = head_ref[here, :]

    @pl.when(col == 0)
    def _():
        upd_ref[:, :PB] = pan_ref[...]


SMEM = pl.BlockSpec(memory_space=pltpu.SMEM)
VMEM = pl.BlockSpec(memory_space=pltpu.VMEM)


def solve(place, noise, own, head, need, inv, ctt):
    return pl.pallas_call(
        solve_kernel,
        in_specs=[SMEM] + [VMEM] * 6,
        out_specs=[VMEM] * 3,
        out_shape=[jax.ShapeDtypeStruct(x.shape, F32) for x in (own, head, ctt)],
        cost_estimate=pl.CostEstimate(
            flops=600_000_000, transcendentals=0, bytes_accessed=3_000_000
        ),
        name="solve",
    )(place, noise[None, :], own, head, need, inv, ctt)


def solve_columns(rows, inv):
    return pl.pallas_call(
        columns_kernel,
        in_specs=[VMEM] * 2,
        out_specs=VMEM,
        out_shape=jax.ShapeDtypeStruct((2, PB, rows.shape[0]), jnp.bfloat16),
        cost_estimate=pl.CostEstimate(
            flops=300_000_000, transcendentals=0, bytes_accessed=2_000_000
        ),
        name="solve_columns",
    )(rows, inv)


def update(place, noise, covariance, targets, panel, mine, other, head, inv):
    rows, width = covariance.shape
    tile = 128
    target_width = targets.shape[1]
    tiled = lambda n: pl.BlockSpec((tile, n), lambda i: (i, 0))
    return pl.pallas_call(
        update_kernel,
        grid=(rows // tile,),
        in_specs=[
            SMEM, pl.BlockSpec((1, tile), lambda i: (0, i)), tiled(width), tiled(target_width),
            tiled(PB), VMEM, VMEM, VMEM, VMEM,
        ],
        out_specs=[tiled(width), tiled(target_width)],
        out_shape=[
            jax.ShapeDtypeStruct((rows, width), F32),
            jax.ShapeDtypeStruct((rows, target_width), F32),
        ],
        scratch_shapes=[
            pltpu.VMEM((2, PB, width), jnp.bfloat16),
            pltpu.VMEM((2, PB, target_width), jnp.bfloat16),
        ],
        compiler_params=pltpu.CompilerParams(vmem_limit_bytes=32 << 20),
        cost_estimate=pl.CostEstimate(
            flops=3_000_000_000, transcendentals=0, bytes_accessed=12_000_000
        ),
        name="update",
    )(
        place,
        noise[None, :],
        pltpu.with_memory_space_constraint(covariance, pltpu.HBM),
        pltpu.with_memory_space_constraint(targets, pltpu.HBM),
        panel, mine, other, head, inv,
    )


def device(x, z_lo, y, z_hi, core):
    return (x * 2 + z_lo) * 16 + y * 4 + z_hi * 2 + core


def spread(value):
    four, two = range(4), range(2)
    index = lax.axis_index("col") * 16 + lax.axis_index("row")
    value = jnp.where(index == 0, value, 0.0)
    rounds = (
        [[(device(0, 0, 0, 0, 0), device(k, 0, 0, 0, 0))] for k in (2, 1, 3)],
        [[(device(x, 0, 0, 0, 0), device(x, 0, k, 0, 0)) for x in four] for k in (2, 1, 3)],
        [
            [(device(x, 0, y, 0, 0), device(x, lo, y, hi, 0)) for x in four for y in four]
            for lo, hi in ((0, 1), (1, 1), (1, 0))
        ],
        [
            [
                (device(x, lo, y, hi, 0), device(x, lo, y, hi, 1))
                for x in four for y in four for lo in two for hi in two
            ]
        ],
    )
    values = []
    for perms in rounds:
        value = sum([lax.ppermute(value, BOTH, perm) for perm in perms], value)
        values.append(value)
    return values


def target_covariance(pos_rows, pos_cols, low, strength, scale):
    distance = (pos_rows[0][:, None] - pos_cols[0][None, :]) ** 2 + (
        pos_rows[1][:, None] - pos_cols[1][None, :]
    ) ** 2
    levels = jnp.arange(strength.shape[0], dtype=jnp.int32)
    weights = strength[:, None, None] / (1.0 + distance[None] / (scale * scale)[:, None, None])
    return jnp.sum(jnp.where(levels[:, None, None] <= low[None, None, :], weights, 0.0), axis=0)


def local(covariance, wfs_map, noise_var, targets, target_pos, strength, scale, tile_layer):
    rows, width = covariance.shape
    target_width = targets.shape[1]
    row, col = lax.axis_index("row"), lax.axis_index("col")
    four, eight, two = range(4), range(8), range(2)
    same_core = [[2 * m + k for m in eight] for k in two]
    swap_places = [
        (c * 16 + 2 * m + k, m * 16 + 2 * c + k) for c in eight for m in eight for k in two
    ]

    panel_in = covariance[:, :PB]
    chunk = lax.all_to_all(panel_in, "col", 0, 0, tiled=True)[: rows // 8]

    noise = jnp.sum(
        jnp.where(
            wfs_map[:, None] == jnp.arange(noise_var.shape[0], dtype=jnp.int32)[None, :],
            noise_var[None, :],
            0.0,
        ),
        axis=1,
    )
    block_ids = jnp.arange(PB, dtype=jnp.int32)
    waves = spread(
        covariance[:PB, :PB]
        + jnp.where(block_ids[:, None] == block_ids[None, :], noise[:PB, None], 0.0)
    )

    own = lax.all_to_all(jnp.tile(chunk, (8, 1)), "col", 0, 0, tiled=True)
    turned = lax.ppermute(chunk, BOTH, swap_places)
    turned, _ = lax.optimization_barrier((turned, own))
    turned = jnp.tile(turned, (8, 1))
    lead, turned = lax.optimization_barrier((waves[-1], turned))
    inv = inverse_of_factor(lead)
    mine = lax.all_to_all(turned, "row", 0, 0, axis_index_groups=same_core, tiled=True)

    head, _ = lax.optimization_barrier((jnp.where(row == 0, targets[:PB], 0.0), waves[2]))
    for perms in (
        [[(0, 4 * y)] for y in (2, 1, 3)],
        [[(4 * y, 4 * y + 2) for y in four]],
        [[(2 * m, 2 * m + 1) for m in eight]],
    ):
        head = sum([lax.ppermute(head, "row", perm) for perm in perms], head)
    need = lax.ppermute(
        jnp.where(lax.rem(row, 2) == 0, head[:, :HB], head[:, HB:]), BOTH, swap_places
    )

    start = row * TILE
    pos_rows = lax.dynamic_slice_in_dim(target_pos, start, TILE, 1)
    pos_cols = lax.dynamic_slice_in_dim(target_pos, col * target_width, target_width, 1)
    level_cols = lax.dynamic_slice_in_dim(tile_layer, col * (target_width // TILE), target_width // TILE, 0)
    level_row = lax.dynamic_slice_in_dim(tile_layer, row, 1, 0)
    low = jnp.repeat(jnp.minimum(level_row, level_cols), TILE)
    ctt = target_covariance(pos_rows, pos_cols, low, strength, scale)

    place = jnp.stack([row, col]).astype(jnp.int32)
    panel, head, error = solve(place, noise, own, head, need, inv, ctt)
    mine, inv = lax.optimization_barrier((mine, inv))
    other = lax.ppermute(mine, "row", [(i, i ^ 1) for i in range(16)])
    mine = solve_columns(mine, inv)
    updated, reconstructor = update(
        place, noise, covariance, targets, panel, mine, other, head, inv
    )
    return updated, panel, reconstructor, error


def solution(mesh):
    placed = (P("row", "col"), P("row"), P(), P("row", "col"), P(), P(), P(), P())
    return jax.shard_map(
        local,
        mesh=mesh,
        in_specs=placed,
        out_specs=(P("row", "col"), P("row", None), P("row", "col"), P("row", "col")),
        check_vma=False,
    )
```

time: 97.1 us -> 113 us (1.16)
  the two profiles are of different devices: /device:TPU:1 before, /device:TPU:24 now
where the time goes in v2:
time: 113 us; the launch traced here: 112 us
  starting transfers between devices  48 us (42%)
  Pallas kernels  29.7 us (26%)
  waiting for transfers between devices  13 us (12%)
  local copies, waits for them, and re-layouts  12 us (11%)
  other arithmetic  8.17 us (7%)
    pallas_call x1, Pallas kernels, inverse_of_factor(): pl.pallas_call(factor_kernel, out_shape=jax.ShapeDtypeStruct((3 * HB, HB)...  15.8 us
    ppermute x1, starting transfers between devices, local(): turned = lax.ppermute(chunk, BOTH, swap_places)  11.8 us
    ppermute x10, starting transfers between devices, spread(): value = sum([lax.ppermute(value, BOTH, perm) for perm in perms], value)  9.9 us
    ppermute x5, starting transfers between devices, local(): head = sum([lax.ppermute(head, 'row', perm) for perm in perms], head)  8.11 us
    pallas_call x1, Pallas kernels, update(): pl.pallas_call(update_kernel, grid=(rows // tile,), in_specs=[SMEM, pl.Bl...  8.08 us
    ppermute x10, waiting for transfers between devices, spread(): value = sum([lax.ppermute(value, BOTH, perm) for perm in perms], value)  7.02 us
    ppermute x1, waiting for transfers between devices, local(): lax.ppermute(jnp.where(lax.rem(row, 2) == 0, head[:, :HB], head[:, HB:]),...  6 us
    all_to_all x1, starting transfers between devices, local(): chunk = lax.all_to_all(panel_in, 'col', 0, 0, tiled=True)[:rows // 8]  5.65 us
  transfers between devices with their start and end apart: 21, of which 3 were waited for; matrix products, arithmetic and copies ran while one was open for 12% of the time, Pallas kernels for 19%

profile of v2, /device:TPU:24, one launch (start us, length us, event | category | flops | bytes accessed | tf_op | source)
XLA Modules:
  0.0 112.0 jit_solution(7148748169898482941)
XLA Ops:
  0.6 0.8 select_reduce_fusion
  1.5 1.1 add_select_fusion
  2.5 0.7 collective-permute-start.1
  3.2 0.7 collective-permute-start.2
  3.9 0.7 collective-permute-start
  4.6 2.1 %slice.38 = f32[768,256]{1,0:T(8,128)} slice(f32[768,1536]{1,0:T(8,128)} %a_ref.1), slice={[0:768], [0:256]} | slice | bytes 1572864 | tf_op jit(solution)/shard_map/slice | solution.py:299
  6.6 5.7 %all-to-all-start = ((f32[8,96,256]{2,1,0:T(8,128)}), f32[8,96,256]{2,1,0:T(8,128)S(1)}, u32[]{:S(2)}, u32[]{:S(2)}) async-start(f32[8,96,256]{2,1,0:T(8,128)} %bitcast.2), calls=%async_computation | async-start | bytes 1572864 | tf_op jit(solution)/shard_map/all_to_all | solution.py:300
  12.3 1.1 add_add_fusion.3
  13.4 1.3 %collective-permute-start.5 = (f32[256,256]{1,0:T(8,128)S(1)}, f32[256,256]{1,0:T(8,128)S(1)}, u32[]{:S(2)}, u32[]{:S(2)}) collective-permute-start(f32[256,256]{1,0:T(8,128)S(1)} %add_add_fusion.3), channel_id=1, source_target_pairs={{0,12},{32,44},{64,76},{96,108}} | collective-permute-start | bytes 786440 | tf_op jit(solution)/shard_map/ppermute | solution.py:275
  14.7 0.7 collective-permute-start.4
  15.4 0.7 collective-permute-start.3
  16.1 0.6 dynamic_slice.12
  16.6 1.0 slice_select_fusion
  17.6 5.2 %collective-permute-done.5 = f32[256,256]{1,0:T(8,128)S(1)} collective-permute-done((f32[256,256]{1,0:T(8,128)S(1)}, f32[256,256]{1,0:T(8,128)S(1)}, u32[]{:S(2)}, u32[]{:S(2)}) %collective-permute-start.5) | collective-permute-done | bytes 262176 | tf_op jit(solution)/shard_map/ppermute | solution.py:275
  22.9 1.3 %collective-permute-start.8 = (f32[256,256]{1,0:T(8,128)S(1)}, f32[256,256]{1,0:T(8,128)S(1)}, u32[]{:S(2)}, u32[]{:S(2)}) collective-permute-start(f32[256,256]{1,0:T(8,128)S(1)} %add_add_fusion.2), channel_id=1, source_target_pairs={{0,16},{4,20},{8,24},{12,28},{32,48},{36,52},{40,56},{44,60},{64,8... | collective-permute-start | bytes 786440 | tf_op jit(solution)/shard_map/ppermute | solution.py:275
  24.2 1.3 %collective-permute-start.7 = (f32[256,256]{1,0:T(8,128)S(1)}, f32[256,256]{1,0:T(8,128)S(1)}, u32[]{:S(2)}, u32[]{:S(2)}) collective-permute-start(f32[256,256]{1,0:T(8,128)S(1)} %add_add_fusion.2), channel_id=1, source_target_pairs={{0,18},{4,22},{8,26},{12,30},{32,50},{36,54},{40,58},{44,62},{64,8... | collective-permute-start | bytes 786440 | tf_op jit(solution)/shard_map/ppermute | solution.py:275
  25.6 1.3 %collective-permute-start.6 = (f32[256,256]{1,0:T(8,128)S(1)}, f32[256,256]{1,0:T(8,128)S(1)}, u32[]{:S(2)}, u32[]{:S(2)}) collective-permute-start(f32[256,256]{1,0:T(8,128)S(1)} %add_add_fusion.2), channel_id=1, source_target_pairs={{0,2},{4,6},{8,10},{12,14},{32,34},{36,38},{40,42},{44,46},{64,66}... | collective-permute-start | bytes 786440 | tf_op jit(solution)/shard_map/ppermute | solution.py:275
  26.9 0.7 dynamic-slice_minimum_fusion
  27.6 0.9 tile.9
  28.6 4.8 %all-to-all-start.1 = ((f32[8,96,256]{2,1,0:T(8,128)}), f32[8,96,256]{2,1,0:T(8,128)S(1)}, u32[]{:S(2)}, u32[]{:S(2)}) async-start(f32[8,96,256]{2,1,0:T(8,128)} %tile.9), calls=%async_computation.1 | async-start | bytes 1572864 | tf_op jit(solution)/shard_map/all_to_all | solution.py:316
  33.4 1.8 %collective-permute-done.6 = f32[256,256]{1,0:T(8,128)S(1)} collective-permute-done((f32[256,256]{1,0:T(8,128)S(1)}, f32[256,256]{1,0:T(8,128)S(1)}, u32[]{:S(2)}, u32[]{:S(2)}) %collective-permute-start.6) | collective-permute-done | bytes 262176 | tf_op jit(solution)/shard_map/ppermute | solution.py:275
  35.2 1.3 %collective-permute-start.11 = (f32[256,256]{1,0:T(8,128)S(1)}, f32[256,256]{1,0:T(8,128)S(1)}, u32[]{:S(2)}, u32[]{:S(2)}) collective-permute-start(f32[256,256]{1,0:T(8,128)S(1)} %slice_select_fusion), channel_id=1, source_target_pairs={{0,12},{16,28},{32,44},{48,60},{64,76},{80,92},{96,108},{112,124}} | collective-permute-start | bytes 786440 | tf_op jit(solution)/shard_map/ppermute | solution.py:330
  36.5 0.7 collective-permute-start.10
  37.2 0.7 collective-permute-start.9
  38.0 11.8 %collective-permute-start.16 = (f32[96,256]{1,0:T(8,128)S(1)}, f32[96,256]{1,0:T(8,128)S(1)}, u32[]{:S(2)}, u32[]{:S(2)}) collective-permute-start(f32[96,256]{1,0:T(8,128)S(1)} %slice_bitcast_fusion), channel_id=1, source_target_pairs={{0,0},{1,1},{2,16},{3,17},{4,32},{5,33},{6,48},{7,49},{8,64},{9,65... | collective-permute-start | bytes 294920 | tf_op jit(solution)/shard_map/ppermute | solution.py:317
  49.8 1.3 %collective-permute-start.15 = (f32[256,256]{1,0:T(8,128)S(1)}, f32[256,256]{1,0:T(8,128)S(1)}, u32[]{:S(2)}, u32[]{:S(2)}) collective-permute-start(f32[256,256]{1,0:T(8,128)S(1)} %add_add_fusion.1), channel_id=1, source_target_pairs={{0,1},{2,3},{16,17},{18,19},{4,5},{6,7},{20,21},{22,23},{8,9},{10,... | collective-permute-start | bytes 786440 | tf_op jit(solution)/shard_map/ppermute | solution.py:275
  51.2 4.2 %collective-permute-start.12 = (f32[256,256]{1,0:T(8,128)S(1)}, f32[256,256]{1,0:T(8,128)S(1)}, u32[]{:S(2)}, u32[]{:S(2)}) collective-permute-start(f32[256,256]{1,0:T(8,128)S(1)} %add_add_fusion), channel_id=1, source_target_pairs={{0,2},{4,6},{8,10},{12,14},{16,18},{20,22},{24,26},{28,30},{32,34}... | collective-permute-start | bytes 786440 | tf_op jit(solution)/shard_map/ppermute | solution.py:330
  55.4 0.7 constant_dynamic-slice_fusion.1
  56.1 0.7 add.92.d_ref
  56.8 1.0 tile.20
  57.9 5.1 %all-to-all-start.2 = ((f32[8,96,256]{2,1,0:T(8,128)}), f32[8,96,256]{2,1,0:T(8,128)S(1)}, u32[]{:S(2)}, u32[]{:S(2)}) async-start(f32[8,96,256]{2,1,0:T(8,128)} %bitcast.12), calls=%async_computation.2 | async-start | bytes 1572864 | tf_op jit(solution)/shard_map/all_to_all | solution.py:322
  63.0 1.3 %collective-permute-start.13 = (f32[256,256]{1,0:T(8,128)S(1)}, f32[256,256]{1,0:T(8,128)S(1)}, u32[]{:S(2)}, u32[]{:S(2)}) collective-permute-start(f32[256,256]{1,0:T(8,128)S(1)} %add.90), channel_id=1, source_target_pairs={{0,1},{2,3},{4,5},{6,7},{8,9},{10,11},{12,13},{14,15},{16,17},{18,... | collective-permute-start | bytes 786440 | tf_op jit(solution)/shard_map/ppermute | solution.py:330
  64.3 0.8 constant_dynamic-slice_fusion
  65.3 15.8 %inverse_factor.1.inv_ref = f32[384,128]{1,0:T(8,128)} custom-call(f32[256,256]{1,0:T(8,128)} %add.92.d_ref), custom_call_target="tpu_custom_call" | custom-call | flops 200000000 | bytes 80000000 | tf_op jit(solution)/shard_map/inverse_factor/pallas_call | solution.py:95
  81.2 2.6 %collective-permute-start.14 = (f32[256,128]{1,0:T(8,128)S(1)}, f32[256,128]{1,0:T(8,128)S(1)}, u32[]{:S(2)}, u32[]{:S(2)}) collective-permute-start(f32[256,128]{1,0:T(8,128)S(1)} %slice_select_fusion.1), channel_id=1, source_target_pairs={{0,0},{1,1},{2,16},{3,17},{4,32},{5,33},{6,48},{7,49},{8,64},{9,65... | collective-permute-start | bytes 393224 | tf_op jit(solution)/shard_map/ppermute | solution.py:331
  83.9 1.8 %fusion.2.ctt_ref = f32[128,256]{1,0:T(8,128)} fusion(f32[35]{0:T(128)S(1)} %mul.19, f32[128,256]{1,0:T(8,128)S(1)} %multiply_add_fusion, f32[35]{0:T(128)S(1)} %copy-done.9, pred[35,256]{1,0:T(8,128)(4,1)S(1)} %iota_compare_fusion.1), kind=kLoop, calls=%fused_computation.3 | loop fusion | flops 5701632 | bytes 271384 | tf_op jit(solution)/shard_map/reduce_sum | solution.py:286
  85.7 0.6 broadcast_in_dim.58.noise_ref
  86.3 0.7 pad_add_fusion.row_ref.place_ref
  86.9 6.0 %collective-permute-done.14.need_ref = f32[256,128]{1,0:T(8,128)S(1)} collective-permute-done((f32[256,128]{1,0:T(8,128)S(1)}, f32[256,128]{1,0:T(8,128)S(1)}, u32[]{:S(2)}, u32[]{:S(2)}) %collective-permute-start.14) | collective-permute-done | bytes 131104 | tf_op jit(solution)/shard_map/ppermute | solution.py:331
  92.9 0.7 copy-done.11
  93.6 3.2 %solve.1 = (f32[768,256]{1,0:T(8,128)}, f32[256,256]{1,0:T(8,128)}, f32[128,256]{1,0:T(8,128)}) custom-call(s32[2]{0:T(128)} %pad_add_fusion.row_ref.place_ref, f32[1,768]{1,0:T(1,128)} %broadcast_in_dim.58.noise_ref, f32[768,256]{1,0:T(8,128)} %bitcast.20, f32[256,256]{1,0:T(8,128)} %copy-done.7, f32[256,128]{1,0:T(8,128)} %copy-done.11, ...), custom_call_target="tpu_custom_call" | custom-call | flops 600000000 | bytes 3000000 | tf_op jit(solution)/shard_map/solve/pallas_call | solution.py:191
  96.8 2.6 %solve_columns.1.mine_ref = bf16[2,256,768]{2,1,0:T(8,128)(2,1)} custom-call(f32[768,256]{1,0:T(8,128)} %bitcast.19, f32[384,128]{1,0:T(8,128)} %inverse_factor.1.inv_ref), custom_call_target="tpu_custom_call" | custom-call | flops 300000000 | bytes 2000000 | tf_op jit(solution)/shard_map/solve_columns/pallas_call | solution.py:204
  99.4 1.1 %copy-done = bf16[2,256,768]{2,1,0:T(8,128)(2,1)S(1)} copy-done((bf16[2,256,768]{2,1,0:T(8,128)(2,1)S(1)}, bf16[2,256,768]{2,1,0:T(8,128)(2,1)}, u32[]{:S(2)}) %copy-start) | copy-done | bytes 786456
  100.5 0.7 copy-done.2
  101.2 1.1 %copy-done.3 = f32[768,256]{1,0:T(8,128)S(1)} copy-done((f32[768,256]{1,0:T(8,128)S(1)}, f32[768,256]{1,0:T(8,128)}, u32[]{:S(2)}) %copy-start.3) | copy-done | bytes 786456
  102.3 0.7 copy-done.4
  103.0 0.9 copy-done.5
  103.9 8.1 %update.1 = (f32[768,1536]{1,0:T(8,128)}, f32[768,256]{1,0:T(8,128)}) custom-call(s32[2]{0:T(128)S(1)} %copy-done.4, f32[1,768]{1,0:T(1,128)S(1)} %copy-done.2, f32[768,1536]{1,0:T(8,128)} %a_ref.1, f32[768,256]{1,0:T(8,128)} %t_ref.1, f32[768,256]{1,0:T(8,128)S(1)} %copy-done.3, bf16[2,256,768]{2,1,0:T(8,128)(2,1)S(1)} %copy-done, ...), custom_call_target="tpu_custom_call" | custom-call | flops 3000000000 | bytes 12000000 | tf_op jit(solution)/shard_map/update/pallas_call | solution.py:221
  (52 shorter events, 0.7 us)
Async XLA Ops:
  0.6 15.4 %copy-start.10 = (s32[16]{0:T(128)S(1)}, s32[16]{0:T(128)}, u32[]{:S(2)}) copy-start(s32[16]{0:T(128)} %param.15) | copy-start | bytes 196
  2.5 9.8 %collective-permute-start.1 = (f32[256,256]{1,0:T(8,128)S(1)}, f32[256,256]{1,0:T(8,128)S(1)}, u32[]{:S(2)}, u32[]{:S(2)}) collective-permute-start(f32[256,256]{1,0:T(8,128)S(1)} %add_select_fusion), channel_id=1, source_target_pairs={{0,32}} | collective-permute-start | bytes 786440 | tf_op jit(solution)/shard_map/ppermute | solution.py:275
  3.2 9.1 %collective-permute-start.2 = (f32[256,256]{1,0:T(8,128)S(1)}, f32[256,256]{1,0:T(8,128)S(1)}, u32[]{:S(2)}, u32[]{:S(2)}) collective-permute-start(f32[256,256]{1,0:T(8,128)S(1)} %add_select_fusion), channel_id=1, source_target_pairs={{0,96}} | collective-permute-start | bytes 786440 | tf_op jit(solution)/shard_map/ppermute | solution.py:275
  3.9 8.4 %collective-permute-start = (f32[256,256]{1,0:T(8,128)S(1)}, f32[256,256]{1,0:T(8,128)S(1)}, u32[]{:S(2)}, u32[]{:S(2)}) collective-permute-start(f32[256,256]{1,0:T(8,128)S(1)} %add_select_fusion), channel_id=1, source_target_pairs={{0,64}} | collective-permute-start | bytes 786440 | tf_op jit(solution)/shard_map/ppermute | solution.py:275
  6.6 21.0 %all-to-all-start = ((f32[8,96,256]{2,1,0:T(8,128)}), f32[8,96,256]{2,1,0:T(8,128)S(1)}, u32[]{:S(2)}, u32[]{:S(2)}) async-start(f32[8,96,256]{2,1,0:T(8,128)} %bitcast.2), calls=%async_computation | async-start | bytes 1572864 | tf_op jit(solution)/shard_map/all_to_all | solution.py:300
  13.4 9.5 %collective-permute-start.5 = (f32[256,256]{1,0:T(8,128)S(1)}, f32[256,256]{1,0:T(8,128)S(1)}, u32[]{:S(2)}, u32[]{:S(2)}) collective-permute-start(f32[256,256]{1,0:T(8,128)S(1)} %add_add_fusion.3), channel_id=1, source_target_pairs={{0,12},{32,44},{64,76},{96,108}} | collective-permute-start | bytes 786440 | tf_op jit(solution)/shard_map/ppermute | solution.py:275
  14.7 8.2 %collective-permute-start.4 = (f32[256,256]{1,0:T(8,128)S(1)}, f32[256,256]{1,0:T(8,128)S(1)}, u32[]{:S(2)}, u32[]{:S(2)}) collective-permute-start(f32[256,256]{1,0:T(8,128)S(1)} %add_add_fusion.3), channel_id=1, source_target_pairs={{0,4},{32,36},{64,68},{96,100}} | collective-permute-start | bytes 786440 | tf_op jit(solution)/shard_map/ppermute | solution.py:275
  15.4 7.5 %collective-permute-start.3 = (f32[256,256]{1,0:T(8,128)S(1)}, f32[256,256]{1,0:T(8,128)S(1)}, u32[]{:S(2)}, u32[]{:S(2)}) collective-permute-start(f32[256,256]{1,0:T(8,128)S(1)} %add_add_fusion.3), channel_id=1, source_target_pairs={{0,8},{32,40},{64,72},{96,104}} | collective-permute-start | bytes 786440 | tf_op jit(solution)/shard_map/ppermute | solution.py:275
  22.9 10.4 %collective-permute-start.8 = (f32[256,256]{1,0:T(8,128)S(1)}, f32[256,256]{1,0:T(8,128)S(1)}, u32[]{:S(2)}, u32[]{:S(2)}) collective-permute-start(f32[256,256]{1,0:T(8,128)S(1)} %add_add_fusion.2), channel_id=1, source_target_pairs={{0,16},{4,20},{8,24},{12,28},{32,48},{36,52},{40,56},{44,60},{64,8... | collective-permute-start | bytes 786440 | tf_op jit(solution)/shard_map/ppermute | solution.py:275
  24.2 9.1 %collective-permute-start.7 = (f32[256,256]{1,0:T(8,128)S(1)}, f32[256,256]{1,0:T(8,128)S(1)}, u32[]{:S(2)}, u32[]{:S(2)}) collective-permute-start(f32[256,256]{1,0:T(8,128)S(1)} %add_add_fusion.2), channel_id=1, source_target_pairs={{0,18},{4,22},{8,26},{12,30},{32,50},{36,54},{40,58},{44,62},{64,8... | collective-permute-start | bytes 786440 | tf_op jit(solution)/shard_map/ppermute | solution.py:275
  25.6 9.6 %collective-permute-start.6 = (f32[256,256]{1,0:T(8,128)S(1)}, f32[256,256]{1,0:T(8,128)S(1)}, u32[]{:S(2)}, u32[]{:S(2)}) collective-permute-start(f32[256,256]{1,0:T(8,128)S(1)} %add_add_fusion.2), channel_id=1, source_target_pairs={{0,2},{4,6},{8,10},{12,14},{32,34},{36,38},{40,42},{44,46},{64,66}... | collective-permute-start | bytes 786440 | tf_op jit(solution)/shard_map/ppermute | solution.py:275
  27.6 37.6 %copy-start.12 = (f32[35]{0:T(128)S(1)}, f32[35]{0:T(128)}, u32[]{:S(2)}) copy-start(f32[35]{0:T(128)} %param.14) | copy-start | bytes 424
  28.6 28.3 %all-to-all-start.1 = ((f32[8,96,256]{2,1,0:T(8,128)}), f32[8,96,256]{2,1,0:T(8,128)S(1)}, u32[]{:S(2)}, u32[]{:S(2)}) async-start(f32[8,96,256]{2,1,0:T(8,128)} %tile.9), calls=%async_computation.1 | async-start | bytes 1572864 | tf_op jit(solution)/shard_map/all_to_all | solution.py:316
  33.4 50.5 %copy-start.9 = (f32[35]{0:T(128)S(1)}, f32[35]{0:T(128)}, u32[]{:S(2)}) copy-start(f32[35]{0:T(128)} %param.13) | copy-start | bytes 424
  35.2 15.9 %collective-permute-start.11 = (f32[256,256]{1,0:T(8,128)S(1)}, f32[256,256]{1,0:T(8,128)S(1)}, u32[]{:S(2)}, u32[]{:S(2)}) collective-permute-start(f32[256,256]{1,0:T(8,128)S(1)} %slice_select_fusion), channel_id=1, source_target_pairs={{0,12},{16,28},{32,44},{48,60},{64,76},{80,92},{96,108},{112,124}} | collective-permute-start | bytes 786440 | tf_op jit(solution)/shard_map/ppermute | solution.py:330
  36.5 14.6 %collective-permute-start.10 = (f32[256,256]{1,0:T(8,128)S(1)}, f32[256,256]{1,0:T(8,128)S(1)}, u32[]{:S(2)}, u32[]{:S(2)}) collective-permute-start(f32[256,256]{1,0:T(8,128)S(1)} %slice_select_fusion), channel_id=1, source_target_pairs={{0,4},{16,20},{32,36},{48,52},{64,68},{80,84},{96,100},{112,116}} | collective-permute-start | bytes 786440 | tf_op jit(solution)/shard_map/ppermute | solution.py:330
  37.2 13.9 %collective-permute-start.9 = (f32[256,256]{1,0:T(8,128)S(1)}, f32[256,256]{1,0:T(8,128)S(1)}, u32[]{:S(2)}, u32[]{:S(2)}) collective-permute-start(f32[256,256]{1,0:T(8,128)S(1)} %slice_select_fusion), channel_id=1, source_target_pairs={{0,8},{16,24},{32,40},{48,56},{64,72},{80,88},{96,104},{112,120}} | collective-permute-start | bytes 786440 | tf_op jit(solution)/shard_map/ppermute | solution.py:330
  38.0 18.9 %collective-permute-start.16 = (f32[96,256]{1,0:T(8,128)S(1)}, f32[96,256]{1,0:T(8,128)S(1)}, u32[]{:S(2)}, u32[]{:S(2)}) collective-permute-start(f32[96,256]{1,0:T(8,128)S(1)} %slice_bitcast_fusion), channel_id=1, source_target_pairs={{0,0},{1,1},{2,16},{3,17},{4,32},{5,33},{6,48},{7,49},{8,64},{9,65... | collective-permute-start | bytes 294920 | tf_op jit(solution)/shard_map/ppermute | solution.py:317
  49.8 6.3 %collective-permute-start.15 = (f32[256,256]{1,0:T(8,128)S(1)}, f32[256,256]{1,0:T(8,128)S(1)}, u32[]{:S(2)}, u32[]{:S(2)}) collective-permute-start(f32[256,256]{1,0:T(8,128)S(1)} %add_add_fusion.1), channel_id=1, source_target_pairs={{0,1},{2,3},{16,17},{18,19},{4,5},{6,7},{20,21},{22,23},{8,9},{10,... | collective-permute-start | bytes 786440 | tf_op jit(solution)/shard_map/ppermute | solution.py:275
  51.2 11.7 %collective-permute-start.12 = (f32[256,256]{1,0:T(8,128)S(1)}, f32[256,256]{1,0:T(8,128)S(1)}, u32[]{:S(2)}, u32[]{:S(2)}) collective-permute-start(f32[256,256]{1,0:T(8,128)S(1)} %add_add_fusion), channel_id=1, source_target_pairs={{0,2},{4,6},{8,10},{12,14},{16,18},{20,22},{24,26},{28,30},{32,34}... | collective-permute-start | bytes 786440 | tf_op jit(solution)/shard_map/ppermute | solution.py:330
  56.8 36.1 %copy-start.8 = (f32[8,96,256]{2,1,0:T(8,128)}, f32[8,96,256]{2,1,0:T(8,128)S(1)}, u32[]{:S(2)}) copy-start(f32[8,96,256]{2,1,0:T(8,128)S(1)} %all-to-all-done.1) | copy-start | bytes 2359300
  57.9 25.9 %all-to-all-start.2 = ((f32[8,96,256]{2,1,0:T(8,128)}), f32[8,96,256]{2,1,0:T(8,128)S(1)}, u32[]{:S(2)}, u32[]{:S(2)}) async-start(f32[8,96,256]{2,1,0:T(8,128)} %bitcast.12), calls=%async_computation.2 | async-start | bytes 1572864 | tf_op jit(solution)/shard_map/all_to_all | solution.py:322
  63.0 18.1 %collective-permute-start.13 = (f32[256,256]{1,0:T(8,128)S(1)}, f32[256,256]{1,0:T(8,128)S(1)}, u32[]{:S(2)}, u32[]{:S(2)}) collective-permute-start(f32[256,256]{1,0:T(8,128)S(1)} %add.90), channel_id=1, source_target_pairs={{0,1},{2,3},{4,5},{6,7},{8,9},{10,11},{12,13},{14,15},{16,17},{18,... | collective-permute-start | bytes 786440 | tf_op jit(solution)/shard_map/ppermute | solution.py:330
  81.1 18.2 %copy-start.1 = (f32[384,128]{1,0:T(8,128)S(1)}, f32[384,128]{1,0:T(8,128)}, u32[]{:S(2)}) copy-start(f32[384,128]{1,0:T(8,128)} %inverse_factor.1.inv_ref) | copy-start | bytes 589828
  81.2 11.8 %copy-start.7 = (f32[256,256]{1,0:T(8,128)}, f32[256,256]{1,0:T(8,128)S(1)}, u32[]{:S(2)}) copy-start(f32[256,256]{1,0:T(8,128)S(1)} %add.91.head_ref) | copy-start | bytes 786436
  81.2 11.7 %collective-permute-start.14 = (f32[256,128]{1,0:T(8,128)S(1)}, f32[256,128]{1,0:T(8,128)S(1)}, u32[]{:S(2)}, u32[]{:S(2)}) collective-permute-start(f32[256,128]{1,0:T(8,128)S(1)} %slice_select_fusion.1), channel_id=1, source_target_pairs={{0,0},{1,1},{2,16},{3,17},{4,32},{5,33},{6,48},{7,49},{8,64},{9,65... | collective-permute-start | bytes 393224 | tf_op jit(solution)/shard_map/ppermute | solution.py:331
  83.8 13.0 %copy-start.6 = (f32[8,96,256]{2,1,0:T(8,128)}, f32[8,96,256]{2,1,0:T(8,128)S(1)}, u32[]{:S(2)}) copy-start(f32[8,96,256]{2,1,0:T(8,128)S(1)} %all-to-all-done.2) | copy-start | bytes 2359300
  83.8 15.5 %collective-permute-start.17 = (f32[768,256]{1,0:T(8,128)S(1)}, f32[768,256]{1,0:T(8,128)S(1)}, u32[]{:S(2)}, u32[]{:S(2)}) collective-permute-start(f32[768,256]{1,0:T(8,128)S(1)} %bitcast.18), channel_id=1, source_target_pairs={{0,1},{1,0},{2,3},{3,2},{4,5},{5,4},{6,7},{7,6},{8,9},{9,8},{10,11... | collective-permute-start | bytes 2359304 | tf_op jit(solution)/shard_map/ppermute | solution.py:346
  92.9 0.7 copy-start.11
  99.4 1.1 %copy-start = (bf16[2,256,768]{2,1,0:T(8,128)(2,1)S(1)}, bf16[2,256,768]{2,1,0:T(8,128)(2,1)}, u32[]{:S(2)}) copy-start(bf16[2,256,768]{2,1,0:T(8,128)(2,1)} %solve_columns.1.mine_ref) | copy-start | bytes 2359300
  100.5 0.7 copy-start.2
  101.2 1.1 %copy-start.3 = (f32[768,256]{1,0:T(8,128)S(1)}, f32[768,256]{1,0:T(8,128)}, u32[]{:S(2)}) copy-start(f32[768,256]{1,0:T(8,128)} %get-tuple-element.12.pan_ref) | copy-start | bytes 2359300
  102.3 0.7 copy-start.4
  103.0 0.9 copy-start.5

commit v3 on v1

v3 whole, which is shorter than its diff:
```python
import functools

import jax
import jax.numpy as jnp
from jax import lax
from jax.experimental import pallas as pl
from jax.experimental.pallas import tpu as pltpu
from jax.sharding import PartitionSpec as P

PB = 256
HB = 128
TILE = 128
BOTH = ("col", "row")
precise = lax.Precision.HIGHEST
F32 = jnp.float32


def mm(a, b, dims=((1,), (0,))):
    return lax.dot_general(a, b, (dims, ((), ())), precision=precise, preferred_element_type=F32)


def split(x):
    hi = x.astype(jnp.bfloat16)
    return hi, (x - hi.astype(F32)).astype(jnp.bfloat16)


def left(x, axis=1):
    hi, lo = split(x)
    return jnp.concatenate([hi, hi, lo], axis=axis)


def right(x, axis=1):
    hi, lo = split(x)
    return jnp.concatenate([hi, lo, hi], axis=axis)


def dot3(a, b, dims=((1,), (0,))):
    return lax.dot_general(a, b, (dims, ((), ())), preferred_element_type=F32)


def inverse_factor(a_ref, w_ref):
    n = a_ref.shape[0]
    rows = lax.broadcasted_iota(jnp.int32, (n, n), 0)
    lanes = lax.broadcasted_iota(jnp.int32, (n, n), 1)
    groups = rows.reshape(n // 8, 8, n)
    w_ref[...] = jnp.where(rows == lanes, 1.0, 0.0).astype(F32)

    def pick(x, index):
        return jnp.take_along_axis(
            x, jnp.full(x.shape, index, jnp.int32), axis=1, mode="promise_in_bounds"
        )

    def step(it, carry):
        k = it * 4
        a = a_ref[...]
        c = [pick(a, k + t).reshape(n // 8, 8, n) for t in range(4)]
        a = a.reshape(n // 8, 8, n)
        w = w_ref[...].reshape(n // 8, 8, n)
        r = [jnp.broadcast_to(a_ref[pl.ds(k + t, 1), :], (8, n)) for t in range(4)]
        v = [jnp.broadcast_to(w_ref[pl.ds(k + t, 1), :], (8, n)) for t in range(4)]
        g = [[pick(r[t], k + s) for s in range(4)] for t in range(4)]
        inv = []
        for t in range(4):
            inv.append(1.0 / g[t][t])
            for s in range(t + 1, 4):
                m = g[t][s] * inv[t]
                for u in range(s, 4):
                    g[s][u] = g[s][u] - m * g[t][u]
                r[s] = r[s] - m * r[t]
                v[s] = v[s] - m * v[t]
        for t in range(4):
            m = c[t] * inv[t]
            for s in range(t + 1, 4):
                c[s] = c[s] - m * g[t][s]
            m = jnp.where(groups >= k + 4, m, 0.0)
            a = a - m * r[t]
            w = w - m * v[t]
        a_ref[...] = a.reshape(n, n)
        w_ref[...] = w.reshape(n, n)
        for t in range(4):
            d = g[t][t]
            y = lax.rsqrt(d)
            y = y * (1.5 - 0.5 * d * y * y)
            w_ref[pl.ds(k + t, 1), :] = (v[t] * y)[:1]
        return carry

    lax.fori_loop(0, n // 4, step, 0)


def factor_kernel(d_ref, out_ref, a_ref, w1_ref, w2_ref):
    a_ref[...] = d_ref[:HB, :HB]
    inverse_factor(a_ref, w1_ref)
    first = w1_ref[...]
    low = mm(d_ref[HB:, :HB], first, ((1,), (1,)))
    a_ref[...] = d_ref[HB:, HB:] - mm(low, low, ((1,), (1,)))
    inverse_factor(a_ref, w2_ref)
    second = w2_ref[...]
    out_ref[:HB, :] = first
    out_ref[HB:PB, :] = -mm(second, mm(low, first))
    out_ref[PB:, :] = second


def inverse_of_factor(block):
    return pl.pallas_call(
        factor_kernel,
        out_shape=jax.ShapeDtypeStruct((3 * HB, HB), F32),
        scratch_shapes=[pltpu.VMEM((HB, HB), F32)] * 3,
        compiler_params=pltpu.CompilerParams(vmem_limit_bytes=8 << 20),
        cost_estimate=pl.CostEstimate(
            flops=200_000_000, transcendentals=0, bytes_accessed=80_000_000
        ),
        name="inverse_factor",
    )(block)


def two_halves(ref, base):
    stack = ref[:, base : base + 24, :].reshape(-1, HB)
    half = stack.shape[0] // 2
    return jnp.concatenate([stack[:half], stack[half:]], axis=1)


def noise_row(noise_ref, wfs):
    noise = jnp.zeros(wfs.shape, F32)
    for s in range(noise_ref.shape[0]):
        noise = jnp.where(wfs == s, noise_ref[s], noise)
    return noise


def iotas():
    shape = (PB, PB)
    return lax.broadcasted_iota(jnp.int32, shape, 0), lax.broadcasted_iota(jnp.int32, shape, 1)


def solve_kernel(
    place_ref, noise_ref, wfs_ref, own_ref, inv_ref, a_ref, t_ref,
    pan_ref, inv3_ref, pair_ref, mine_ref, a_out, t_out, sems,
):
    copies = [
        pltpu.make_async_copy(a_ref, a_out, sems.at[0]),
        pltpu.make_async_copy(t_ref, t_out, sems.at[1]),
    ]
    for copy in copies:
        copy.start()
    inv = jnp.concatenate(
        [
            jnp.concatenate([inv_ref[:HB, :], jnp.zeros((HB, HB), F32)], axis=1),
            jnp.concatenate([inv_ref[HB:PB, :], inv_ref[PB:, :]], axis=1),
        ],
        axis=0,
    )
    inv3_ref[...] = left(inv)
    inv3 = inv3_ref[...]
    pan_ref[...] = dot3(right(two_halves(own_ref, 0)), inv3, ((1,), (1,)))

    @pl.when(place_ref[0] == 0)
    def _():
        sub, lane = iotas()
        noise = noise_row(noise_ref, wfs_ref[:, :PB])
        block = two_halves(own_ref, 0)[:PB] + jnp.where(sub == lane, noise, 0.0)
        lead = dot3(right(block), inv3, ((1,), (1,)))
        pan_ref[:PB, :] = jnp.where(lane > sub, 0.0, lead)

    pair_ref[...] = left(pan_ref[...])
    mine_ref[...] = right(dot3(inv3, right(two_halves(own_ref, 24)), ((1,), (1,))), axis=0)
    for copy in copies:
        copy.wait()


def solve(place, noise_var, wfs, own, inv, covariance, targets):
    rows = covariance.shape[0]
    anywhere = pl.BlockSpec(memory_space=pl.ANY)
    far = lambda x: pltpu.with_memory_space_constraint(x, pltpu.HBM)
    return pl.pallas_call(
        solve_kernel,
        in_specs=[SMEM, SMEM, VMEM, VMEM, VMEM, anywhere, anywhere],
        out_specs=[VMEM] * 6,
        out_shape=[
            pltpu.VMEM((rows, PB), F32),
            pltpu.VMEM((PB, 3 * PB), jnp.bfloat16),
            pltpu.VMEM((rows, 3 * PB), jnp.bfloat16),
            pltpu.VMEM((3 * PB, rows), jnp.bfloat16),
            pltpu.VMEM(covariance.shape, F32),
            pltpu.VMEM(targets.shape, F32),
        ],
        scratch_shapes=[pltpu.SemaphoreType.DMA((2,))],
        compiler_params=pltpu.CompilerParams(vmem_limit_bytes=20 << 20),
        cost_estimate=pl.CostEstimate(
            flops=1_000_000_000, transcendentals=0, bytes_accessed=6_000_000
        ),
        name="solve",
    )(place, noise_var, wfs[None, :], own, inv, far(covariance), far(targets))


def update_kernel(
    place_ref, noise_ref, wfs_ref, a_ref, t_ref, own_ref, other_ref, panel_ref, inv3_ref, pair_ref,
    mine_ref, ctt_ref, upd_ref, pan_ref, rec_ref, err_ref, theirs_ref, head_ref, head3_ref,
):
    i = pl.program_id(0)
    row, col = place_ref[0], place_ref[1]
    core = lax.rem(row, 2)
    tile, width = upd_ref.shape
    half = width // 2

    @pl.when(i == 0)
    def _():
        inv3 = inv3_ref[...]
        raw = right(two_halves(other_ref, 0))
        theirs_ref[...] = right(dot3(inv3, raw, ((1,), (1,))), axis=0)
        mine = own_ref[:, 52:56, :].reshape(PB, HB)
        other = other_ref[:, 28:32, :].reshape(PB, HB)
        first = jnp.where(core == 0, mine, other)
        last = jnp.where(core == 0, other, mine)
        head = dot3(inv3, right(jnp.concatenate([first, last], axis=1), axis=0))
        head_ref[...] = head
        head3_ref[...] = right(head, axis=0)
        need = dot3(inv3, right(own_ref[:, 48:52, :].reshape(PB, HB), axis=0))
        err_ref[...] = ctt_ref[...] - dot3(left(need, axis=0), head3_ref[...], ((0,), (0,)))

    here = pl.ds(pl.multiple_of(i * tile, tile), tile)
    pair = pair_ref[here, :]
    for at, ref in ((core, mine_ref), (1 - core, theirs_ref)):
        where = pl.ds(pl.multiple_of(at * half, half), half)
        upd_ref[:, where] = a_ref[here, where] - dot3(pair, ref[...])
    pan_ref[...] = panel_ref[here, :]
    rec_ref[...] = t_ref[here, :] - dot3(pair, head3_ref[...])

    @pl.when(lax.div(row, 2) == col)
    def _():
        where = pl.ds(pl.multiple_of(core * half + i * tile, PB), PB)
        sub, lane = iotas()
        noise = noise_row(noise_ref, wfs_ref[...])
        upd_ref[:, where] = upd_ref[:, where] + jnp.where(sub == lane, noise, 0.0)

    @pl.when((row == 0) & (i == 0))
    def _():
        upd_ref[...] = jnp.zeros_like(upd_ref)
        rec_ref[...] = head_ref[...]

    @pl.when(col == 0)
    def _():
        upd_ref[:, :PB] = panel_ref[here, :]


SMEM = pl.BlockSpec(memory_space=pltpu.SMEM)
VMEM = pl.BlockSpec(memory_space=pltpu.VMEM)


def update(place, noise_var, wfs, matrix, targets, own, other, solved, ctt):
    rows, width = matrix.shape
    target_width = targets.shape[1]
    tiled = lambda n: pl.BlockSpec((PB, n), lambda i: (i, 0))
    near = lambda x: pltpu.with_memory_space_constraint(x, pltpu.VMEM)
    return pl.pallas_call(
        update_kernel,
        grid=(rows // PB,),
        in_specs=[SMEM, SMEM, pl.BlockSpec((1, PB), lambda i: (0, i))]
        + [VMEM] * 9,
        out_specs=[
            tiled(width),
            tiled(PB),
            tiled(target_width),
            pl.BlockSpec(ctt.shape, lambda i: (0, 0)),
        ],
        out_shape=[
            jax.ShapeDtypeStruct((rows, width), F32),
            jax.ShapeDtypeStruct((rows, PB), F32),
            jax.ShapeDtypeStruct((rows, target_width), F32),
            jax.ShapeDtypeStruct(ctt.shape, F32),
        ],
        scratch_shapes=[
            pltpu.VMEM((3 * PB, width // 2), jnp.bfloat16),
            pltpu.VMEM((PB, target_width), F32),
            pltpu.VMEM((3 * PB, target_width), jnp.bfloat16),
        ],
        compiler_params=pltpu.CompilerParams(vmem_limit_bytes=20 << 20),
        cost_estimate=pl.CostEstimate(
            flops=2_000_000_000, transcendentals=0, bytes_accessed=7_000_000
        ),
        name="update",
    )(
        place, noise_var, wfs[None, :], near(matrix), near(targets), near(own), near(other),
        *[near(x) for x in solved], near(ctt),
    )


def device(x, z_lo, y, z_hi, core):
    return (x * 2 + z_lo) * 16 + y * 4 + z_hi * 2 + core


def spread(value, first):
    four, two = range(4), range(2)
    index = lax.axis_index("col") * 16 + lax.axis_index("row")
    value = jnp.where(index == 0, value, 0.0)
    rounds = (
        [[(device(0, 0, 0, 0, 0), device(k, 0, 0, 0, 0))] for k in (2, 1, 3)],
        [[(device(x, 0, 0, 0, 0), device(x, 0, k, 0, 0)) for x in four] for k in (2, 1, 3)],
        [
            [(device(x, 0, y, 0, 0), device(x, lo, y, hi, 0)) for x in four for y in four]
            for lo, hi in ((0, 1), (1, 1), (1, 0))
        ],
        [
            [
                (device(x, lo, y, hi, 0), device(x, lo, y, hi, 1))
                for x in four for y in four for lo in two for hi in two
            ]
        ],
    )
    waves = []
    for perms in rounds:
        parts = [lax.ppermute(value, BOTH, perm) for perm in perms]
        value = sum(parts, value)
        if not waves:
            value, _ = lax.optimization_barrier((value, first))
        waves.append(value)
    return waves


def target_covariance(pos_rows, pos_cols, low, strength, scale):
    distance = (pos_rows[0][:, None] - pos_cols[0][None, :]) ** 2 + (
        pos_rows[1][:, None] - pos_cols[1][None, :]
    ) ** 2
    levels = jnp.arange(strength.shape[0], dtype=jnp.int32)
    weights = strength[:, None, None] / (1.0 + distance[None] / (scale * scale)[:, None, None])
    return jnp.sum(jnp.where(levels[:, None, None] <= low[None, None, :], weights, 0.0), axis=0)


def local(covariance, wfs_map, noise_var, targets, target_pos, strength, scale, tile_layer):
    rows, width = covariance.shape
    target_width = targets.shape[1]
    row, col = lax.axis_index("row"), lax.axis_index("col")
    groups = [[c * 16 + 2 * m + k for c in range(8) for m in range(8)] for k in range(2)]
    exchange = lambda x: lax.all_to_all(
        x, BOTH, 0, 0, axis_index_groups=groups, tiled=True
    )

    second = lax.ppermute(targets[:PB, HB:], "row", [(0, 1)])
    half = jnp.where(row == 1, second, targets[:PB, :HB])
    half = jnp.pad(half.reshape(64, 4, HB), ((0, 0), (0, 4), (0, 0)))
    pieces = jnp.concatenate([covariance[:, :HB], covariance[:, HB:PB]], axis=0)
    pieces = jnp.concatenate([pieces.reshape(64, 24, HB), half], axis=1)

    noise = jnp.sum(
        jnp.where(
            wfs_map[:PB, None] == jnp.arange(noise_var.shape[0], dtype=jnp.int32)[None, :],
            noise_var[None, :],
            0.0,
        ),
        axis=1,
    )
    ids = jnp.arange(PB, dtype=jnp.int32)
    waves = spread(
        covariance[:PB, :PB] + jnp.where(ids[:, None] == ids[None, :], noise[:, None], 0.0),
        pieces,
    )
    held = exchange(pieces)
    held, _ = lax.optimization_barrier((held, waves[2]))
    held_panel = held[:8, :24]
    held_head = held.reshape(8, 8, 32, HB)[:, 0, 24:28]

    shape = lambda n: (8, 8, n, HB)
    over_m = lambda x: jnp.broadcast_to(x[None], shape(x.shape[1]))
    over_c = lambda x: jnp.broadcast_to(x[:, None], shape(x.shape[1]))
    wanted = jnp.concatenate(
        [over_m(held_panel), over_c(held_panel), over_m(held_head), over_c(held_head)], axis=2
    ).reshape(64, 56, HB)
    lead, _ = lax.optimization_barrier((waves[-1], wanted))
    inv = inverse_of_factor(lead)
    own, inv = lax.optimization_barrier((exchange(wanted), inv))
    other = lax.ppermute(own[:, 24:], "row", [(i, i ^ 1) for i in range(16)])

    start = row * TILE
    pos_rows = lax.dynamic_slice_in_dim(target_pos, start, TILE, 1)
    pos_cols = lax.dynamic_slice_in_dim(target_pos, col * target_width, target_width, 1)
    level_cols = lax.dynamic_slice_in_dim(tile_layer, col * (target_width // TILE), target_width // TILE, 0)
    level_row = lax.dynamic_slice_in_dim(tile_layer, row, 1, 0)
    low = jnp.repeat(jnp.minimum(level_row, level_cols), TILE)
    ctt = target_covariance(pos_rows, pos_cols, low, strength, scale)

    place = jnp.stack([row, col]).astype(jnp.int32)
    *solved, matrix, near_targets = solve(
        place, noise_var, wfs_map, own, inv, covariance, targets
    )
    return update(
        place, noise_var, wfs_map, matrix, near_targets, own, other, solved, ctt
    )


def solution(mesh):
    placed = (P("row", "col"), P("row"), P(), P("row", "col"), P(), P(), P(), P())
    return jax.shard_map(
        local,
        mesh=mesh,
        in_specs=placed,
        out_specs=(P("row", "col"), P("row", None), P("row", "col"), P("row", "col")),
        check_vma=False,
    )
```

time: 97.1 us -> 89.1 us (0.918)
  starting transfers between devices: 37.4 us -> 21.6 us
  waiting for transfers between devices: 18.1 us -> 28.4 us
  Pallas kernels: 26.6 us -> 23.5 us
    all_to_all x2, starting transfers between devices: 21.2 us -> 11.1 us  [local(): lax.all_to_all(x, BOTH, 0, 0, axis_index_groups=groups, tiled=True)]
    ppermute x10, waiting for transfers between devices: 0.03 us -> 7.62 us  [spread(): parts = [lax.ppermute(value, BOTH, perm) for perm in perms]]
    ppermute x1, starting transfers between devices: 7.59 us -> 1.84 us  [local(): other = lax.ppermute(own[:, 24:], 'row', [(i, i ^ 1) for i in range(16)])]
    ppermute x1, waiting for transfers between devices: 0.01 us -> 5.71 us  [local(): second = lax.ppermute(targets[:PB, HB:], 'row', [(0, 1)])]
    all_to_all x2, waiting for transfers between devices: 17.1 us -> 15.1 us  [local(): lax.all_to_all(x, BOTH, 0, 0, axis_index_groups=groups, tiled=True)]
    pallas_call x1, Pallas kernels: 15.8 us -> 14.2 us  [inverse_of_factor(): pl.pallas_call(factor_kernel, out_shape=jax.ShapeDtypeStruct((3 * HB, HB)...]
    pallas_call x1 -> x2, Pallas kernels: 10.7 us -> 9.31 us  [the longest x1 6.19 us: update(): pl.pallas_call(update_kernel, grid=(rows // PB,), in_specs=[SMEM, SMEM, p...]
    slice x2, local copies, waits for them, and re-layouts: 0.77 us -> 1.87 us  [the longest x1 1.18 us: local(): pieces = jnp.concatenate([covariance[:, :HB], covariance[:, HB:PB]], axis=0)]
  transfers between devices with their start and end apart: 14 -> 14, of which waited for: 2 -> 3; matrix products, arithmetic and copies ran while one was open for 11% -> 10% of each run, Pallas kernels for 16% -> 20%
where the time goes in v3:
time: 89.1 us; the launch traced here: 88.4 us
  waiting for transfers between devices  28.4 us (32%)
  Pallas kernels  23.5 us (26%)
  starting transfers between devices  21.6 us (24%)
  other arithmetic  8.53 us (10%)
  local copies, waits for them, and re-layouts  5.27 us (6%)
  between operations  1 us (1%)
    all_to_all x2, waiting for transfers between devices, local(): lax.all_to_all(x, BOTH, 0, 0, axis_index_groups=groups, tiled=True)  15.1 us
    pallas_call x1, Pallas kernels, inverse_of_factor(): pl.pallas_call(factor_kernel, out_shape=jax.ShapeDtypeStruct((3 * HB, HB)...  14.2 us
    all_to_all x2, starting transfers between devices, local(): lax.all_to_all(x, BOTH, 0, 0, axis_index_groups=groups, tiled=True)  11.1 us
    ppermute x10, waiting for transfers between devices, spread(): parts = [lax.ppermute(value, BOTH, perm) for perm in perms]  7.62 us
    ppermute x10, starting transfers between devices, spread(): parts = [lax.ppermute(value, BOTH, perm) for perm in perms]  7.39 us
    pallas_call x1, Pallas kernels, update(): pl.pallas_call(update_kernel, grid=(rows // PB,), in_specs=[SMEM, SMEM, p...  6.19 us
    ppermute x1, waiting for transfers between devices, local(): second = lax.ppermute(targets[:PB, HB:], 'row', [(0, 1)])  5.71 us
    pallas_call x1, Pallas kernels, solve(): pl.pallas_call(solve_kernel, in_specs=[SMEM, SMEM, VMEM, VMEM, VMEM, anyw...  3.12 us
  transfers between devices with their start and end apart: 14, of which 3 were waited for; matrix products, arithmetic and copies ran while one was open for 10% of the time, Pallas kernels for 20%

profile of v3, /device:TPU:1, one launch (start us, length us, event | category | flops | bytes accessed | tf_op | source)
XLA Modules:
  0.0 88.4 jit_solution(6449158329096400149)
XLA Ops:
  0.6 0.7 slice.48
  1.3 0.7 select_reduce_fusion
  2.1 1.0 %add_select_fusion = f32[256,256]{1,0:T(8,128)S(1)} fusion(f32[768,1536]{1,0:T(8,128)} %a_ref.1, f32[256]{0:T(256)S(1)} %select_reduce_fusion, pred[]{:T(512)S(6)} %eq.33), kind=kLoop, calls=%fused_computation.11 | loop fusion | flops 262144 | bytes 525313 | tf_op jit(solution)/shard_map/jit(_where)/select_n | solution.py:293
  3.1 0.7 collective-permute-start.2
  3.8 0.7 collective-permute-start.3
  4.5 0.7 collective-permute-start.1
  5.2 0.9 %slice.45 = f32[256,128]{1,0:T(8,128)S(1)} slice(f32[768,256]{1,0:T(8,128)} %t_ref.1), slice={[0:256], [128:256]} | slice | bytes 262144 | tf_op jit(solution)/shard_map/slice | solution.py:336
  6.1 1.3 %collective-permute-start = (f32[256,128]{1,0:T(8,128)S(1)}, f32[256,128]{1,0:T(8,128)S(1)}, u32[]{:S(2)}, u32[]{:S(2)}) collective-permute-start(f32[256,128]{1,0:T(8,128)S(1)} %slice.45), channel_id=1, source_target_pairs={{0,1},{16,17},{32,33},{48,49},{64,65},{80,81},{96,97},{112,113}} | collective-permute-start | bytes 393224 | tf_op jit(solution)/shard_map/ppermute | solution.py:336
  7.4 1.2 %fusion.3 = (f32[768,128]{1,0:T(8,128)S(1)}, f32[768,128]{1,0:T(8,128)S(1)}) fusion(f32[768,1536]{1,0:T(8,128)} %a_ref.1), kind=kLoop, calls=%fused_computation.26 | loop fusion | bytes 1572864 | tf_op jit(solution)/shard_map/slice | solution.py:339
  8.6 0.1 pad_maximum_fusion.1
  8.6 5.7 %collective-permute-done = f32[256,128]{1,0:T(8,128)S(1)} collective-permute-done((f32[256,128]{1,0:T(8,128)S(1)}, f32[256,128]{1,0:T(8,128)S(1)}, u32[]{:S(2)}, u32[]{:S(2)}) %collective-permute-start) | collective-permute-done | bytes 131104 | tf_op jit(solution)/shard_map/ppermute | solution.py:336
  14.3 0.9 %slice_select_fusion = f32[256,128]{1,0:T(8,128)S(1)} fusion(f32[256,128]{1,0:T(8,128)S(1)} %collective-permute-done, f32[768,256]{1,0:T(8,128)} %t_ref.1, pred[]{:T(512)S(6)} %eq.32), kind=kLoop, calls=%fused_computation.14 | loop fusion | flops 32768 | bytes 393217 | tf_op jit(solution)/shard_map/jit(_where)/select_n | solution.py:337
  15.3 1.1 %select_maximum_fusion = f32[64,32,128]{2,1,0:T(8,128)} fusion(f32[64,4,128]{2,1,0:T(4,128)S(1)} %bitcast.22, f32[64,24,128]{2,1,0:T(8,128)S(1)} %bitcast.20), kind=kLoop, calls=%fused_computation.5 | loop fusion | flops 786432 | bytes 1966080 | tf_op jit(solution)/shard_map/concatenate | solution.py:340
  16.4 0.0 collective-permute-done.2
  16.4 0.0 collective-permute-done.3
  16.4 1.1 %add_add_fusion.2 = f32[256,256]{1,0:T(8,128)S(1)} fusion(f32[256,256]{1,0:T(8,128)S(1)} %collective-permute-done.3, f32[256,256]{1,0:T(8,128)S(1)} %collective-permute-done.2, f32[256,256]{1,0:T(8,128)S(1)} %collective-permute-done.1, f32[256]{0:T(256)S(1)} %select_reduce_fusion, f32[768,1536]{1,0:T(8,128)} %a_ref.1, pred[]{:T(512)S(6)} %eq.33), kind=kLoop, calls=%fused_computation.10 | loop fusion | flops 458752 | bytes 1311745 | tf_op jit(solution)/shard_map/add | solution.py:311
  17.4 0.7 collective-permute-start.6
  18.1 0.7 collective-permute-start.5
  18.8 0.7 collective-permute-start.4
  19.5 5.7 %all-to-all-start = ((f32[64,32,128]{2,1,0:T(8,128)}), f32[64,32,128]{2,1,0:T(8,128)S(1)}, u32[]{:S(2)}, u32[]{:S(2)}) async-start(f32[64,32,128]{2,1,0:T(8,128)} %select_maximum_fusion), calls=%async_computation | async-start | bytes 2097152 | tf_op jit(solution)/shard_map/all_to_all | solution.py:332
  25.2 0.1 add_add_fusion.1
  25.3 0.7 collective-permute-start.9
  25.9 0.7 collective-permute-start.8
  26.6 0.7 collective-permute-start.7
  27.3 0.1 add_add_fusion
  27.4 15.1 %all-to-all-done = f32[64,32,128]{2,1,0:T(8,128)S(1)} async-done(((f32[64,32,128]{2,1,0:T(8,128)}), f32[64,32,128]{2,1,0:T(8,128)S(1)}, u32[]{:S(2)}, u32[]{:S(2)}) %all-to-all-start) | async-done | bytes 1048608 | tf_op jit(solution)/shard_map/all_to_all | solution.py:332
  42.6 0.0 copy-start.3
  42.6 0.0 copy-start.1
  42.6 0.0 copy-start.4
  42.6 0.1 broadcast_in_dim.85
  42.7 0.1 broadcast_in_dim.84
  42.8 1.4 %pad_maximum_fusion = f32[8,8,56,128]{3,2,1,0:T(8,128)} fusion(f32[8,8,4,128]{3,2,1,0:T(4,128)S(1)} %broadcast_in_dim.88, f32[8,8,4,128]{3,2,1,0:T(4,128)S(1)} %broadcast_in_dim.87, f32[8,8,24,128]{3,2,1,0:T(8,128)S(1)} %broadcast_in_dim.85, f32[8,8,24,128]{3,2,1,0:T(8,128)S(1)} %broadcast_in_dim.84), kind=kLoop, calls=%fused_computation.4 | loop fusion | flops 1376256 | bytes 3670016 | tf_op jit(solution)/shard_map/concatenate | solution.py:363
  44.2 5.5 %all-to-all-start.1 = ((f32[64,56,128]{2,1,0:T(8,128)}), f32[64,56,128]{2,1,0:T(8,128)S(1)}, u32[]{:S(2)}, u32[]{:S(2)}) async-start(f32[64,56,128]{2,1,0:T(8,128)} %bitcast.19), calls=%async_computation.1 | async-start | bytes 3670016 | tf_op jit(solution)/shard_map/all_to_all | solution.py:332
  49.7 0.6 dynamic_slice.12
  50.3 0.7 dynamic-slice_minimum_fusion
  51.0 0.7 constant_dynamic-slice_fusion.1
  51.7 0.8 constant_dynamic-slice_fusion
  52.5 0.1 broadcast_bitcast_fusion
  52.6 1.3 %collective-permute-start.10 = (f32[256,256]{1,0:T(8,128)S(1)}, f32[256,256]{1,0:T(8,128)S(1)}, u32[]{:S(2)}, u32[]{:S(2)}) collective-permute-start(f32[256,256]{1,0:T(8,128)S(1)} %add_add_fusion), channel_id=1, source_target_pairs={{0,1},{2,3},{16,17},{18,19},{4,5},{6,7},{20,21},{22,23},{8,9},{10,... | collective-permute-start | bytes 786440 | tf_op jit(solution)/shard_map/ppermute | solution.py:310
  53.9 0.1 pad_add_fusion.place_ref
  54.0 0.1 multiply_add_fusion
  54.1 7.6 %collective-permute-done.10 = f32[256,256]{1,0:T(8,128)S(1)} collective-permute-done((f32[256,256]{1,0:T(8,128)S(1)}, f32[256,256]{1,0:T(8,128)S(1)}, u32[]{:S(2)}, u32[]{:S(2)}) %collective-permute-start.10) | collective-permute-done | bytes 262176 | tf_op jit(solution)/shard_map/ppermute | solution.py:310
  61.7 14.2 %inverse_factor.1.inv_ref = f32[384,128]{1,0:T(8,128)S(1)} custom-call(f32[256,256]{1,0:T(8,128)S(1)} %add.74.d_ref), custom_call_target="tpu_custom_call" | custom-call | flops 200000000 | bytes 80000000 | tf_op jit(solution)/shard_map/inverse_factor/pallas_call | solution.py:104
  75.9 0.1 slice.51
  76.1 1.8 %collective-permute-start.11 = (f32[64,32,128]{2,1,0:T(8,128)S(1)}, f32[64,32,128]{2,1,0:T(8,128)S(1)}, u32[]{:S(2)}, u32[]{:S(2)}) collective-permute-start(f32[64,32,128]{2,1,0:T(8,128)S(1)} %slice.51), channel_id=1, source_target_pairs={{0,1},{1,0},{2,3},{3,2},{4,5},{5,4},{6,7},{7,6},{8,9},{9,8},{10,11... | collective-permute-start | bytes 3145736 | tf_op jit(solution)/shard_map/ppermute | solution.py:369
  77.9 1.1 %fusion.2.ctt_ref = f32[128,256]{1,0:T(8,128)S(1)} fusion(f32[35]{0:T(128)S(1)} %mul.19, f32[128,256]{1,0:T(8,128)S(1)} %multiply_add_fusion, f32[35]{0:T(128)S(1)} %copy-done.2, pred[35,256]{1,0:T(8,128)(4,1)S(1)} %iota_compare_fusion.2), kind=kLoop, calls=%fused_computation.3 | loop fusion | flops 5701632 | bytes 271384 | tf_op jit(solution)/shard_map/reduce_sum | solution.py:324
  79.1 3.1 %solve.1 = (f32[768,256]{1,0:T(8,128)S(1)}, bf16[256,768]{1,0:T(8,128)(2,1)S(1)}, bf16[768,768]{1,0:T(8,128)(2,1)S(1)}, bf16[768,768]{1,0:T(8,128)(2,1)S(1)}, f3...) custom-call(s32[2]{0:T(128)S(1)} %pad_add_fusion.place_ref, f32[6]{0:T(128)S(1)} %copy-done, ...), custom_call_target="tpu_custom_call" | custom-call | flops 1000000000 | bytes 6000000 | tf_op jit(solution)/shard_map/solve/pallas_call | solution.py:173
  82.2 6.2 %update.1 = (f32[768,1536]{1,0:T(8,128)}, f32[768,256]{1,0:T(8,128)}, f32[768,256]{1,0:T(8,128)}, f32[128,256]{1,0:T(8,128)}) custom-call(s32[2]{0:T(128)S(1)} %pad_add_fusion.place_ref, f32[6]{0:T(128)S(1)} %copy-done, s32[1,768]{1,0:T(1,128)S(1)} %broadcast_in_dim.52.wfs_ref, f32[768,1536]{1,0:T(8,128)S(1)} %get-tuple-element.20.a_ref, ...), custom_call_target="tpu_custom_call" | custom-call | flops 2000000000 | bytes 7000000 | tf_op jit(solution)/shard_map/update/pallas_call | solution.py:253
  (25 shorter events, 0.1 us)
Async XLA Ops:
  3.1 13.2 %collective-permute-start.2 = (f32[256,256]{1,0:T(8,128)S(1)}, f32[256,256]{1,0:T(8,128)S(1)}, u32[]{:S(2)}, u32[]{:S(2)}) collective-permute-start(f32[256,256]{1,0:T(8,128)S(1)} %add_select_fusion), channel_id=1, source_target_pairs={{0,32}} | collective-permute-start | bytes 786440 | tf_op jit(solution)/shard_map/ppermute | solution.py:310
  3.8 12.6 %collective-permute-start.3 = (f32[256,256]{1,0:T(8,128)S(1)}, f32[256,256]{1,0:T(8,128)S(1)}, u32[]{:S(2)}, u32[]{:S(2)}) collective-permute-start(f32[256,256]{1,0:T(8,128)S(1)} %add_select_fusion), channel_id=1, source_target_pairs={{0,96}} | collective-permute-start | bytes 786440 | tf_op jit(solution)/shard_map/ppermute | solution.py:310
  4.5 11.9 %collective-permute-start.1 = (f32[256,256]{1,0:T(8,128)S(1)}, f32[256,256]{1,0:T(8,128)S(1)}, u32[]{:S(2)}, u32[]{:S(2)}) collective-permute-start(f32[256,256]{1,0:T(8,128)S(1)} %add_select_fusion), channel_id=1, source_target_pairs={{0,64}} | collective-permute-start | bytes 786440 | tf_op jit(solution)/shard_map/ppermute | solution.py:310
  6.1 8.3 %collective-permute-start = (f32[256,128]{1,0:T(8,128)S(1)}, f32[256,128]{1,0:T(8,128)S(1)}, u32[]{:S(2)}, u32[]{:S(2)}) collective-permute-start(f32[256,128]{1,0:T(8,128)S(1)} %slice.45), channel_id=1, source_target_pairs={{0,1},{16,17},{32,33},{48,49},{64,65},{80,81},{96,97},{112,113}} | collective-permute-start | bytes 393224 | tf_op jit(solution)/shard_map/ppermute | solution.py:336
  17.4 7.7 %collective-permute-start.6 = (f32[256,256]{1,0:T(8,128)S(1)}, f32[256,256]{1,0:T(8,128)S(1)}, u32[]{:S(2)}, u32[]{:S(2)}) collective-permute-start(f32[256,256]{1,0:T(8,128)S(1)} %add_add_fusion.2), channel_id=1, source_target_pairs={{0,12},{32,44},{64,76},{96,108}} | collective-permute-start | bytes 786440 | tf_op jit(solution)/shard_map/ppermute | solution.py:310
  18.1 7.0 %collective-permute-start.5 = (f32[256,256]{1,0:T(8,128)S(1)}, f32[256,256]{1,0:T(8,128)S(1)}, u32[]{:S(2)}, u32[]{:S(2)}) collective-permute-start(f32[256,256]{1,0:T(8,128)S(1)} %add_add_fusion.2), channel_id=1, source_target_pairs={{0,4},{32,36},{64,68},{96,100}} | collective-permute-start | bytes 786440 | tf_op jit(solution)/shard_map/ppermute | solution.py:310
  18.8 6.4 %collective-permute-start.4 = (f32[256,256]{1,0:T(8,128)S(1)}, f32[256,256]{1,0:T(8,128)S(1)}, u32[]{:S(2)}, u32[]{:S(2)}) collective-permute-start(f32[256,256]{1,0:T(8,128)S(1)} %add_add_fusion.2), channel_id=1, source_target_pairs={{0,8},{32,40},{64,72},{96,104}} | collective-permute-start | bytes 786440 | tf_op jit(solution)/shard_map/ppermute | solution.py:310
  19.5 23.0 %all-to-all-start = ((f32[64,32,128]{2,1,0:T(8,128)}), f32[64,32,128]{2,1,0:T(8,128)S(1)}, u32[]{:S(2)}, u32[]{:S(2)}) async-start(f32[64,32,128]{2,1,0:T(8,128)} %select_maximum_fusion), calls=%async_computation | async-start | bytes 2097152 | tf_op jit(solution)/shard_map/all_to_all | solution.py:332
  25.3 2.1 %collective-permute-start.9 = (f32[256,256]{1,0:T(8,128)S(1)}, f32[256,256]{1,0:T(8,128)S(1)}, u32[]{:S(2)}, u32[]{:S(2)}) collective-permute-start(f32[256,256]{1,0:T(8,128)S(1)} %add_add_fusion.1), channel_id=1, source_target_pairs={{0,16},{4,20},{8,24},{12,28},{32,48},{36,52},{40,56},{44,60},{64,8... | collective-permute-start | bytes 786440 | tf_op jit(solution)/shard_map/ppermute | solution.py:310
  25.9 1.4 %collective-permute-start.8 = (f32[256,256]{1,0:T(8,128)S(1)}, f32[256,256]{1,0:T(8,128)S(1)}, u32[]{:S(2)}, u32[]{:S(2)}) collective-permute-start(f32[256,256]{1,0:T(8,128)S(1)} %add_add_fusion.1), channel_id=1, source_target_pairs={{0,18},{4,22},{8,26},{12,30},{32,50},{36,54},{40,58},{44,62},{64,8... | collective-permute-start | bytes 786440 | tf_op jit(solution)/shard_map/ppermute | solution.py:310
  26.6 0.7 collective-permute-start.7
  42.6 7.0 %copy-start.3 = (s32[16]{0:T(128)S(1)}, s32[16]{0:T(128)}, u32[]{:S(2)}) copy-start(s32[16]{0:T(128)} %param.15) | copy-start | bytes 196
  42.6 11.3 %copy-start.1 = (s32[768]{0:T(1024)S(1)}, s32[768]{0:T(1024)}, u32[]{:S(2)}) copy-start(s32[768]{0:T(1024)} %param.9) | copy-start | bytes 9220
  42.6 11.3 %copy-start.4 = (f32[35]{0:T(128)S(1)}, f32[35]{0:T(128)}, u32[]{:S(2)}) copy-start(f32[35]{0:T(128)} %param.14) | copy-start | bytes 424
  44.2 33.7 %copy-start.2 = (f32[35]{0:T(128)S(1)}, f32[35]{0:T(128)}, u32[]{:S(2)}) copy-start(f32[35]{0:T(128)} %param.13) | copy-start | bytes 424
  44.2 34.9 %copy-start = (f32[6]{0:T(128)S(1)}, f32[6]{0:T(128)}, u32[]{:S(2)}) copy-start(f32[6]{0:T(128)} %noise_ref.3) | copy-start | bytes 76
  44.2 31.8 %all-to-all-start.1 = ((f32[64,56,128]{2,1,0:T(8,128)}), f32[64,56,128]{2,1,0:T(8,128)S(1)}, u32[]{:S(2)}, u32[]{:S(2)}) async-start(f32[64,56,128]{2,1,0:T(8,128)} %bitcast.19), calls=%async_computation.1 | async-start | bytes 3670016 | tf_op jit(solution)/shard_map/all_to_all | solution.py:332
  52.6 9.1 %collective-permute-start.10 = (f32[256,256]{1,0:T(8,128)S(1)}, f32[256,256]{1,0:T(8,128)S(1)}, u32[]{:S(2)}, u32[]{:S(2)}) collective-permute-start(f32[256,256]{1,0:T(8,128)S(1)} %add_add_fusion), channel_id=1, source_target_pairs={{0,1},{2,3},{16,17},{18,19},{4,5},{6,7},{20,21},{22,23},{8,9},{10,... | collective-permute-start | bytes 786440 | tf_op jit(solution)/shard_map/ppermute | solution.py:310
  76.1 6.1 %collective-permute-start.11 = (f32[64,32,128]{2,1,0:T(8,128)S(1)}, f32[64,32,128]{2,1,0:T(8,128)S(1)}, u32[]{:S(2)}, u32[]{:S(2)}) collective-permute-start(f32[64,32,128]{2,1,0:T(8,128)S(1)} %slice.51), channel_id=1, source_target_pairs={{0,1},{1,0},{2,3},{3,2},{4,5},{5,4},{6,7},{7,6},{8,9},{9,8},{10,11... | collective-permute-start | bytes 3145736 | tf_op jit(solution)/shard_map/ppermute | solution.py:369

commit v4 on v3

--- a/solution.py
+++ b/solution.py
@@ -88,11 +88,11 @@
 
 
 def factor_kernel(d_ref, out_ref, a_ref, w1_ref, w2_ref):
-    a_ref[...] = d_ref[:HB, :HB]
+    a_ref[...] = d_ref[:HB, :]
     inverse_factor(a_ref, w1_ref)
     first = w1_ref[...]
-    low = mm(d_ref[HB:, :HB], first, ((1,), (1,)))
-    a_ref[...] = d_ref[HB:, HB:] - mm(low, low, ((1,), (1,)))
+    low = mm(d_ref[HB:PB, :], first, ((1,), (1,)))
+    a_ref[...] = d_ref[PB:, :] - mm(low, low, ((1,), (1,)))
     inverse_factor(a_ref, w2_ref)
     second = w2_ref[...]
     out_ref[:HB, :] = first
@@ -188,7 +188,7 @@
             flops=1_000_000_000, transcendentals=0, bytes_accessed=6_000_000
         ),
         name="solve",
-    )(place, noise_var, wfs[None, :], own, inv, far(covariance), far(targets))
+    )(place, noise_var, wfs, own, inv, far(covariance), far(targets))
 
 
 def update_kernel(
@@ -278,20 +278,67 @@
         ),
         name="update",
     )(
-        place, noise_var, wfs[None, :], near(matrix), near(targets), near(own), near(other),
+        place, noise_var, wfs, near(matrix), near(targets), near(own), near(other),
         *[near(x) for x in solved], near(ctt),
     )
+
+
+def pieces_kernel(a_ref, t_ref, second_ref, out_ref):
+    half = jnp.where(lax.axis_index("row") == 1, second_ref[...], t_ref[...])
+    count = out_ref.shape[0] // 2
+    out_ref[:count, :24, :] = a_ref[:, :HB].reshape(count, 24, HB)
+    out_ref[count:, :24, :] = a_ref[:, HB:].reshape(count, 24, HB)
+    half = half.reshape(2 * count, 4, HB)
+    out_ref[:, 24:, :] = jnp.concatenate([half, jnp.zeros_like(half)], axis=1)
+
+
+def pieces_of(covariance, targets, second):
+    far = lambda x: pltpu.with_memory_space_constraint(x, pltpu.HBM)
+    rows = covariance.shape[0]
+    first = lambda *shape: pl.BlockSpec(shape, lambda i: (0,) * len(shape))
+    return pl.pallas_call(
+        pieces_kernel,
+        grid=(1,),
+        in_specs=[first(rows, PB), first(PB, HB), first(PB, HB)],
+        out_specs=first(64, 32, HB),
+        out_shape=jax.ShapeDtypeStruct((64, 32, HB), F32),
+        compiler_params=pltpu.CompilerParams(vmem_limit_bytes=8 << 20),
+        cost_estimate=pl.CostEstimate(flops=0, transcendentals=0, bytes_accessed=2_000_000),
+        name="pieces",
+    )(far(covariance), far(targets), second)
+
+
+def lead_kernel(a_ref, noise_ref, out_ref):
+    sub = lax.broadcasted_iota(jnp.int32, (HB, HB), 0)
+    eye = sub == lax.broadcasted_iota(jnp.int32, (HB, HB), 1)
+    here = (lax.axis_index("row") == 0) & (lax.axis_index("col") == 0)
+    keep = lambda x: jnp.where(here, x, 0.0)
+    out_ref[:HB] = keep(a_ref[:HB, :HB] + jnp.where(eye, noise_ref[:, :HB], 0.0))
+    out_ref[HB:PB] = keep(a_ref[HB:, :HB])
+    out_ref[PB:] = keep(a_ref[HB:, HB:] + jnp.where(eye, noise_ref[:, HB:], 0.0))
+
+
+def lead_of(covariance, noise):
+    first = lambda *shape: pl.BlockSpec(shape, lambda i: (0, 0))
+    return pl.pallas_call(
+        lead_kernel,
+        grid=(1,),
+        in_specs=[first(PB, PB), first(1, PB)],
+        out_specs=first(3 * HB, HB),
+        out_shape=jax.ShapeDtypeStruct((3 * HB, HB), F32),
+        compiler_params=pltpu.CompilerParams(vmem_limit_bytes=4 << 20),
+        cost_estimate=pl.CostEstimate(flops=0, transcendentals=0, bytes_accessed=500_000),
+        name="lead",
+    )(pltpu.with_memory_space_constraint(covariance, pltpu.HBM), noise)
 
 
 def device(x, z_lo, y, z_hi, core):
     return (x * 2 + z_lo) * 16 + y * 4 + z_hi * 2 + core
 
 
-def spread(value, first):
+def rounds_of():
     four, two = range(4), range(2)
-    index = lax.axis_index("col") * 16 + lax.axis_index("row")
-    value = jnp.where(index == 0, value, 0.0)
-    rounds = (
+    return (
         [[(device(0, 0, 0, 0, 0), device(k, 0, 0, 0, 0))] for k in (2, 1, 3)],
         [[(device(x, 0, 0, 0, 0), device(x, 0, k, 0, 0)) for x in four] for k in (2, 1, 3)],
         [
@@ -305,14 +352,10 @@
             ]
         ],
     )
-    waves = []
-    for perms in rounds:
-        parts = [lax.ppermute(value, BOTH, perm) for perm in perms]
-        value = sum(parts, value)
-        if not waves:
-            value, _ = lax.optimization_barrier((value, first))
-        waves.append(value)
-    return waves
+
+
+def wave(value, perms):
+    return sum([lax.ppermute(value, BOTH, perm) for perm in perms], value)
 
 
 def target_covariance(pos_rows, pos_cols, low, strength, scale):
@@ -334,26 +377,33 @@
     )
 
     second = lax.ppermute(targets[:PB, HB:], "row", [(0, 1)])
-    half = jnp.where(row == 1, second, targets[:PB, :HB])
-    half = jnp.pad(half.reshape(64, 4, HB), ((0, 0), (0, 4), (0, 0)))
-    pieces = jnp.concatenate([covariance[:, :HB], covariance[:, HB:PB]], axis=0)
-    pieces = jnp.concatenate([pieces.reshape(64, 24, HB), half], axis=1)
-
+    pieces = pieces_of(covariance, targets, second)
+
+    kinds = jnp.arange(noise_var.shape[0], dtype=jnp.int32)[:, None]
     noise = jnp.sum(
-        jnp.where(
-            wfs_map[:PB, None] == jnp.arange(noise_var.shape[0], dtype=jnp.int32)[None, :],
-            noise_var[None, :],
-            0.0,
-        ),
-        axis=1,
-    )
-    ids = jnp.arange(PB, dtype=jnp.int32)
-    waves = spread(
-        covariance[:PB, :PB] + jnp.where(ids[:, None] == ids[None, :], noise[:, None], 0.0),
-        pieces,
+        jnp.where(wfs_map[None, :PB] == kinds, noise_var[:, None], 0.0), axis=0, keepdims=True
+    )
+    lead = lead_of(covariance, noise)
+    along_x, along_y, along_z, to_core = rounds_of()
+    lead, _ = lax.optimization_barrier((wave(lead, along_x), pieces))
+    lead = wave(lead, along_y)
+
+    position, levels, _ = lax.optimization_barrier((target_pos, tile_layer, lead))
+    start = row * TILE
+    pos_rows = lax.dynamic_slice_in_dim(position, start, TILE, 1)
+    pos_cols = lax.dynamic_slice_in_dim(position, col * target_width, target_width, 1)
+    level_cols = lax.dynamic_slice_in_dim(levels, col * (target_width // TILE), target_width // TILE, 0)
+    level_row = lax.dynamic_slice_in_dim(levels, row, 1, 0)
+    low = jnp.repeat(jnp.minimum(level_row, level_cols), TILE)
+    ctt = target_covariance(pos_rows, pos_cols, low, strength, scale)
+
+    place = jnp.stack([row, col]).astype(jnp.int32)
+    wfs_row, place, _ = lax.optimization_barrier((wfs_map, place, lead))
+    wfs_row = wfs_row[None, :]
+    lead, ctt, wfs_row, place = lax.optimization_barrier(
+        (wave(lead, along_z), ctt, wfs_row, place)
     )
     held = exchange(pieces)
-    held, _ = lax.optimization_barrier((held, waves[2]))
     held_panel = held[:8, :24]
     held_head = held.reshape(8, 8, 32, HB)[:, 0, 24:28]
 
@@ -363,25 +413,17 @@
     wanted = jnp.concatenate(
         [over_m(held_panel), over_c(held_panel), over_m(held_head), over_c(held_head)], axis=2
     ).reshape(64, 56, HB)
-    lead, _ = lax.optimization_barrier((waves[-1], wanted))
+    wanted, _ = lax.optimization_barrier((wanted, lead))
+    lead, _ = lax.optimization_barrier((wave(lead, to_core), wanted))
     inv = inverse_of_factor(lead)
     own, inv = lax.optimization_barrier((exchange(wanted), inv))
     other = lax.ppermute(own[:, 24:], "row", [(i, i ^ 1) for i in range(16)])
 
-    start = row * TILE
-    pos_rows = lax.dynamic_slice_in_dim(target_pos, start, TILE, 1)
-    pos_cols = lax.dynamic_slice_in_dim(target_pos, col * target_width, target_width, 1)
-    level_cols = lax.dynamic_slice_in_dim(tile_layer, col * (target_width // TILE), target_width // TILE, 0)
-    level_row = lax.dynamic_slice_in_dim(tile_layer, row, 1, 0)
-    low = jnp.repeat(jnp.minimum(level_row, level_cols), TILE)
-    ctt = target_covariance(pos_rows, pos_cols, low, strength, scale)
-
-    place = jnp.stack([row, col]).astype(jnp.int32)
     *solved, matrix, near_targets = solve(
-        place, noise_var, wfs_map, own, inv, covariance, targets
+        place, noise_var, wfs_row, own, inv, covariance, targets
     )
     return update(
-        place, noise_var, wfs_map, matrix, near_targets, own, other, solved, ctt
+        place, noise_var, wfs_row, matrix, near_targets, own, other, solved, ctt
     )
 
 

time: 89.1 us -> 85.6 us (0.961)
  other arithmetic: 8.53 us -> 4.33 us
  waiting for transfers between devices: 28.4 us -> 24.6 us
  Pallas kernels: 23.5 us -> 26.7 us
  starting transfers between devices: 21.6 us -> 24.2 us
  local copies, waits for them, and re-layouts: 5.27 us -> 4.11 us
    all_to_all x2, waiting for transfers between devices: 15.1 us -> 10.1 us  [local(): lax.all_to_all(x, BOTH, 0, 0, axis_index_groups=groups, tiled=True)]
    ppermute x1, starting transfers between devices: 1.84 us -> 5.73 us  [local(): other = lax.ppermute(own[:, 24:], 'row', [(i, i ^ 1) for i in range(16)])]
    pallas_call x0 -> x2, Pallas kernels: none -> 3.18 us  [the longest x1 2.21 us: pieces_of(): pl.pallas_call(pieces_kernel, grid=(1,), in_specs=[first(rows, PB), first...]
    select_n x2 -> x0, other arithmetic: 1.97 us -> none  [the longest x1 1.05 us: spread(): value = jnp.where(index == 0, value, 0.0)]
    ppermute x1, waiting for transfers between devices: 5.71 us -> 7.58 us  [local(): second = lax.ppermute(targets[:PB, HB:], 'row', [(0, 1)])]
    all_to_all x2, starting transfers between devices: 11.1 us -> 9.71 us  [local(): lax.all_to_all(x, BOTH, 0, 0, axis_index_groups=groups, tiled=True)]
    slice x2 -> x1, local copies, waits for them, and re-layouts: 1.87 us -> 0.69 us  [local(): wfs_map[None, :PB] == kinds]
    concatenate x2 -> x0, other arithmetic: 1.14 us -> none  [the longest x1 1.09 us: local(): pieces = jnp.concatenate([pieces.reshape(64, 24, HB), half], axis=1)]
  transfers between devices with their start and end apart: 14 -> 14, of which waited for: 3 -> 3; matrix products, arithmetic and copies ran while one was open for 10% -> 6% of each run, Pallas kernels for 20% -> 23%
where the time goes in v4:
time: 85.6 us; the launch traced here: 84.9 us
  Pallas kernels  26.7 us (31%)
  waiting for transfers between devices  24.6 us (29%)
  starting transfers between devices  24.2 us (28%)
  other arithmetic  4.33 us (5%)
  local copies, waits for them, and re-layouts  4.11 us (5%)
  between operations  1 us (1%)
    pallas_call x1, Pallas kernels, inverse_of_factor(): pl.pallas_call(factor_kernel, out_shape=jax.ShapeDtypeStruct((3 * HB, HB)...  14.2 us
    all_to_all x2, waiting for transfers between devices, local(): lax.all_to_all(x, BOTH, 0, 0, axis_index_groups=groups, tiled=True)  10.1 us
    all_to_all x2, starting transfers between devices, local(): lax.all_to_all(x, BOTH, 0, 0, axis_index_groups=groups, tiled=True)  9.71 us
    ppermute x1, waiting for transfers between devices, local(): second = lax.ppermute(targets[:PB, HB:], 'row', [(0, 1)])  7.58 us
    ppermute x10, starting transfers between devices, wave(): return sum([lax.ppermute(value, BOTH, perm) for perm in perms], value)  7.35 us
    ppermute x10, waiting for transfers between devices, wave(): return sum([lax.ppermute(value, BOTH, perm) for perm in perms], value)  6.86 us
    pallas_call x1, Pallas kernels, update(): pl.pallas_call(update_kernel, grid=(rows // PB,), in_specs=[SMEM, SMEM, p...  6.19 us
    ppermute x1, starting transfers between devices, local(): other = lax.ppermute(own[:, 24:], 'row', [(i, i ^ 1) for i in range(16)])  5.73 us
  transfers between devices with their start and end apart: 14, of which 3 were waited for; matrix products, arithmetic and copies ran while one was open for 6% of the time, Pallas kernels for 23%

profile of v4, /device:TPU:1, one launch (start us, length us, event | category | flops | bytes accessed | tf_op | source)
XLA Modules:
  0.0 84.9 jit_solution(2107548862695631739)
XLA Ops:
  0.6 0.7 slice.31
  1.3 0.7 select_reduce_fusion
  2.1 1.0 %lead.1 = f32[384,128]{1,0:T(8,128)S(1)} custom-call(f32[768,1536]{1,0:T(8,128)} %a_ref.5, f32[1,256]{1,0:T(1,128)S(1)} %bitcast.16), custom_call_target="tpu_custom_call" | custom-call | bytes 500000 | tf_op jit(solution)/shard_map/lead/pallas_call | solution.py:323
  3.0 0.0 copy-start.4
  3.1 0.7 collective-permute-start.2
  3.7 0.7 collective-permute-start.1
  4.4 0.7 collective-permute-start
  5.1 0.9 %slice.32 = f32[256,128]{1,0:T(8,128)S(1)} slice(f32[768,256]{1,0:T(8,128)} %t_ref.3), slice={[0:256], [128:256]} | slice | bytes 262144 | tf_op jit(solution)/shard_map/slice | solution.py:379
  6.0 0.0 copy-start.3
  6.0 0.0 copy-start.2
  6.0 0.0 copy-start.1
  6.1 1.4 %collective-permute-start.3 = (f32[256,128]{1,0:T(8,128)S(1)}, f32[256,128]{1,0:T(8,128)S(1)}, u32[]{:S(2)}, u32[]{:S(2)}) collective-permute-start(f32[256,128]{1,0:T(8,128)S(1)} %slice.32), channel_id=1, source_target_pairs={{0,1},{16,17},{32,33},{48,49},{64,65},{80,81},{96,97},{112,113}} | collective-permute-start | bytes 393224 | tf_op jit(solution)/shard_map/ppermute | solution.py:379
  7.5 7.6 %collective-permute-done.3.second_ref = f32[256,128]{1,0:T(8,128)S(1)} collective-permute-done((f32[256,128]{1,0:T(8,128)S(1)}, f32[256,128]{1,0:T(8,128)S(1)}, u32[]{:S(2)}, u32[]{:S(2)}) %collective-permute-start.3) | collective-permute-done | bytes 131104 | tf_op jit(solution)/shard_map/ppermute | solution.py:379
  15.1 2.2 %pieces.1 = f32[64,32,128]{2,1,0:T(8,128)} custom-call(f32[768,1536]{1,0:T(8,128)} %a_ref.5, f32[768,256]{1,0:T(8,128)} %t_ref.3, f32[256,128]{1,0:T(8,128)S(1)} %collective-permute-done.3.second_ref), custom_call_target="tpu_custom_call" | custom-call | bytes 2000000 | tf_op jit(solution)/shard_map/pieces/pallas_call | solution.py:299
  17.3 0.0 collective-permute-done.2
  17.3 0.0 collective-permute-done.1
  17.3 0.7 collective-permute-start.6
  18.0 0.7 collective-permute-start.5
  18.7 0.7 collective-permute-start.4
  19.4 0.1 pad_add_fusion.place_ref
  19.5 4.7 %all-to-all-start = ((f32[64,32,128]{2,1,0:T(8,128)}), f32[64,32,128]{2,1,0:T(8,128)S(1)}, u32[]{:S(2)}, u32[]{:S(2)}) async-start(f32[64,32,128]{2,1,0:T(8,128)} %pieces.1), calls=%async_computation | async-start | bytes 2097152 | tf_op jit(solution)/shard_map/all_to_all | solution.py:375
  24.1 0.0 collective-permute-done.6
  24.2 0.0 collective-permute-done.5
  24.2 0.7 collective-permute-start.9
  24.9 0.7 collective-permute-start.8
  25.6 0.7 collective-permute-start.7
  26.3 0.6 dynamic_slice.12
  26.9 0.7 dynamic-slice_minimum_fusion
  27.6 0.1 broadcast_bitcast_fusion
  27.7 0.7 constant_dynamic-slice_fusion.1
  28.4 0.8 constant_dynamic-slice_fusion
  29.2 0.1 multiply_add_fusion
  29.3 1.1 %fusion.2.ctt_ref = f32[128,256]{1,0:T(8,128)S(1)} fusion(f32[35]{0:T(128)S(1)} %mul.15, f32[128,256]{1,0:T(8,128)S(1)} %multiply_add_fusion, f32[35]{0:T(128)S(1)} %copy-done.2, pred[35,256]{1,0:T(8,128)(4,1)S(1)} %iota_compare_fusion), kind=kLoop, calls=%fused_computation.3 | loop fusion | flops 5701632 | bytes 271384 | tf_op jit(solution)/shard_map/reduce_sum | solution.py:367
  30.5 0.0 collective-permute-done.9
  30.5 0.0 collective-permute-done.8
  30.6 10.1 %all-to-all-done = f32[64,32,128]{2,1,0:T(8,128)S(1)} async-done(((f32[64,32,128]{2,1,0:T(8,128)}), f32[64,32,128]{2,1,0:T(8,128)S(1)}, u32[]{:S(2)}, u32[]{:S(2)}) %all-to-all-start) | async-done | bytes 1048608 | tf_op jit(solution)/shard_map/all_to_all | solution.py:375
  40.8 0.1 broadcast_in_dim.72
  40.8 0.1 broadcast_in_dim.71
  40.9 0.0 copy-start
  40.9 1.4 %pad_maximum_fusion = f32[8,8,56,128]{3,2,1,0:T(8,128)} fusion(f32[8,8,4,128]{3,2,1,0:T(4,128)S(1)} %broadcast_in_dim.75, f32[8,8,4,128]{3,2,1,0:T(4,128)S(1)} %broadcast_in_dim.74, f32[8,8,24,128]{3,2,1,0:T(8,128)S(1)} %broadcast_in_dim.72, f32[8,8,24,128]{3,2,1,0:T(8,128)S(1)} %broadcast_in_dim.71), kind=kLoop, calls=%fused_computation.4 | loop fusion | flops 1376256 | bytes 3670016 | tf_op jit(solution)/shard_map/concatenate | solution.py:413
  42.3 5.1 %all-to-all-start.1 = ((f32[64,56,128]{2,1,0:T(8,128)}), f32[64,56,128]{2,1,0:T(8,128)S(1)}, u32[]{:S(2)}, u32[]{:S(2)}) async-start(f32[64,56,128]{2,1,0:T(8,128)} %bitcast.17), calls=%async_computation.1 | async-start | bytes 3670016 | tf_op jit(solution)/shard_map/all_to_all | solution.py:375
  47.3 1.3 %collective-permute-start.10 = (f32[384,128]{1,0:T(8,128)S(1)}, f32[384,128]{1,0:T(8,128)S(1)}, u32[]{:S(2)}, u32[]{:S(2)}) collective-permute-start(f32[384,128]{1,0:T(8,128)S(1)} %add_add_fusion), channel_id=1, source_target_pairs={{0,1},{2,3},{16,17},{18,19},{4,5},{6,7},{20,21},{22,23},{8,9},{10,... | collective-permute-start | bytes 589832 | tf_op jit(solution)/shard_map/ppermute | solution.py:358
  48.6 6.8 %collective-permute-done.10 = f32[384,128]{1,0:T(8,128)S(1)} collective-permute-done((f32[384,128]{1,0:T(8,128)S(1)}, f32[384,128]{1,0:T(8,128)S(1)}, u32[]{:S(2)}, u32[]{:S(2)}) %collective-permute-start.10) | collective-permute-done | bytes 196640 | tf_op jit(solution)/shard_map/ppermute | solution.py:358
  55.5 14.2 %inverse_factor.1.inv_ref = f32[384,128]{1,0:T(8,128)S(1)} custom-call(f32[384,128]{1,0:T(8,128)S(1)} %add.71.d_ref), custom_call_target="tpu_custom_call" | custom-call | flops 200000000 | bytes 80000000 | tf_op jit(solution)/shard_map/inverse_factor/pallas_call | solution.py:104
  69.7 0.1 slice.41
  69.9 5.7 %collective-permute-start.11 = (f32[64,32,128]{2,1,0:T(8,128)S(1)}, f32[64,32,128]{2,1,0:T(8,128)S(1)}, u32[]{:S(2)}, u32[]{:S(2)}) collective-permute-start(f32[64,32,128]{2,1,0:T(8,128)S(1)} %slice.41), channel_id=1, source_target_pairs={{0,1},{1,0},{2,3},{3,2},{4,5},{5,4},{6,7},{7,6},{8,9},{9,8},{10,11... | collective-permute-start | bytes 3145736 | tf_op jit(solution)/shard_map/ppermute | solution.py:420
  75.6 3.1 %solve.1 = (f32[768,256]{1,0:T(8,128)S(1)}, bf16[256,768]{1,0:T(8,128)(2,1)S(1)}, bf16[768,768]{1,0:T(8,128)(2,1)S(1)}, bf16[768,768]{1,0:T(8,128)(2,1)S(1)}, f3...) custom-call(s32[2]{0:T(128)S(1)} %pad_add_fusion.place_ref, f32[6]{0:T(128)S(1)} %copy-done, ...), custom_call_target="tpu_custom_call" | custom-call | flops 1000000000 | bytes 6000000 | tf_op jit(solution)/shard_map/solve/pallas_call | solution.py:173
  78.7 6.2 %update.1 = (f32[768,1536]{1,0:T(8,128)}, f32[768,256]{1,0:T(8,128)}, f32[768,256]{1,0:T(8,128)}, f32[128,256]{1,0:T(8,128)}) custom-call(s32[2]{0:T(128)S(1)} %pad_add_fusion.place_ref, f32[6]{0:T(128)S(1)} %copy-done, s32[1,768]{1,0:T(1,128)S(1)} %broadcast_in_dim.70.wfs_ref, f32[768,1536]{1,0:T(8,128)S(1)} %get-tuple-element.35.a_ref, ...), custom_call_target="tpu_custom_call" | custom-call | flops 2000000000 | bytes 7000000 | tf_op jit(solution)/shard_map/update/pallas_call | solution.py:253
  (22 shorter events, 0.3 us)
Async XLA Ops:
  3.0 16.3 %copy-start.4 = (f32[35]{0:T(128)S(1)}, f32[35]{0:T(128)}, u32[]{:S(2)}) copy-start(f32[35]{0:T(128)} %param.14) | copy-start | bytes 424
  3.1 14.2 %collective-permute-start.2 = (f32[384,128]{1,0:T(8,128)S(1)}, f32[384,128]{1,0:T(8,128)S(1)}, u32[]{:S(2)}, u32[]{:S(2)}) collective-permute-start(f32[384,128]{1,0:T(8,128)S(1)} %lead.1), channel_id=1, source_target_pairs={{0,96}} | collective-permute-start | bytes 589832 | tf_op jit(solution)/shard_map/ppermute | solution.py:358
  3.7 13.5 %collective-permute-start.1 = (f32[384,128]{1,0:T(8,128)S(1)}, f32[384,128]{1,0:T(8,128)S(1)}, u32[]{:S(2)}, u32[]{:S(2)}) collective-permute-start(f32[384,128]{1,0:T(8,128)S(1)} %lead.1), channel_id=1, source_target_pairs={{0,32}} | collective-permute-start | bytes 589832 | tf_op jit(solution)/shard_map/ppermute | solution.py:358
  4.4 12.9 %collective-permute-start = (f32[384,128]{1,0:T(8,128)S(1)}, f32[384,128]{1,0:T(8,128)S(1)}, u32[]{:S(2)}, u32[]{:S(2)}) collective-permute-start(f32[384,128]{1,0:T(8,128)S(1)} %lead.1), channel_id=1, source_target_pairs={{0,64}} | collective-permute-start | bytes 589832 | tf_op jit(solution)/shard_map/ppermute | solution.py:358
  6.0 20.3 %copy-start.3 = (s32[16]{0:T(128)S(1)}, s32[16]{0:T(128)}, u32[]{:S(2)}) copy-start(s32[16]{0:T(128)} %param.15) | copy-start | bytes 196
  6.0 23.3 %copy-start.2 = (f32[35]{0:T(128)S(1)}, f32[35]{0:T(128)}, u32[]{:S(2)}) copy-start(f32[35]{0:T(128)} %param.13) | copy-start | bytes 424
  6.0 24.4 %copy-start.1 = (s32[768]{0:T(1024)S(1)}, s32[768]{0:T(1024)}, u32[]{:S(2)}) copy-start(s32[768]{0:T(1024)} %param.9) | copy-start | bytes 9220
  6.1 9.0 %collective-permute-start.3 = (f32[256,128]{1,0:T(8,128)S(1)}, f32[256,128]{1,0:T(8,128)S(1)}, u32[]{:S(2)}, u32[]{:S(2)}) collective-permute-start(f32[256,128]{1,0:T(8,128)S(1)} %slice.32), channel_id=1, source_target_pairs={{0,1},{16,17},{32,33},{48,49},{64,65},{80,81},{96,97},{112,113}} | collective-permute-start | bytes 393224 | tf_op jit(solution)/shard_map/ppermute | solution.py:379
  17.3 6.8 %collective-permute-start.6 = (f32[384,128]{1,0:T(8,128)S(1)}, f32[384,128]{1,0:T(8,128)S(1)}, u32[]{:S(2)}, u32[]{:S(2)}) collective-permute-start(f32[384,128]{1,0:T(8,128)S(1)} %add_add_fusion.2), channel_id=1, source_target_pairs={{0,12},{32,44},{64,76},{96,108}} | collective-permute-start | bytes 589832 | tf_op jit(solution)/shard_map/ppermute | solution.py:358
  18.0 6.1 %collective-permute-start.5 = (f32[384,128]{1,0:T(8,128)S(1)}, f32[384,128]{1,0:T(8,128)S(1)}, u32[]{:S(2)}, u32[]{:S(2)}) collective-permute-start(f32[384,128]{1,0:T(8,128)S(1)} %add_add_fusion.2), channel_id=1, source_target_pairs={{0,4},{32,36},{64,68},{96,100}} | collective-permute-start | bytes 589832 | tf_op jit(solution)/shard_map/ppermute | solution.py:358
  18.7 5.5 %collective-permute-start.4 = (f32[384,128]{1,0:T(8,128)S(1)}, f32[384,128]{1,0:T(8,128)S(1)}, u32[]{:S(2)}, u32[]{:S(2)}) collective-permute-start(f32[384,128]{1,0:T(8,128)S(1)} %add_add_fusion.2), channel_id=1, source_target_pairs={{0,8},{32,40},{64,72},{96,104}} | collective-permute-start | bytes 589832 | tf_op jit(solution)/shard_map/ppermute | solution.py:358
  19.5 21.2 %all-to-all-start = ((f32[64,32,128]{2,1,0:T(8,128)}), f32[64,32,128]{2,1,0:T(8,128)S(1)}, u32[]{:S(2)}, u32[]{:S(2)}) async-start(f32[64,32,128]{2,1,0:T(8,128)} %pieces.1), calls=%async_computation | async-start | bytes 2097152 | tf_op jit(solution)/shard_map/all_to_all | solution.py:375
  24.2 6.3 %collective-permute-start.9 = (f32[384,128]{1,0:T(8,128)S(1)}, f32[384,128]{1,0:T(8,128)S(1)}, u32[]{:S(2)}, u32[]{:S(2)}) collective-permute-start(f32[384,128]{1,0:T(8,128)S(1)} %add_add_fusion.1), channel_id=1, source_target_pairs={{0,16},{4,20},{8,24},{12,28},{32,48},{36,52},{40,56},{44,60},{64,8... | collective-permute-start | bytes 589832 | tf_op jit(solution)/shard_map/ppermute | solution.py:358
  24.9 5.6 %collective-permute-start.8 = (f32[384,128]{1,0:T(8,128)S(1)}, f32[384,128]{1,0:T(8,128)S(1)}, u32[]{:S(2)}, u32[]{:S(2)}) collective-permute-start(f32[384,128]{1,0:T(8,128)S(1)} %add_add_fusion.1), channel_id=1, source_target_pairs={{0,18},{4,22},{8,26},{12,30},{32,50},{36,54},{40,58},{44,62},{64,8... | collective-permute-start | bytes 589832 | tf_op jit(solution)/shard_map/ppermute | solution.py:358
  25.6 4.9 %collective-permute-start.7 = (f32[384,128]{1,0:T(8,128)S(1)}, f32[384,128]{1,0:T(8,128)S(1)}, u32[]{:S(2)}, u32[]{:S(2)}) collective-permute-start(f32[384,128]{1,0:T(8,128)S(1)} %add_add_fusion.1), channel_id=1, source_target_pairs={{0,2},{4,6},{8,10},{12,14},{32,34},{36,38},{40,42},{44,46},{64,66}... | collective-permute-start | bytes 589832 | tf_op jit(solution)/shard_map/ppermute | solution.py:358
  40.9 34.7 %copy-start = (f32[6]{0:T(128)S(1)}, f32[6]{0:T(128)}, u32[]{:S(2)}) copy-start(f32[6]{0:T(128)} %noise_ref.3) | copy-start | bytes 76
  42.3 27.5 %all-to-all-start.1 = ((f32[64,56,128]{2,1,0:T(8,128)}), f32[64,56,128]{2,1,0:T(8,128)S(1)}, u32[]{:S(2)}, u32[]{:S(2)}) async-start(f32[64,56,128]{2,1,0:T(8,128)} %bitcast.17), calls=%async_computation.1 | async-start | bytes 3670016 | tf_op jit(solution)/shard_map/all_to_all | solution.py:375
  47.3 8.1 %collective-permute-start.10 = (f32[384,128]{1,0:T(8,128)S(1)}, f32[384,128]{1,0:T(8,128)S(1)}, u32[]{:S(2)}, u32[]{:S(2)}) collective-permute-start(f32[384,128]{1,0:T(8,128)S(1)} %add_add_fusion), channel_id=1, source_target_pairs={{0,1},{2,3},{16,17},{18,19},{4,5},{6,7},{20,21},{22,23},{8,9},{10,... | collective-permute-start | bytes 589832 | tf_op jit(solution)/shard_map/ppermute | solution.py:358
  69.9 8.9 %collective-permute-start.11 = (f32[64,32,128]{2,1,0:T(8,128)S(1)}, f32[64,32,128]{2,1,0:T(8,128)S(1)}, u32[]{:S(2)}, u32[]{:S(2)}) collective-permute-start(f32[64,32,128]{2,1,0:T(8,128)S(1)} %slice.41), channel_id=1, source_target_pairs={{0,1},{1,0},{2,3},{3,2},{4,5},{5,4},{6,7},{7,6},{8,9},{9,8},{10,11... | collective-permute-start | bytes 3145736 | tf_op jit(solution)/shard_map/ppermute | solution.py:420

commit v5 on v4

--- a/solution.py
+++ b/solution.py
@@ -13,6 +13,8 @@
 BOTH = ("col", "row")
 precise = lax.Precision.HIGHEST
 F32 = jnp.float32
+SMEM = pl.BlockSpec(memory_space=pltpu.SMEM)
+VMEM = pl.BlockSpec(memory_space=pltpu.VMEM)
 
 
 def mm(a, b, dims=((1,), (0,))):
@@ -87,7 +89,15 @@
     lax.fori_loop(0, n // 4, step, 0)
 
 
-def factor_kernel(d_ref, out_ref, a_ref, w1_ref, w2_ref):
+def factor_kernel(
+    d_ref, big_ref, t_ref, out_ref, big_out, t_out, a_ref, w1_ref, w2_ref, sems
+):
+    copies = [
+        pltpu.make_async_copy(big_ref, big_out, sems.at[0]),
+        pltpu.make_async_copy(t_ref, t_out, sems.at[1]),
+    ]
+    for copy in copies:
+        copy.start()
     a_ref[...] = d_ref[:HB, :]
     inverse_factor(a_ref, w1_ref)
     first = w1_ref[...]
@@ -98,19 +108,29 @@
     out_ref[:HB, :] = first
     out_ref[HB:PB, :] = -mm(second, mm(low, first))
     out_ref[PB:, :] = second
-
-
-def inverse_of_factor(block):
+    for copy in copies:
+        copy.wait()
+
+
+def inverse_of_factor(block, covariance, targets):
+    anywhere = pl.BlockSpec(memory_space=pl.ANY)
+    far = lambda x: pltpu.with_memory_space_constraint(x, pltpu.HBM)
     return pl.pallas_call(
         factor_kernel,
-        out_shape=jax.ShapeDtypeStruct((3 * HB, HB), F32),
-        scratch_shapes=[pltpu.VMEM((HB, HB), F32)] * 3,
+        in_specs=[VMEM, anywhere, anywhere],
+        out_specs=[VMEM] * 3,
+        out_shape=[
+            pltpu.VMEM((3 * HB, HB), F32),
+            pltpu.VMEM(covariance.shape, F32),
+            pltpu.VMEM(targets.shape, F32),
+        ],
+        scratch_shapes=[pltpu.VMEM((HB, HB), F32)] * 3 + [pltpu.SemaphoreType.DMA((2,))],
         compiler_params=pltpu.CompilerParams(vmem_limit_bytes=8 << 20),
         cost_estimate=pl.CostEstimate(
             flops=200_000_000, transcendentals=0, bytes_accessed=80_000_000
         ),
         name="inverse_factor",
-    )(block)
+    )(block, far(covariance), far(targets))
 
 
 def two_halves(ref, base):
@@ -132,15 +152,8 @@
 
 
 def solve_kernel(
-    place_ref, noise_ref, wfs_ref, own_ref, inv_ref, a_ref, t_ref,
-    pan_ref, inv3_ref, pair_ref, mine_ref, a_out, t_out, sems,
+    place_ref, noise_ref, wfs_ref, own_ref, inv_ref, pan_ref, inv3_ref, pair_ref, mine_ref
 ):
-    copies = [
-        pltpu.make_async_copy(a_ref, a_out, sems.at[0]),
-        pltpu.make_async_copy(t_ref, t_out, sems.at[1]),
-    ]
-    for copy in copies:
-        copy.start()
     inv = jnp.concatenate(
         [
             jnp.concatenate([inv_ref[:HB, :], jnp.zeros((HB, HB), F32)], axis=1),
@@ -162,33 +175,40 @@
 
     pair_ref[...] = left(pan_ref[...])
     mine_ref[...] = right(dot3(inv3, right(two_halves(own_ref, 24)), ((1,), (1,))), axis=0)
-    for copy in copies:
-        copy.wait()
-
-
-def solve(place, noise_var, wfs, own, inv, covariance, targets):
-    rows = covariance.shape[0]
-    anywhere = pl.BlockSpec(memory_space=pl.ANY)
-    far = lambda x: pltpu.with_memory_space_constraint(x, pltpu.HBM)
+
+
+def share_kernel(own_ref, out_ref):
+    out_ref[...] = own_ref[:, 24:, :]
+
+
+def share_of(own):
+    return pl.pallas_call(
+        share_kernel,
+        in_specs=[VMEM],
+        out_specs=VMEM,
+        out_shape=pltpu.VMEM((own.shape[0], own.shape[1] - 24, HB), F32),
+        compiler_params=pltpu.CompilerParams(vmem_limit_bytes=1 << 20),
+        name="share",
+    )(own)
+
+
+def solve(place, noise_var, wfs, own, inv, rows):
     return pl.pallas_call(
         solve_kernel,
-        in_specs=[SMEM, SMEM, VMEM, VMEM, VMEM, anywhere, anywhere],
-        out_specs=[VMEM] * 6,
+        in_specs=[SMEM, SMEM, VMEM, VMEM, VMEM],
+        out_specs=[VMEM] * 4,
         out_shape=[
             pltpu.VMEM((rows, PB), F32),
             pltpu.VMEM((PB, 3 * PB), jnp.bfloat16),
             pltpu.VMEM((rows, 3 * PB), jnp.bfloat16),
             pltpu.VMEM((3 * PB, rows), jnp.bfloat16),
-            pltpu.VMEM(covariance.shape, F32),
-            pltpu.VMEM(targets.shape, F32),
-        ],
-        scratch_shapes=[pltpu.SemaphoreType.DMA((2,))],
+        ],
         compiler_params=pltpu.CompilerParams(vmem_limit_bytes=20 << 20),
         cost_estimate=pl.CostEstimate(
             flops=1_000_000_000, transcendentals=0, bytes_accessed=6_000_000
         ),
         name="solve",
-    )(place, noise_var, wfs, own, inv, far(covariance), far(targets))
+    )(place, noise_var, wfs, own, inv)
 
 
 def update_kernel(
@@ -241,10 +261,6 @@
         upd_ref[:, :PB] = panel_ref[here, :]
 
 
-SMEM = pl.BlockSpec(memory_space=pltpu.SMEM)
-VMEM = pl.BlockSpec(memory_space=pltpu.VMEM)
-
-
 def update(place, noise_var, wfs, matrix, targets, own, other, solved, ctt):
     rows, width = matrix.shape
     target_width = targets.shape[1]
@@ -308,28 +324,39 @@
     )(far(covariance), far(targets), second)
 
 
-def lead_kernel(a_ref, noise_ref, out_ref):
+def lead_kernel(a_ref, noise_ref, wfs_ref, t_ref, out_ref, half_ref):
+    noise = noise_row(noise_ref, wfs_ref[...][None, :])
     sub = lax.broadcasted_iota(jnp.int32, (HB, HB), 0)
     eye = sub == lax.broadcasted_iota(jnp.int32, (HB, HB), 1)
     here = (lax.axis_index("row") == 0) & (lax.axis_index("col") == 0)
     keep = lambda x: jnp.where(here, x, 0.0)
-    out_ref[:HB] = keep(a_ref[:HB, :HB] + jnp.where(eye, noise_ref[:, :HB], 0.0))
+    out_ref[:HB] = keep(a_ref[:HB, :HB] + jnp.where(eye, noise[:, :HB], 0.0))
     out_ref[HB:PB] = keep(a_ref[HB:, :HB])
-    out_ref[PB:] = keep(a_ref[HB:, HB:] + jnp.where(eye, noise_ref[:, HB:], 0.0))
-
-
-def lead_of(covariance, noise):
+    out_ref[PB:] = keep(a_ref[HB:, HB:] + jnp.where(eye, noise[:, HB:], 0.0))
+    half_ref[...] = t_ref[...]
+
+
+def lead_of(covariance, noise_var, wfs, targets):
+    far = lambda x: pltpu.with_memory_space_constraint(x, pltpu.HBM)
     first = lambda *shape: pl.BlockSpec(shape, lambda i: (0, 0))
     return pl.pallas_call(
         lead_kernel,
         grid=(1,),
-        in_specs=[first(PB, PB), first(1, PB)],
-        out_specs=first(3 * HB, HB),
-        out_shape=jax.ShapeDtypeStruct((3 * HB, HB), F32),
+        in_specs=[
+            first(PB, PB),
+            SMEM,
+            pl.BlockSpec((PB,), lambda i: (0,)),
+            pl.BlockSpec((PB, HB), lambda i: (0, 1)),
+        ],
+        out_specs=[first(3 * HB, HB), first(PB, HB)],
+        out_shape=[
+            jax.ShapeDtypeStruct((3 * HB, HB), F32),
+            jax.ShapeDtypeStruct((PB, HB), F32),
+        ],
         compiler_params=pltpu.CompilerParams(vmem_limit_bytes=4 << 20),
-        cost_estimate=pl.CostEstimate(flops=0, transcendentals=0, bytes_accessed=500_000),
+        cost_estimate=pl.CostEstimate(flops=0, transcendentals=0, bytes_accessed=800_000),
         name="lead",
-    )(pltpu.with_memory_space_constraint(covariance, pltpu.HBM), noise)
+    )(far(covariance), far(noise_var), far(wfs), far(targets))
 
 
 def device(x, z_lo, y, z_hi, core):
@@ -376,14 +403,10 @@
         x, BOTH, 0, 0, axis_index_groups=groups, tiled=True
     )
 
-    second = lax.ppermute(targets[:PB, HB:], "row", [(0, 1)])
+    lead, second = lead_of(covariance, noise_var, wfs_map, targets)
+    second = lax.ppermute(second, "row", [(0, 1)])
     pieces = pieces_of(covariance, targets, second)
 
-    kinds = jnp.arange(noise_var.shape[0], dtype=jnp.int32)[:, None]
-    noise = jnp.sum(
-        jnp.where(wfs_map[None, :PB] == kinds, noise_var[:, None], 0.0), axis=0, keepdims=True
-    )
-    lead = lead_of(covariance, noise)
     along_x, along_y, along_z, to_core = rounds_of()
     lead, _ = lax.optimization_barrier((wave(lead, along_x), pieces))
     lead = wave(lead, along_y)
@@ -415,13 +438,11 @@
     ).reshape(64, 56, HB)
     wanted, _ = lax.optimization_barrier((wanted, lead))
     lead, _ = lax.optimization_barrier((wave(lead, to_core), wanted))
-    inv = inverse_of_factor(lead)
+    inv, matrix, near_targets = inverse_of_factor(lead, covariance, targets)
     own, inv = lax.optimization_barrier((exchange(wanted), inv))
-    other = lax.ppermute(own[:, 24:], "row", [(i, i ^ 1) for i in range(16)])
-
-    *solved, matrix, near_targets = solve(
-        place, noise_var, wfs_row, own, inv, covariance, targets
-    )
+    other = lax.ppermute(share_of(own), "row", [(i, i ^ 1) for i in range(16)])
+
+    solved = solve(place, noise_var, wfs_row, own, inv, rows)
     return update(
         place, noise_var, wfs_row, matrix, near_targets, own, other, solved, ctt
     )

time: 85.6 us -> 83.5 us (0.975)
  Pallas kernels: 26.7 us -> 25.6 us
    unnamed x10 -> x14, local copies, waits for them, and re-layouts: 0.03 us -> 2.22 us
    all_to_all x2, starting transfers between devices: 9.71 us -> 11.8 us  [local(): lax.all_to_all(x, BOTH, 0, 0, axis_index_groups=groups, tiled=True)]
    ppermute x2, starting transfers between devices: 7.15 us -> 5.16 us  [the longest x1 3.73 us: local(): other = lax.ppermute(share_of(own), 'row', [(i, i ^ 1) for i in range(16)])]
    slice x3 -> x0, local copies, waits for them, and re-layouts: 1.73 us -> none  [the longest x1 0.92 us: local(): second = lax.ppermute(targets[:PB, HB:], 'row', [(0, 1)])]
    pallas_call x3 -> x4, Pallas kernels: 18.3 us -> 17.2 us  [the longest x1 14.3 us: inverse_of_factor(): pl.pallas_call(factor_kernel, in_specs=[VMEM, anywhere, anywhere], out_sp...]
    all_to_all x2, waiting for transfers between devices: 10.1 us -> 9.16 us  [local(): lax.all_to_all(x, BOTH, 0, 0, axis_index_groups=groups, tiled=True)]
  transfers between devices with their start and end apart: 14 -> 14, of which waited for: 3 -> 4; matrix products, arithmetic and copies ran while one was open for 6% -> 5% of each run, Pallas kernels for 23% -> 22%
where the time goes in v5:
time: 83.5 us; the launch traced here: 82.9 us
  Pallas kernels  25.6 us (31%)
  starting transfers between devices  24.3 us (29%)
  waiting for transfers between devices  23.8 us (29%)
  local copies, waits for them, and re-layouts  4.56 us (5%)
  other arithmetic  3.66 us (4%)
  between operations  0.99 us (1%)
    pallas_call x1, Pallas kernels, inverse_of_factor(): pl.pallas_call(factor_kernel, in_specs=[VMEM, anywhere, anywhere], out_sp...  14.3 us
    all_to_all x2, starting transfers between devices, local(): lax.all_to_all(x, BOTH, 0, 0, axis_index_groups=groups, tiled=True)  11.8 us
    all_to_all x2, waiting for transfers between devices, local(): lax.all_to_all(x, BOTH, 0, 0, axis_index_groups=groups, tiled=True)  9.16 us
    ppermute x1, waiting for transfers between devices, local(): second = lax.ppermute(second, 'row', [(0, 1)])  7.58 us
    ppermute x10, starting transfers between devices, wave(): return sum([lax.ppermute(value, BOTH, perm) for perm in perms], value)  7.35 us
    ppermute x10, waiting for transfers between devices, wave(): return sum([lax.ppermute(value, BOTH, perm) for perm in perms], value)  6.63 us
    pallas_call x1, Pallas kernels, update(): pl.pallas_call(update_kernel, grid=(rows // PB,), in_specs=[SMEM, SMEM, p...  6.19 us
    ppermute x1, starting transfers between devices, local(): other = lax.ppermute(share_of(own), 'row', [(i, i ^ 1) for i in range(16)])  3.73 us
  transfers between devices with their start and end apart: 14, of which 4 were waited for; matrix products, arithmetic and copies ran while one was open for 5% of the time, Pallas kernels for 22%

profile of v5, /device:TPU:1, one launch (start us, length us, event | category | flops | bytes accessed | tf_op | source)
XLA Modules:
  0.0 82.9 jit_solution(15600079945543771987)
XLA Ops:
  0.6 1.0 %lead.1 = (f32[384,128]{1,0:T(8,128)S(1)}, f32[256,128]{1,0:T(8,128)S(1)}) custom-call(f32[768,1536]{1,0:T(8,128)} %big_ref.1, f32[6]{0:T(128)} %noise_ref.5, s32[768]{0:T(1024)} %wfs_ref.1, f32[768,256]{1,0:T(8,128)} %t_ref.5), custom_call_target="tpu_custom_call" | custom-call | bytes 800000 | tf_op jit(solution)/shard_map/lead/pallas_call | solution.py:342
  1.7 0.0 copy-start.6
  1.7 0.7 collective-permute-start.2
  2.4 0.7 collective-permute-start.1
  3.1 0.7 collective-permute-start
  3.7 0.0 copy-start.5
  3.7 0.0 copy-start.4
  3.8 0.0 copy-start.3
  3.8 1.4 %collective-permute-start.3 = (f32[256,128]{1,0:T(8,128)S(1)}, f32[256,128]{1,0:T(8,128)S(1)}, u32[]{:S(2)}, u32[]{:S(2)}) collective-permute-start(f32[256,128]{1,0:T(8,128)S(1)} %get-tuple-element.27), channel_id=1, source_target_pairs={{0,1},{16,17},{32,33},{48,49},{64,65},{80,81},{96,97},{112,113}} | collective-permute-start | bytes 393224 | tf_op jit(solution)/shard_map/ppermute | solution.py:407
  5.2 7.6 %collective-permute-done.3.second_ref = f32[256,128]{1,0:T(8,128)S(1)} collective-permute-done((f32[256,128]{1,0:T(8,128)S(1)}, f32[256,128]{1,0:T(8,128)S(1)}, u32[]{:S(2)}, u32[]{:S(2)}) %collective-permute-start.3) | collective-permute-done | bytes 131104 | tf_op jit(solution)/shard_map/ppermute | solution.py:407
  12.8 2.2 %pieces.1 = f32[64,32,128]{2,1,0:T(8,128)} custom-call(f32[768,1536]{1,0:T(8,128)} %big_ref.1, f32[768,256]{1,0:T(8,128)} %t_ref.5, f32[256,128]{1,0:T(8,128)S(1)} %collective-permute-done.3.second_ref), custom_call_target="tpu_custom_call" | custom-call | bytes 2000000 | tf_op jit(solution)/shard_map/pieces/pallas_call | solution.py:315
  15.0 0.0 collective-permute-done.2
  15.0 0.0 collective-permute-done.1
  15.0 0.0 collective-permute-done
  15.1 0.7 collective-permute-start.6
  15.7 0.7 collective-permute-start.5
  16.4 0.7 collective-permute-start.4
  17.1 0.1 pad_add_fusion.place_ref
  17.2 4.7 %all-to-all-start = ((f32[64,32,128]{2,1,0:T(8,128)}), f32[64,32,128]{2,1,0:T(8,128)S(1)}, u32[]{:S(2)}, u32[]{:S(2)}) async-start(f32[64,32,128]{2,1,0:T(8,128)} %pieces.1), calls=%async_computation | async-start | bytes 2097152 | tf_op jit(solution)/shard_map/all_to_all | solution.py:402
  21.9 0.0 collective-permute-done.5
  21.9 0.0 collective-permute-done.4
  21.9 0.7 collective-permute-start.9
  22.6 0.7 collective-permute-start.8
  23.3 0.7 collective-permute-start.7
  24.0 0.6 dynamic_slice.12
  24.6 0.7 dynamic-slice_minimum_fusion
  25.3 0.1 broadcast_bitcast_fusion
  25.4 0.7 constant_dynamic-slice_fusion.1
  26.1 0.8 %constant_dynamic-slice_fusion = (f32[1,256]{1,0:T(1,128)S(1)}, f32[1,256]{1,0:T(1,128)S(1)}) fusion(f32[2,2048]{1,0:T(2,128)} %param.12, s32[]{:T(128)S(6)} %select_n.19, s32[]{:T(128)S(6)} %add.73), kind=kLoop, calls=%fused_computation.15 | loop fusion | bytes 4104 | tf_op jit(solution)/shard_map/slice | solution.py:389
  26.9 0.1 multiply_add_fusion
  27.0 1.1 %fusion.2.ctt_ref = f32[128,256]{1,0:T(8,128)S(1)} fusion(f32[35]{0:T(128)S(1)} %mul.15, f32[128,256]{1,0:T(8,128)S(1)} %multiply_add_fusion, f32[35]{0:T(128)S(1)} %copy-done.4, pred[35,256]{1,0:T(8,128)(4,1)S(1)} %iota_compare_fusion), kind=kLoop, calls=%fused_computation.3 | loop fusion | flops 5701632 | bytes 271384 | tf_op jit(solution)/shard_map/reduce_sum | solution.py:394
  28.2 0.1 add_add_fusion
  28.3 9.2 %all-to-all-done = f32[64,32,128]{2,1,0:T(8,128)S(1)} async-done(((f32[64,32,128]{2,1,0:T(8,128)}), f32[64,32,128]{2,1,0:T(8,128)S(1)}, u32[]{:S(2)}, u32[]{:S(2)}) %all-to-all-start) | async-done | bytes 1048608 | tf_op jit(solution)/shard_map/all_to_all | solution.py:402
  37.5 0.1 broadcast_in_dim.51
  37.6 0.1 broadcast_in_dim.50
  37.6 1.4 %pad_maximum_fusion = f32[8,8,56,128]{3,2,1,0:T(8,128)} fusion(f32[8,8,4,128]{3,2,1,0:T(4,128)S(1)} %broadcast_in_dim.54, f32[8,8,4,128]{3,2,1,0:T(4,128)S(1)} %broadcast_in_dim.53, f32[8,8,24,128]{3,2,1,0:T(8,128)S(1)} %broadcast_in_dim.51, f32[8,8,24,128]{3,2,1,0:T(8,128)S(1)} %broadcast_in_dim.50), kind=kLoop, calls=%fused_computation.4 | loop fusion | flops 1376256 | bytes 3670016 | tf_op jit(solution)/shard_map/concatenate | solution.py:436
  39.1 7.1 %all-to-all-start.1 = ((f32[64,56,128]{2,1,0:T(8,128)}), f32[64,56,128]{2,1,0:T(8,128)S(1)}, u32[]{:S(2)}, u32[]{:S(2)}) async-start(f32[64,56,128]{2,1,0:T(8,128)} %bitcast.15), calls=%async_computation.1 | async-start | bytes 3670016 | tf_op jit(solution)/shard_map/all_to_all | solution.py:402
  46.2 0.0 copy-start.2
  46.2 1.3 %collective-permute-start.10 = (f32[384,128]{1,0:T(8,128)S(1)}, f32[384,128]{1,0:T(8,128)S(1)}, u32[]{:S(2)}, u32[]{:S(2)}) collective-permute-start(f32[384,128]{1,0:T(8,128)S(1)} %add_add_fusion), channel_id=1, source_target_pairs={{0,1},{2,3},{16,17},{18,19},{4,5},{6,7},{20,21},{22,23},{8,9},{10,... | collective-permute-start | bytes 589832 | tf_op jit(solution)/shard_map/ppermute | solution.py:385
  47.5 6.6 %collective-permute-done.10 = f32[384,128]{1,0:T(8,128)S(1)} collective-permute-done((f32[384,128]{1,0:T(8,128)S(1)}, f32[384,128]{1,0:T(8,128)S(1)}, u32[]{:S(2)}, u32[]{:S(2)}) %collective-permute-start.10) | collective-permute-done | bytes 196640 | tf_op jit(solution)/shard_map/ppermute | solution.py:385
  54.2 14.3 %inverse_factor.1 = (f32[384,128]{1,0:T(8,128)S(1)}, f32[768,1536]{1,0:T(8,128)S(1)}, f32[768,256]{1,0:T(8,128)S(1)}) custom-call(f32[384,128]{1,0:T(8,128)S(1)} %add.71.d_ref, f32[768,1536]{1,0:T(8,128)} %big_ref.1, f32[768,256]{1,0:T(8,128)} %t_ref.5), custom_call_target="tpu_custom_call" | custom-call | flops 200000000 | bytes 80000000 | tf_op jit(solution)/shard_map/inverse_factor/pallas_call | solution.py:118
  68.4 0.0 copy-start
  68.4 2.2 %copy-done = f32[768,1536]{1,0:T(8,128)} copy-done((f32[768,1536]{1,0:T(8,128)}, f32[768,1536]{1,0:T(8,128)S(1)}, u32[]{:S(2)}) %copy-start) | copy-done | bytes 4718616
  70.6 0.1 share.1
  70.7 3.7 %collective-permute-start.11 = (f32[64,32,128]{2,1,0:T(8,128)S(1)}, f32[64,32,128]{2,1,0:T(8,128)S(1)}, u32[]{:S(2)}, u32[]{:S(2)}) collective-permute-start(f32[64,32,128]{2,1,0:T(8,128)S(1)} %share.1), channel_id=1, source_target_pairs={{0,1},{1,0},{2,3},{3,2},{4,5},{5,4},{6,7},{7,6},{8,9},{9,8},{10,11... | collective-permute-start | bytes 3145736 | tf_op jit(solution)/shard_map/ppermute | solution.py:443
  74.4 1.8 %solve.1 = (f32[768,256]{1,0:T(8,128)S(1)}, bf16[256,768]{1,0:T(8,128)(2,1)S(1)}, bf16[768,768]{1,0:T(8,128)(2,1)S(1)}, bf16[768,768]{1,0:T(8,128)(2,1)S(1)}) custom-call(s32[2]{0:T(128)S(1)} %pad_add_fusion.place_ref, f32[6]{0:T(128)S(1)} %copy-done.2, s32[1,768]{1,0:T(1,128)S(1)} %broadcast_in_dim.49.wfs_ref, f32[64,56,128]{2,1,0:T(8,128)S(1)} %all-to-all-done.1.own_ref, ...), custom_call_target="tpu_custom_call" | custom-call | flops 1000000000 | bytes 6000000 | tf_op jit(solution)/shard_map/solve/pallas_call | solution.py:196
  76.2 0.5 collective-permute-done.11.other_ref
  76.7 6.2 %update.1 = (f32[768,1536]{1,0:T(8,128)}, f32[768,256]{1,0:T(8,128)}, f32[768,256]{1,0:T(8,128)}, f32[128,256]{1,0:T(8,128)}) custom-call(s32[2]{0:T(128)S(1)} %pad_add_fusion.place_ref, f32[6]{0:T(128)S(1)} %copy-done.2, s32[1,768]{1,0:T(1,128)S(1)} %broadcast_in_dim.49.wfs_ref, f32[768,1536]{1,0:T(8,128)S(1)} %copy-done.1, ...), custom_call_target="tpu_custom_call" | custom-call | flops 2000000000 | bytes 7000000 | tf_op jit(solution)/shard_map/update/pallas_call | solution.py:269
  (23 shorter events, 0.2 us)
Async XLA Ops:
  1.7 15.4 %copy-start.6 = (f32[35]{0:T(128)S(1)}, f32[35]{0:T(128)}, u32[]{:S(2)}) copy-start(f32[35]{0:T(128)} %param.14) | copy-start | bytes 424
  1.7 13.3 %collective-permute-start.2 = (f32[384,128]{1,0:T(8,128)S(1)}, f32[384,128]{1,0:T(8,128)S(1)}, u32[]{:S(2)}, u32[]{:S(2)}) collective-permute-start(f32[384,128]{1,0:T(8,128)S(1)} %get-tuple-element.26), channel_id=1, source_target_pairs={{0,96}} | collective-permute-start | bytes 589832 | tf_op jit(solution)/shard_map/ppermute | solution.py:385
  2.4 12.6 %collective-permute-start.1 = (f32[384,128]{1,0:T(8,128)S(1)}, f32[384,128]{1,0:T(8,128)S(1)}, u32[]{:S(2)}, u32[]{:S(2)}) collective-permute-start(f32[384,128]{1,0:T(8,128)S(1)} %get-tuple-element.26), channel_id=1, source_target_pairs={{0,32}} | collective-permute-start | bytes 589832 | tf_op jit(solution)/shard_map/ppermute | solution.py:385
  3.1 11.9 %collective-permute-start = (f32[384,128]{1,0:T(8,128)S(1)}, f32[384,128]{1,0:T(8,128)S(1)}, u32[]{:S(2)}, u32[]{:S(2)}) collective-permute-start(f32[384,128]{1,0:T(8,128)S(1)} %get-tuple-element.26), channel_id=1, source_target_pairs={{0,64}} | collective-permute-start | bytes 589832 | tf_op jit(solution)/shard_map/ppermute | solution.py:385
  3.7 20.3 %copy-start.5 = (s32[16]{0:T(128)S(1)}, s32[16]{0:T(128)}, u32[]{:S(2)}) copy-start(s32[16]{0:T(128)} %param.15) | copy-start | bytes 196
  3.7 23.3 %copy-start.4 = (f32[35]{0:T(128)S(1)}, f32[35]{0:T(128)}, u32[]{:S(2)}) copy-start(f32[35]{0:T(128)} %param.13) | copy-start | bytes 424
  3.8 24.4 %copy-start.3 = (s32[768]{0:T(1024)S(1)}, s32[768]{0:T(1024)}, u32[]{:S(2)}) copy-start(s32[768]{0:T(1024)} %wfs_ref.1) | copy-start | bytes 9220
  3.8 9.0 %collective-permute-start.3 = (f32[256,128]{1,0:T(8,128)S(1)}, f32[256,128]{1,0:T(8,128)S(1)}, u32[]{:S(2)}, u32[]{:S(2)}) collective-permute-start(f32[256,128]{1,0:T(8,128)S(1)} %get-tuple-element.27), channel_id=1, source_target_pairs={{0,1},{16,17},{32,33},{48,49},{64,65},{80,81},{96,97},{112,113}} | collective-permute-start | bytes 393224 | tf_op jit(solution)/shard_map/ppermute | solution.py:407
  15.1 6.8 %collective-permute-start.6 = (f32[384,128]{1,0:T(8,128)S(1)}, f32[384,128]{1,0:T(8,128)S(1)}, u32[]{:S(2)}, u32[]{:S(2)}) collective-permute-start(f32[384,128]{1,0:T(8,128)S(1)} %add_add_fusion.2), channel_id=1, source_target_pairs={{0,12},{32,44},{64,76},{96,108}} | collective-permute-start | bytes 589832 | tf_op jit(solution)/shard_map/ppermute | solution.py:385
  15.7 6.1 %collective-permute-start.5 = (f32[384,128]{1,0:T(8,128)S(1)}, f32[384,128]{1,0:T(8,128)S(1)}, u32[]{:S(2)}, u32[]{:S(2)}) collective-permute-start(f32[384,128]{1,0:T(8,128)S(1)} %add_add_fusion.2), channel_id=1, source_target_pairs={{0,4},{32,36},{64,68},{96,100}} | collective-permute-start | bytes 589832 | tf_op jit(solution)/shard_map/ppermute | solution.py:385
  16.4 5.5 %collective-permute-start.4 = (f32[384,128]{1,0:T(8,128)S(1)}, f32[384,128]{1,0:T(8,128)S(1)}, u32[]{:S(2)}, u32[]{:S(2)}) collective-permute-start(f32[384,128]{1,0:T(8,128)S(1)} %add_add_fusion.2), channel_id=1, source_target_pairs={{0,8},{32,40},{64,72},{96,104}} | collective-permute-start | bytes 589832 | tf_op jit(solution)/shard_map/ppermute | solution.py:385
  17.2 20.3 %all-to-all-start = ((f32[64,32,128]{2,1,0:T(8,128)}), f32[64,32,128]{2,1,0:T(8,128)S(1)}, u32[]{:S(2)}, u32[]{:S(2)}) async-start(f32[64,32,128]{2,1,0:T(8,128)} %pieces.1), calls=%async_computation | async-start | bytes 2097152 | tf_op jit(solution)/shard_map/all_to_all | solution.py:402
  21.9 6.3 %collective-permute-start.9 = (f32[384,128]{1,0:T(8,128)S(1)}, f32[384,128]{1,0:T(8,128)S(1)}, u32[]{:S(2)}, u32[]{:S(2)}) collective-permute-start(f32[384,128]{1,0:T(8,128)S(1)} %add_add_fusion.1), channel_id=1, source_target_pairs={{0,16},{4,20},{8,24},{12,28},{32,48},{36,52},{40,56},{44,60},{64,8... | collective-permute-start | bytes 589832 | tf_op jit(solution)/shard_map/ppermute | solution.py:385
  22.6 5.6 %collective-permute-start.8 = (f32[384,128]{1,0:T(8,128)S(1)}, f32[384,128]{1,0:T(8,128)S(1)}, u32[]{:S(2)}, u32[]{:S(2)}) collective-permute-start(f32[384,128]{1,0:T(8,128)S(1)} %add_add_fusion.1), channel_id=1, source_target_pairs={{0,18},{4,22},{8,26},{12,30},{32,50},{36,54},{40,58},{44,62},{64,8... | collective-permute-start | bytes 589832 | tf_op jit(solution)/shard_map/ppermute | solution.py:385
  23.3 4.9 %collective-permute-start.7 = (f32[384,128]{1,0:T(8,128)S(1)}, f32[384,128]{1,0:T(8,128)S(1)}, u32[]{:S(2)}, u32[]{:S(2)}) collective-permute-start(f32[384,128]{1,0:T(8,128)S(1)} %add_add_fusion.1), channel_id=1, source_target_pairs={{0,2},{4,6},{8,10},{12,14},{32,34},{36,38},{40,42},{44,46},{64,66}... | collective-permute-start | bytes 589832 | tf_op jit(solution)/shard_map/ppermute | solution.py:385
  39.1 31.5 %all-to-all-start.1 = ((f32[64,56,128]{2,1,0:T(8,128)}), f32[64,56,128]{2,1,0:T(8,128)S(1)}, u32[]{:S(2)}, u32[]{:S(2)}) async-start(f32[64,56,128]{2,1,0:T(8,128)} %bitcast.15), calls=%async_computation.1 | async-start | bytes 3670016 | tf_op jit(solution)/shard_map/all_to_all | solution.py:402
  46.2 28.2 %copy-start.2 = (f32[6]{0:T(128)S(1)}, f32[6]{0:T(128)}, u32[]{:S(2)}) copy-start(f32[6]{0:T(128)} %noise_ref.5) | copy-start | bytes 76
  46.2 7.9 %collective-permute-start.10 = (f32[384,128]{1,0:T(8,128)S(1)}, f32[384,128]{1,0:T(8,128)S(1)}, u32[]{:S(2)}, u32[]{:S(2)}) collective-permute-start(f32[384,128]{1,0:T(8,128)S(1)} %add_add_fusion), channel_id=1, source_target_pairs={{0,1},{2,3},{16,17},{18,19},{4,5},{6,7},{20,21},{22,23},{8,9},{10,... | collective-permute-start | bytes 589832 | tf_op jit(solution)/shard_map/ppermute | solution.py:385
  68.4 2.2 %copy-start = (f32[768,1536]{1,0:T(8,128)}, f32[768,1536]{1,0:T(8,128)S(1)}, u32[]{:S(2)}) copy-start(f32[768,1536]{1,0:T(8,128)S(1)} %get-tuple-element.38.a_ref) | copy-start | bytes 14155780
  70.6 6.1 %copy-start.1 = (f32[768,1536]{1,0:T(8,128)S(1)}, f32[768,1536]{1,0:T(8,128)}, u32[]{:S(2)}) copy-start(f32[768,1536]{1,0:T(8,128)} %copy-done) | copy-start | bytes 14155780
  70.7 6.0 %collective-permute-start.11 = (f32[64,32,128]{2,1,0:T(8,128)S(1)}, f32[64,32,128]{2,1,0:T(8,128)S(1)}, u32[]{:S(2)}, u32[]{:S(2)}) collective-permute-start(f32[64,32,128]{2,1,0:T(8,128)S(1)} %share.1), channel_id=1, source_target_pairs={{0,1},{1,0},{2,3},{3,2},{4,5},{5,4},{6,7},{7,6},{8,9},{9,8},{10,11... | collective-permute-start | bytes 3145736 | tf_op jit(solution)/shard_map/ppermute | solution.py:443

commit v6 on v5

--- a/solution.py
+++ b/solution.py
@@ -152,7 +152,8 @@
 
 
 def solve_kernel(
-    place_ref, noise_ref, wfs_ref, own_ref, inv_ref, pan_ref, inv3_ref, pair_ref, mine_ref
+    place_ref, noise_ref, wfs_ref, own_ref, inv_ref, pan_ref, inv3_ref, pair_ref, mine_ref, far_ref,
+    sem,
 ):
     inv = jnp.concatenate(
         [
@@ -173,8 +174,11 @@
         lead = dot3(right(block), inv3, ((1,), (1,)))
         pan_ref[:PB, :] = jnp.where(lane > sub, 0.0, lead)
 
+    copy = pltpu.make_async_copy(pan_ref, far_ref, sem)
+    copy.start()
     pair_ref[...] = left(pan_ref[...])
     mine_ref[...] = right(dot3(inv3, right(two_halves(own_ref, 24)), ((1,), (1,))), axis=0)
+    copy.wait()
 
 
 def share_kernel(own_ref, out_ref):
@@ -196,13 +200,15 @@
     return pl.pallas_call(
         solve_kernel,
         in_specs=[SMEM, SMEM, VMEM, VMEM, VMEM],
-        out_specs=[VMEM] * 4,
+        out_specs=[VMEM] * 4 + [pl.BlockSpec(memory_space=pl.ANY)],
         out_shape=[
             pltpu.VMEM((rows, PB), F32),
             pltpu.VMEM((PB, 3 * PB), jnp.bfloat16),
             pltpu.VMEM((rows, 3 * PB), jnp.bfloat16),
             pltpu.VMEM((3 * PB, rows), jnp.bfloat16),
-        ],
+            jax.ShapeDtypeStruct((rows, PB), F32),
+        ],
+        scratch_shapes=[pltpu.SemaphoreType.DMA],
         compiler_params=pltpu.CompilerParams(vmem_limit_bytes=20 << 20),
         cost_estimate=pl.CostEstimate(
             flops=1_000_000_000, transcendentals=0, bytes_accessed=6_000_000
@@ -213,7 +219,7 @@
 
 def update_kernel(
     place_ref, noise_ref, wfs_ref, a_ref, t_ref, own_ref, other_ref, panel_ref, inv3_ref, pair_ref,
-    mine_ref, ctt_ref, upd_ref, pan_ref, rec_ref, err_ref, theirs_ref, head_ref, head3_ref,
+    mine_ref, ctt_ref, upd_ref, rec_ref, err_ref, theirs_ref, head_ref, head3_ref,
 ):
     i = pl.program_id(0)
     row, col = place_ref[0], place_ref[1]
@@ -241,7 +247,6 @@
     for at, ref in ((core, mine_ref), (1 - core, theirs_ref)):
         where = pl.ds(pl.multiple_of(at * half, half), half)
         upd_ref[:, where] = a_ref[here, where] - dot3(pair, ref[...])
-    pan_ref[...] = panel_ref[here, :]
     rec_ref[...] = t_ref[here, :] - dot3(pair, head3_ref[...])
 
     @pl.when(lax.div(row, 2) == col)
@@ -273,13 +278,11 @@
         + [VMEM] * 9,
         out_specs=[
             tiled(width),
-            tiled(PB),
             tiled(target_width),
             pl.BlockSpec(ctt.shape, lambda i: (0, 0)),
         ],
         out_shape=[
             jax.ShapeDtypeStruct((rows, width), F32),
-            jax.ShapeDtypeStruct((rows, PB), F32),
             jax.ShapeDtypeStruct((rows, target_width), F32),
             jax.ShapeDtypeStruct(ctt.shape, F32),
         ],
@@ -300,23 +303,22 @@
 
 
 def pieces_kernel(a_ref, t_ref, second_ref, out_ref):
+    count = out_ref.shape[0]
     half = jnp.where(lax.axis_index("row") == 1, second_ref[...], t_ref[...])
-    count = out_ref.shape[0] // 2
-    out_ref[:count, :24, :] = a_ref[:, :HB].reshape(count, 24, HB)
-    out_ref[count:, :24, :] = a_ref[:, HB:].reshape(count, 24, HB)
-    half = half.reshape(2 * count, 4, HB)
+    half = half.reshape(count, 4, HB)
+    out_ref[:, :24, :] = a_ref[...].reshape(count, 24, HB)
     out_ref[:, 24:, :] = jnp.concatenate([half, jnp.zeros_like(half)], axis=1)
 
 
 def pieces_of(covariance, targets, second):
     far = lambda x: pltpu.with_memory_space_constraint(x, pltpu.HBM)
     rows = covariance.shape[0]
-    first = lambda *shape: pl.BlockSpec(shape, lambda i: (0,) * len(shape))
+    part = pl.BlockSpec((HB, HB), lambda i: (i, 0))
     return pl.pallas_call(
         pieces_kernel,
-        grid=(1,),
-        in_specs=[first(rows, PB), first(PB, HB), first(PB, HB)],
-        out_specs=first(64, 32, HB),
+        grid=(2,),
+        in_specs=[pl.BlockSpec((rows, HB), lambda i: (0, i)), part, part],
+        out_specs=pl.BlockSpec((32, 32, HB), lambda i: (i, 0, 0)),
         out_shape=jax.ShapeDtypeStruct((64, 32, HB), F32),
         compiler_params=pltpu.CompilerParams(vmem_limit_bytes=8 << 20),
         cost_estimate=pl.CostEstimate(flops=0, transcendentals=0, bytes_accessed=2_000_000),
@@ -442,10 +444,11 @@
     own, inv = lax.optimization_barrier((exchange(wanted), inv))
     other = lax.ppermute(share_of(own), "row", [(i, i ^ 1) for i in range(16)])
 
-    solved = solve(place, noise_var, wfs_row, own, inv, rows)
-    return update(
+    *solved, panel = solve(place, noise_var, wfs_row, own, inv, rows)
+    updated, reconstructor, error = update(
         place, noise_var, wfs_row, matrix, near_targets, own, other, solved, ctt
     )
+    return updated, panel, reconstructor, error
 
 
 def solution(mesh):

time: 83.5 us -> 83.1 us (level)
  no operation moved by 1% of the time
where the time goes in v6:
time: 83.1 us; the launch traced here: 82.5 us
  Pallas kernels  25.4 us (31%)
  starting transfers between devices  24.4 us (29%)
  waiting for transfers between devices  23.6 us (28%)
  local copies, waits for them, and re-layouts  4.56 us (5%)
  other arithmetic  3.66 us (4%)
  between operations  1 us (1%)
    pallas_call x1, Pallas kernels, inverse_of_factor(): pl.pallas_call(factor_kernel, in_specs=[VMEM, anywhere, anywhere], out_sp...  14.2 us
    all_to_all x2, starting transfers between devices, local(): lax.all_to_all(x, BOTH, 0, 0, axis_index_groups=groups, tiled=True)  12 us
    all_to_all x2, waiting for transfers between devices, local(): lax.all_to_all(x, BOTH, 0, 0, axis_index_groups=groups, tiled=True)  8.91 us
    ppermute x1, waiting for transfers between devices, local(): second = lax.ppermute(second, 'row', [(0, 1)])  7.58 us
    ppermute x10, starting transfers between devices, wave(): return sum([lax.ppermute(value, BOTH, perm) for perm in perms], value)  7.35 us
    ppermute x10, waiting for transfers between devices, wave(): return sum([lax.ppermute(value, BOTH, perm) for perm in perms], value)  6.76 us
    pallas_call x1, Pallas kernels, update(): pl.pallas_call(update_kernel, grid=(rows // PB,), in_specs=[SMEM, SMEM, p...  6.05 us
    ppermute x1, starting transfers between devices, local(): other = lax.ppermute(share_of(own), 'row', [(i, i ^ 1) for i in range(16)])  3.61 us
  transfers between devices with their start and end apart: 14, of which 4 were waited for; matrix products, arithmetic and copies ran while one was open for 5% of the time, Pallas kernels for 22%

profile of v6, /device:TPU:1, one launch (start us, length us, event | category | flops | bytes accessed | tf_op | source)
XLA Modules:
  0.0 82.5 jit_solution(12570466843817008845)
XLA Ops:
  0.6 1.0 %lead.1 = (f32[384,128]{1,0:T(8,128)S(1)}, f32[256,128]{1,0:T(8,128)S(1)}) custom-call(f32[768,1536]{1,0:T(8,128)} %big_ref.1, f32[6]{0:T(128)} %noise_ref.5, s32[768]{0:T(1024)} %wfs_ref.1, f32[768,256]{1,0:T(8,128)} %t_ref.5), custom_call_target="tpu_custom_call" | custom-call | bytes 800000 | tf_op jit(solution)/shard_map/lead/pallas_call | solution.py:344
  1.7 0.0 copy-start.6
  1.7 0.7 collective-permute-start.2
  2.4 0.7 collective-permute-start.1
  3.1 0.7 collective-permute-start
  3.7 0.0 copy-start.5
  3.7 0.0 copy-start.4
  3.8 0.0 copy-start.3
  3.8 1.4 %collective-permute-start.3 = (f32[256,128]{1,0:T(8,128)S(1)}, f32[256,128]{1,0:T(8,128)S(1)}, u32[]{:S(2)}, u32[]{:S(2)}) collective-permute-start(f32[256,128]{1,0:T(8,128)S(1)} %get-tuple-element.31), channel_id=1, source_target_pairs={{0,1},{16,17},{32,33},{48,49},{64,65},{80,81},{96,97},{112,113}} | collective-permute-start | bytes 393224 | tf_op jit(solution)/shard_map/ppermute | solution.py:409
  5.2 7.6 %collective-permute-done.3.second_ref = f32[256,128]{1,0:T(8,128)S(1)} collective-permute-done((f32[256,128]{1,0:T(8,128)S(1)}, f32[256,128]{1,0:T(8,128)S(1)}, u32[]{:S(2)}, u32[]{:S(2)}) %collective-permute-start.3) | collective-permute-done | bytes 131104 | tf_op jit(solution)/shard_map/ppermute | solution.py:409
  12.8 2.0 %pieces.1 = f32[64,32,128]{2,1,0:T(8,128)} custom-call(f32[768,1536]{1,0:T(8,128)} %big_ref.1, f32[768,256]{1,0:T(8,128)} %t_ref.5, f32[256,128]{1,0:T(8,128)S(1)} %collective-permute-done.3.second_ref), custom_call_target="tpu_custom_call" | custom-call | bytes 2000000 | tf_op jit(solution)/shard_map/pieces/pallas_call | solution.py:317
  14.8 0.0 collective-permute-done
  14.9 0.7 collective-permute-start.6
  15.5 0.7 collective-permute-start.5
  16.2 0.7 collective-permute-start.4
  16.9 0.1 pad_add_fusion.place_ref
  17.0 4.7 %all-to-all-start = ((f32[64,32,128]{2,1,0:T(8,128)}), f32[64,32,128]{2,1,0:T(8,128)S(1)}, u32[]{:S(2)}, u32[]{:S(2)}) async-start(f32[64,32,128]{2,1,0:T(8,128)} %pieces.1), calls=%async_computation | async-start | bytes 2097152 | tf_op jit(solution)/shard_map/all_to_all | solution.py:404
  21.7 0.0 collective-permute-done.6
  21.7 0.0 collective-permute-done.4
  21.8 0.7 collective-permute-start.9
  22.4 0.7 collective-permute-start.8
  23.1 0.7 collective-permute-start.7
  23.8 0.6 dynamic_slice.12
  24.4 0.7 dynamic-slice_minimum_fusion
  25.1 0.1 broadcast_bitcast_fusion
  25.2 0.7 constant_dynamic-slice_fusion.1
  25.9 0.8 %constant_dynamic-slice_fusion = (f32[1,256]{1,0:T(1,128)S(1)}, f32[1,256]{1,0:T(1,128)S(1)}) fusion(f32[2,2048]{1,0:T(2,128)} %param.12, s32[]{:T(128)S(6)} %select_n.19, s32[]{:T(128)S(6)} %add.73), kind=kLoop, calls=%fused_computation.15 | loop fusion | bytes 4104 | tf_op jit(solution)/shard_map/slice | solution.py:391
  26.7 0.1 multiply_add_fusion
  26.9 1.1 %fusion.2.ctt_ref = f32[128,256]{1,0:T(8,128)S(1)} fusion(f32[35]{0:T(128)S(1)} %mul.15, f32[128,256]{1,0:T(8,128)S(1)} %multiply_add_fusion, f32[35]{0:T(128)S(1)} %copy-done.4, pred[35,256]{1,0:T(8,128)(4,1)S(1)} %iota_compare_fusion), kind=kLoop, calls=%fused_computation.3 | loop fusion | flops 5701632 | bytes 271384 | tf_op jit(solution)/shard_map/reduce_sum | solution.py:396
  28.0 0.0 collective-permute-done.8
  28.0 0.0 collective-permute-done.7
  28.0 0.1 add_add_fusion
  28.1 8.9 %all-to-all-done = f32[64,32,128]{2,1,0:T(8,128)S(1)} async-done(((f32[64,32,128]{2,1,0:T(8,128)}), f32[64,32,128]{2,1,0:T(8,128)S(1)}, u32[]{:S(2)}, u32[]{:S(2)}) %all-to-all-start) | async-done | bytes 1048608 | tf_op jit(solution)/shard_map/all_to_all | solution.py:404
  37.1 0.1 broadcast_in_dim.51
  37.1 0.1 broadcast_in_dim.50
  37.2 1.4 %pad_maximum_fusion = f32[8,8,56,128]{3,2,1,0:T(8,128)} fusion(f32[8,8,4,128]{3,2,1,0:T(4,128)S(1)} %broadcast_in_dim.54, f32[8,8,4,128]{3,2,1,0:T(4,128)S(1)} %broadcast_in_dim.53, f32[8,8,24,128]{3,2,1,0:T(8,128)S(1)} %broadcast_in_dim.51, f32[8,8,24,128]{3,2,1,0:T(8,128)S(1)} %broadcast_in_dim.50), kind=kLoop, calls=%fused_computation.4 | loop fusion | flops 1376256 | bytes 3670016 | tf_op jit(solution)/shard_map/concatenate | solution.py:438
  38.6 7.3 %all-to-all-start.1 = ((f32[64,56,128]{2,1,0:T(8,128)}), f32[64,56,128]{2,1,0:T(8,128)S(1)}, u32[]{:S(2)}, u32[]{:S(2)}) async-start(f32[64,56,128]{2,1,0:T(8,128)} %bitcast.15), calls=%async_computation.1 | async-start | bytes 3670016 | tf_op jit(solution)/shard_map/all_to_all | solution.py:404
  46.0 0.0 copy-start.2
  46.0 1.3 %collective-permute-start.10 = (f32[384,128]{1,0:T(8,128)S(1)}, f32[384,128]{1,0:T(8,128)S(1)}, u32[]{:S(2)}, u32[]{:S(2)}) collective-permute-start(f32[384,128]{1,0:T(8,128)S(1)} %add_add_fusion), channel_id=1, source_target_pairs={{0,1},{2,3},{16,17},{18,19},{4,5},{6,7},{20,21},{22,23},{8,9},{10,... | collective-permute-start | bytes 589832 | tf_op jit(solution)/shard_map/ppermute | solution.py:387
  47.3 6.7 %collective-permute-done.10 = f32[384,128]{1,0:T(8,128)S(1)} collective-permute-done((f32[384,128]{1,0:T(8,128)S(1)}, f32[384,128]{1,0:T(8,128)S(1)}, u32[]{:S(2)}, u32[]{:S(2)}) %collective-permute-start.10) | collective-permute-done | bytes 196640 | tf_op jit(solution)/shard_map/ppermute | solution.py:387
  54.0 14.2 %inverse_factor.1 = (f32[384,128]{1,0:T(8,128)S(1)}, f32[768,1536]{1,0:T(8,128)S(1)}, f32[768,256]{1,0:T(8,128)S(1)}) custom-call(f32[384,128]{1,0:T(8,128)S(1)} %add.71.d_ref, f32[768,1536]{1,0:T(8,128)} %big_ref.1, f32[768,256]{1,0:T(8,128)} %t_ref.5), custom_call_target="tpu_custom_call" | custom-call | flops 200000000 | bytes 80000000 | tf_op jit(solution)/shard_map/inverse_factor/pallas_call | solution.py:118
  68.3 0.0 copy-start
  68.3 2.2 %copy-done = f32[768,1536]{1,0:T(8,128)} copy-done((f32[768,1536]{1,0:T(8,128)}, f32[768,1536]{1,0:T(8,128)S(1)}, u32[]{:S(2)}) %copy-start) | copy-done | bytes 4718616
  70.5 0.1 share.1
  70.6 3.6 %collective-permute-start.11 = (f32[64,32,128]{2,1,0:T(8,128)S(1)}, f32[64,32,128]{2,1,0:T(8,128)S(1)}, u32[]{:S(2)}, u32[]{:S(2)}) collective-permute-start(f32[64,32,128]{2,1,0:T(8,128)S(1)} %share.1), channel_id=1, source_target_pairs={{0,1},{1,0},{2,3},{3,2},{4,5},{5,4},{6,7},{7,6},{8,9},{9,8},{10,11... | collective-permute-start | bytes 3145736 | tf_op jit(solution)/shard_map/ppermute | solution.py:445
  74.2 2.0 %solve.1 = (f32[768,256]{1,0:T(8,128)S(1)}, bf16[256,768]{1,0:T(8,128)(2,1)S(1)}, bf16[768,768]{1,0:T(8,128)(2,1)S(1)}, bf16[768,768]{1,0:T(8,128)(2,1)S(1)}, f32[768,256]{1,0:T(8,128)}) custom-call(s32[2]{0:T(128)S(1)} %pad_add_fusion.place_ref, f32[6]{0:T(128)S(1)} %copy-done.2, s32[1,768]{1,0:T(1,128)S(1)} %broadcast_in_dim.49.wfs_ref, ...), custom_call_target="tpu_custom_call" | custom-call | flops 1000000000 | bytes 6000000 | tf_op jit(solution)/shard_map/solve/pallas_call | solution.py:200
  76.1 0.3 collective-permute-done.11.other_ref
  76.5 6.1 %update.1 = (f32[768,1536]{1,0:T(8,128)}, f32[768,256]{1,0:T(8,128)}, f32[128,256]{1,0:T(8,128)}) custom-call(s32[2]{0:T(128)S(1)} %pad_add_fusion.place_ref, f32[6]{0:T(128)S(1)} %copy-done.2, s32[1,768]{1,0:T(1,128)S(1)} %broadcast_in_dim.49.wfs_ref, f32[768,1536]{1,0:T(8,128)S(1)} %copy-done.1, f32[768,256]{1,0:T(8,128)S(1)} %get-tuple-element.43.t_ref, ...), custom_call_target="tpu_custom_call" | custom-call | flops 2000000000 | bytes 7000000 | tf_op jit(solution)/shard_map/update/pallas_call | solution.py:274
  (23 shorter events, 0.2 us)
Async XLA Ops:
  1.7 15.2 %copy-start.6 = (f32[35]{0:T(128)S(1)}, f32[35]{0:T(128)}, u32[]{:S(2)}) copy-start(f32[35]{0:T(128)} %param.14) | copy-start | bytes 424
  1.7 13.1 %collective-permute-start.2 = (f32[384,128]{1,0:T(8,128)S(1)}, f32[384,128]{1,0:T(8,128)S(1)}, u32[]{:S(2)}, u32[]{:S(2)}) collective-permute-start(f32[384,128]{1,0:T(8,128)S(1)} %get-tuple-element.30), channel_id=1, source_target_pairs={{0,96}} | collective-permute-start | bytes 589832 | tf_op jit(solution)/shard_map/ppermute | solution.py:387
  2.4 12.4 %collective-permute-start.1 = (f32[384,128]{1,0:T(8,128)S(1)}, f32[384,128]{1,0:T(8,128)S(1)}, u32[]{:S(2)}, u32[]{:S(2)}) collective-permute-start(f32[384,128]{1,0:T(8,128)S(1)} %get-tuple-element.30), channel_id=1, source_target_pairs={{0,32}} | collective-permute-start | bytes 589832 | tf_op jit(solution)/shard_map/ppermute | solution.py:387
  3.1 11.8 %collective-permute-start = (f32[384,128]{1,0:T(8,128)S(1)}, f32[384,128]{1,0:T(8,128)S(1)}, u32[]{:S(2)}, u32[]{:S(2)}) collective-permute-start(f32[384,128]{1,0:T(8,128)S(1)} %get-tuple-element.30), channel_id=1, source_target_pairs={{0,64}} | collective-permute-start | bytes 589832 | tf_op jit(solution)/shard_map/ppermute | solution.py:387
  3.7 20.1 %copy-start.5 = (s32[16]{0:T(128)S(1)}, s32[16]{0:T(128)}, u32[]{:S(2)}) copy-start(s32[16]{0:T(128)} %param.15) | copy-start | bytes 196
  3.7 23.1 %copy-start.4 = (f32[35]{0:T(128)S(1)}, f32[35]{0:T(128)}, u32[]{:S(2)}) copy-start(f32[35]{0:T(128)} %param.13) | copy-start | bytes 424
  3.8 24.2 %copy-start.3 = (s32[768]{0:T(1024)S(1)}, s32[768]{0:T(1024)}, u32[]{:S(2)}) copy-start(s32[768]{0:T(1024)} %wfs_ref.1) | copy-start | bytes 9220
  3.8 9.0 %collective-permute-start.3 = (f32[256,128]{1,0:T(8,128)S(1)}, f32[256,128]{1,0:T(8,128)S(1)}, u32[]{:S(2)}, u32[]{:S(2)}) collective-permute-start(f32[256,128]{1,0:T(8,128)S(1)} %get-tuple-element.31), channel_id=1, source_target_pairs={{0,1},{16,17},{32,33},{48,49},{64,65},{80,81},{96,97},{112,113}} | collective-permute-start | bytes 393224 | tf_op jit(solution)/shard_map/ppermute | solution.py:409
  14.9 6.8 %collective-permute-start.6 = (f32[384,128]{1,0:T(8,128)S(1)}, f32[384,128]{1,0:T(8,128)S(1)}, u32[]{:S(2)}, u32[]{:S(2)}) collective-permute-start(f32[384,128]{1,0:T(8,128)S(1)} %add_add_fusion.2), channel_id=1, source_target_pairs={{0,12},{32,44},{64,76},{96,108}} | collective-permute-start | bytes 589832 | tf_op jit(solution)/shard_map/ppermute | solution.py:387
  15.5 6.1 %collective-permute-start.5 = (f32[384,128]{1,0:T(8,128)S(1)}, f32[384,128]{1,0:T(8,128)S(1)}, u32[]{:S(2)}, u32[]{:S(2)}) collective-permute-start(f32[384,128]{1,0:T(8,128)S(1)} %add_add_fusion.2), channel_id=1, source_target_pairs={{0,4},{32,36},{64,68},{96,100}} | collective-permute-start | bytes 589832 | tf_op jit(solution)/shard_map/ppermute | solution.py:387
  16.2 5.5 %collective-permute-start.4 = (f32[384,128]{1,0:T(8,128)S(1)}, f32[384,128]{1,0:T(8,128)S(1)}, u32[]{:S(2)}, u32[]{:S(2)}) collective-permute-start(f32[384,128]{1,0:T(8,128)S(1)} %add_add_fusion.2), channel_id=1, source_target_pairs={{0,8},{32,40},{64,72},{96,104}} | collective-permute-start | bytes 589832 | tf_op jit(solution)/shard_map/ppermute | solution.py:387
  17.0 20.0 %all-to-all-start = ((f32[64,32,128]{2,1,0:T(8,128)}), f32[64,32,128]{2,1,0:T(8,128)S(1)}, u32[]{:S(2)}, u32[]{:S(2)}) async-start(f32[64,32,128]{2,1,0:T(8,128)} %pieces.1), calls=%async_computation | async-start | bytes 2097152 | tf_op jit(solution)/shard_map/all_to_all | solution.py:404
  21.8 6.3 %collective-permute-start.9 = (f32[384,128]{1,0:T(8,128)S(1)}, f32[384,128]{1,0:T(8,128)S(1)}, u32[]{:S(2)}, u32[]{:S(2)}) collective-permute-start(f32[384,128]{1,0:T(8,128)S(1)} %add_add_fusion.1), channel_id=1, source_target_pairs={{0,16},{4,20},{8,24},{12,28},{32,48},{36,52},{40,56},{44,60},{64,8... | collective-permute-start | bytes 589832 | tf_op jit(solution)/shard_map/ppermute | solution.py:387
  22.4 5.6 %collective-permute-start.8 = (f32[384,128]{1,0:T(8,128)S(1)}, f32[384,128]{1,0:T(8,128)S(1)}, u32[]{:S(2)}, u32[]{:S(2)}) collective-permute-start(f32[384,128]{1,0:T(8,128)S(1)} %add_add_fusion.1), channel_id=1, source_target_pairs={{0,18},{4,22},{8,26},{12,30},{32,50},{36,54},{40,58},{44,62},{64,8... | collective-permute-start | bytes 589832 | tf_op jit(solution)/shard_map/ppermute | solution.py:387
  23.1 4.9 %collective-permute-start.7 = (f32[384,128]{1,0:T(8,128)S(1)}, f32[384,128]{1,0:T(8,128)S(1)}, u32[]{:S(2)}, u32[]{:S(2)}) collective-permute-start(f32[384,128]{1,0:T(8,128)S(1)} %add_add_fusion.1), channel_id=1, source_target_pairs={{0,2},{4,6},{8,10},{12,14},{32,34},{36,38},{40,42},{44,46},{64,66}... | collective-permute-start | bytes 589832 | tf_op jit(solution)/shard_map/ppermute | solution.py:387
  38.6 31.8 %all-to-all-start.1 = ((f32[64,56,128]{2,1,0:T(8,128)}), f32[64,56,128]{2,1,0:T(8,128)S(1)}, u32[]{:S(2)}, u32[]{:S(2)}) async-start(f32[64,56,128]{2,1,0:T(8,128)} %bitcast.15), calls=%async_computation.1 | async-start | bytes 3670016 | tf_op jit(solution)/shard_map/all_to_all | solution.py:404
  46.0 28.2 %copy-start.2 = (f32[6]{0:T(128)S(1)}, f32[6]{0:T(128)}, u32[]{:S(2)}) copy-start(f32[6]{0:T(128)} %noise_ref.5) | copy-start | bytes 76
  46.0 8.0 %collective-permute-start.10 = (f32[384,128]{1,0:T(8,128)S(1)}, f32[384,128]{1,0:T(8,128)S(1)}, u32[]{:S(2)}, u32[]{:S(2)}) collective-permute-start(f32[384,128]{1,0:T(8,128)S(1)} %add_add_fusion), channel_id=1, source_target_pairs={{0,1},{2,3},{16,17},{18,19},{4,5},{6,7},{20,21},{22,23},{8,9},{10,... | collective-permute-start | bytes 589832 | tf_op jit(solution)/shard_map/ppermute | solution.py:387
  68.3 2.2 %copy-start = (f32[768,1536]{1,0:T(8,128)}, f32[768,1536]{1,0:T(8,128)S(1)}, u32[]{:S(2)}) copy-start(f32[768,1536]{1,0:T(8,128)S(1)} %get-tuple-element.42.a_ref) | copy-start | bytes 14155780
  70.5 6.0 %copy-start.1 = (f32[768,1536]{1,0:T(8,128)S(1)}, f32[768,1536]{1,0:T(8,128)}, u32[]{:S(2)}) copy-start(f32[768,1536]{1,0:T(8,128)} %copy-done) | copy-start | bytes 14155780
  70.6 5.9 %collective-permute-start.11 = (f32[64,32,128]{2,1,0:T(8,128)S(1)}, f32[64,32,128]{2,1,0:T(8,128)S(1)}, u32[]{:S(2)}, u32[]{:S(2)}) collective-permute-start(f32[64,32,128]{2,1,0:T(8,128)S(1)} %share.1), channel_id=1, source_target_pairs={{0,1},{1,0},{2,3},{3,2},{4,5},{5,4},{6,7},{7,6},{8,9},{9,8},{10,11... | collective-permute-start | bytes 3145736 | tf_op jit(solution)/shard_map/ppermute | solution.py:445

commit v7 on v6

--- a/solution.py
+++ b/solution.py
@@ -368,8 +368,8 @@
 def rounds_of():
     four, two = range(4), range(2)
     return (
-        [[(device(0, 0, 0, 0, 0), device(k, 0, 0, 0, 0))] for k in (2, 1, 3)],
-        [[(device(x, 0, 0, 0, 0), device(x, 0, k, 0, 0)) for x in four] for k in (2, 1, 3)],
+        [[(device(0, 0, 0, 0, 0), device(k, 0, 0, 0, 0))] for k in (1, 3, 2)],
+        [[(device(x, 0, 0, 0, 0), device(x, 0, k, 0, 0)) for x in four] for k in (1, 3, 2)],
         [
             [(device(x, 0, y, 0, 0), device(x, lo, y, hi, 0)) for x in four for y in four]
             for lo, hi in ((0, 1), (1, 1), (1, 0))

time: 83.1 us -> 82.3 us (level)
  starting transfers between devices: 24.4 us -> 21.9 us
  waiting for transfers between devices: 23.6 us -> 25.2 us
    all_to_all x2, starting transfers between devices: 12 us -> 9.65 us  [local(): lax.all_to_all(x, BOTH, 0, 0, axis_index_groups=groups, tiled=True)]
    all_to_all x2, waiting for transfers between devices: 8.91 us -> 10.1 us  [local(): lax.all_to_all(x, BOTH, 0, 0, axis_index_groups=groups, tiled=True)]
where the time goes in v7:
time: 82.3 us; the launch traced here: 81.7 us
  Pallas kernels  25.4 us (31%)
  waiting for transfers between devices  25.2 us (31%)
  starting transfers between devices  21.9 us (27%)
  local copies, waits for them, and re-layouts  4.56 us (6%)
  other arithmetic  3.66 us (4%)
  between operations  1 us (1%)
    pallas_call x1, Pallas kernels, inverse_of_factor(): pl.pallas_call(factor_kernel, in_specs=[VMEM, anywhere, anywhere], out_sp...  14.2 us
    all_to_all x2, waiting for transfers between devices, local(): lax.all_to_all(x, BOTH, 0, 0, axis_index_groups=groups, tiled=True)  10.1 us
    all_to_all x2, starting transfers between devices, local(): lax.all_to_all(x, BOTH, 0, 0, axis_index_groups=groups, tiled=True)  9.65 us
    ppermute x1, waiting for transfers between devices, local(): second = lax.ppermute(second, 'row', [(0, 1)])  7.85 us
    ppermute x10, starting transfers between devices, wave(): return sum([lax.ppermute(value, BOTH, perm) for perm in perms], value)  7.35 us
    ppermute x10, waiting for transfers between devices, wave(): return sum([lax.ppermute(value, BOTH, perm) for perm in perms], value)  6.9 us
    pallas_call x1, Pallas kernels, update(): pl.pallas_call(update_kernel, grid=(rows // PB,), in_specs=[SMEM, SMEM, p...  6.06 us
    ppermute x1, starting transfers between devices, local(): other = lax.ppermute(share_of(own), 'row', [(i, i ^ 1) for i in range(16)])  3.47 us
  transfers between devices with their start and end apart: 14, of which 4 were waited for; matrix products, arithmetic and copies ran while one was open for 5% of the time, Pallas kernels for 22%

profile of v7, /device:TPU:1, one launch (start us, length us, event | category | flops | bytes accessed | tf_op | source)
XLA Modules:
  0.0 81.7 jit_solution(5593111865959921938)
XLA Ops:
  0.6 1.0 %lead.1 = (f32[384,128]{1,0:T(8,128)S(1)}, f32[256,128]{1,0:T(8,128)S(1)}) custom-call(f32[768,1536]{1,0:T(8,128)} %big_ref.1, f32[6]{0:T(128)} %noise_ref.5, s32[768]{0:T(1024)} %wfs_ref.1, f32[768,256]{1,0:T(8,128)} %t_ref.5), custom_call_target="tpu_custom_call" | custom-call | bytes 800000 | tf_op jit(solution)/shard_map/lead/pallas_call | solution.py:344
  1.7 0.0 copy-start.6
  1.7 0.7 collective-permute-start.2
  2.4 0.7 collective-permute-start.1
  3.1 0.7 collective-permute-start
  3.7 0.0 copy-start.5
  3.7 0.0 copy-start.4
  3.8 0.0 copy-start.3
  3.8 1.4 %collective-permute-start.3 = (f32[256,128]{1,0:T(8,128)S(1)}, f32[256,128]{1,0:T(8,128)S(1)}, u32[]{:S(2)}, u32[]{:S(2)}) collective-permute-start(f32[256,128]{1,0:T(8,128)S(1)} %get-tuple-element.31), channel_id=1, source_target_pairs={{0,1},{16,17},{32,33},{48,49},{64,65},{80,81},{96,97},{112,113}} | collective-permute-start | bytes 393224 | tf_op jit(solution)/shard_map/ppermute | solution.py:409
  5.2 7.8 %collective-permute-done.3.second_ref = f32[256,128]{1,0:T(8,128)S(1)} collective-permute-done((f32[256,128]{1,0:T(8,128)S(1)}, f32[256,128]{1,0:T(8,128)S(1)}, u32[]{:S(2)}, u32[]{:S(2)}) %collective-permute-start.3) | collective-permute-done | bytes 131104 | tf_op jit(solution)/shard_map/ppermute | solution.py:409
  13.0 2.0 %pieces.1 = f32[64,32,128]{2,1,0:T(8,128)} custom-call(f32[768,1536]{1,0:T(8,128)} %big_ref.1, f32[768,256]{1,0:T(8,128)} %t_ref.5, f32[256,128]{1,0:T(8,128)S(1)} %collective-permute-done.3.second_ref), custom_call_target="tpu_custom_call" | custom-call | bytes 2000000 | tf_op jit(solution)/shard_map/pieces/pallas_call | solution.py:317
  15.1 0.0 collective-permute-done
  15.1 0.7 collective-permute-start.6
  15.8 0.7 collective-permute-start.5
  16.5 0.7 collective-permute-start.4
  17.2 0.1 pad_add_fusion.place_ref
  17.3 4.7 %all-to-all-start = ((f32[64,32,128]{2,1,0:T(8,128)}), f32[64,32,128]{2,1,0:T(8,128)S(1)}, u32[]{:S(2)}, u32[]{:S(2)}) async-start(f32[64,32,128]{2,1,0:T(8,128)} %pieces.1), calls=%async_computation | async-start | bytes 2097152 | tf_op jit(solution)/shard_map/all_to_all | solution.py:404
  21.9 0.0 collective-permute-done.6
  22.0 0.0 collective-permute-done.4
  22.0 0.7 collective-permute-start.9
  22.7 0.7 collective-permute-start.8
  23.4 0.7 collective-permute-start.7
  24.1 0.6 dynamic_slice.12
  24.7 0.7 dynamic-slice_minimum_fusion
  25.4 0.1 broadcast_bitcast_fusion
  25.5 0.7 constant_dynamic-slice_fusion.1
  26.2 0.8 %constant_dynamic-slice_fusion = (f32[1,256]{1,0:T(1,128)S(1)}, f32[1,256]{1,0:T(1,128)S(1)}) fusion(f32[2,2048]{1,0:T(2,128)} %param.12, s32[]{:T(128)S(6)} %select_n.19, s32[]{:T(128)S(6)} %add.73), kind=kLoop, calls=%fused_computation.15 | loop fusion | bytes 4104 | tf_op jit(solution)/shard_map/slice | solution.py:391
  27.0 0.1 multiply_add_fusion
  27.1 1.1 %fusion.2.ctt_ref = f32[128,256]{1,0:T(8,128)S(1)} fusion(f32[35]{0:T(128)S(1)} %mul.15, f32[128,256]{1,0:T(8,128)S(1)} %multiply_add_fusion, f32[35]{0:T(128)S(1)} %copy-done.4, pred[35,256]{1,0:T(8,128)(4,1)S(1)} %iota_compare_fusion), kind=kLoop, calls=%fused_computation.3 | loop fusion | flops 5701632 | bytes 271384 | tf_op jit(solution)/shard_map/reduce_sum | solution.py:396
  28.3 0.0 collective-permute-done.8
  28.3 0.0 collective-permute-done.7
  28.3 0.1 add_add_fusion
  28.4 10.1 %all-to-all-done = f32[64,32,128]{2,1,0:T(8,128)S(1)} async-done(((f32[64,32,128]{2,1,0:T(8,128)}), f32[64,32,128]{2,1,0:T(8,128)S(1)}, u32[]{:S(2)}, u32[]{:S(2)}) %all-to-all-start) | async-done | bytes 1048608 | tf_op jit(solution)/shard_map/all_to_all | solution.py:404
  38.6 0.1 broadcast_in_dim.51
  38.6 0.1 broadcast_in_dim.50
  38.7 1.4 %pad_maximum_fusion = f32[8,8,56,128]{3,2,1,0:T(8,128)} fusion(f32[8,8,4,128]{3,2,1,0:T(4,128)S(1)} %broadcast_in_dim.54, f32[8,8,4,128]{3,2,1,0:T(4,128)S(1)} %broadcast_in_dim.53, f32[8,8,24,128]{3,2,1,0:T(8,128)S(1)} %broadcast_in_dim.51, f32[8,8,24,128]{3,2,1,0:T(8,128)S(1)} %broadcast_in_dim.50), kind=kLoop, calls=%fused_computation.4 | loop fusion | flops 1376256 | bytes 3670016 | tf_op jit(solution)/shard_map/concatenate | solution.py:438
  40.1 5.0 %all-to-all-start.1 = ((f32[64,56,128]{2,1,0:T(8,128)}), f32[64,56,128]{2,1,0:T(8,128)S(1)}, u32[]{:S(2)}, u32[]{:S(2)}) async-start(f32[64,56,128]{2,1,0:T(8,128)} %bitcast.15), calls=%async_computation.1 | async-start | bytes 3670016 | tf_op jit(solution)/shard_map/all_to_all | solution.py:404
  45.1 0.0 copy-start.2
  45.1 1.3 %collective-permute-start.10 = (f32[384,128]{1,0:T(8,128)S(1)}, f32[384,128]{1,0:T(8,128)S(1)}, u32[]{:S(2)}, u32[]{:S(2)}) collective-permute-start(f32[384,128]{1,0:T(8,128)S(1)} %add_add_fusion), channel_id=1, source_target_pairs={{0,1},{2,3},{16,17},{18,19},{4,5},{6,7},{20,21},{22,23},{8,9},{10,... | collective-permute-start | bytes 589832 | tf_op jit(solution)/shard_map/ppermute | solution.py:387
  46.4 6.9 %collective-permute-done.10 = f32[384,128]{1,0:T(8,128)S(1)} collective-permute-done((f32[384,128]{1,0:T(8,128)S(1)}, f32[384,128]{1,0:T(8,128)S(1)}, u32[]{:S(2)}, u32[]{:S(2)}) %collective-permute-start.10) | collective-permute-done | bytes 196640 | tf_op jit(solution)/shard_map/ppermute | solution.py:387
  53.3 14.2 %inverse_factor.1 = (f32[384,128]{1,0:T(8,128)S(1)}, f32[768,1536]{1,0:T(8,128)S(1)}, f32[768,256]{1,0:T(8,128)S(1)}) custom-call(f32[384,128]{1,0:T(8,128)S(1)} %add.71.d_ref, f32[768,1536]{1,0:T(8,128)} %big_ref.1, f32[768,256]{1,0:T(8,128)} %t_ref.5), custom_call_target="tpu_custom_call" | custom-call | flops 200000000 | bytes 80000000 | tf_op jit(solution)/shard_map/inverse_factor/pallas_call | solution.py:118
  67.6 0.0 copy-start
  67.6 2.2 %copy-done = f32[768,1536]{1,0:T(8,128)} copy-done((f32[768,1536]{1,0:T(8,128)}, f32[768,1536]{1,0:T(8,128)S(1)}, u32[]{:S(2)}) %copy-start) | copy-done | bytes 4718616
  69.8 0.1 share.1
  69.9 3.5 %collective-permute-start.11 = (f32[64,32,128]{2,1,0:T(8,128)S(1)}, f32[64,32,128]{2,1,0:T(8,128)S(1)}, u32[]{:S(2)}, u32[]{:S(2)}) collective-permute-start(f32[64,32,128]{2,1,0:T(8,128)S(1)} %share.1), channel_id=1, source_target_pairs={{0,1},{1,0},{2,3},{3,2},{4,5},{5,4},{6,7},{7,6},{8,9},{9,8},{10,11... | collective-permute-start | bytes 3145736 | tf_op jit(solution)/shard_map/ppermute | solution.py:445
  73.3 2.0 %solve.1 = (f32[768,256]{1,0:T(8,128)S(1)}, bf16[256,768]{1,0:T(8,128)(2,1)S(1)}, bf16[768,768]{1,0:T(8,128)(2,1)S(1)}, bf16[768,768]{1,0:T(8,128)(2,1)S(1)}, f32[768,256]{1,0:T(8,128)}) custom-call(s32[2]{0:T(128)S(1)} %pad_add_fusion.place_ref, f32[6]{0:T(128)S(1)} %copy-done.2, s32[1,768]{1,0:T(1,128)S(1)} %broadcast_in_dim.49.wfs_ref, ...), custom_call_target="tpu_custom_call" | custom-call | flops 1000000000 | bytes 6000000 | tf_op jit(solution)/shard_map/solve/pallas_call | solution.py:200
  75.3 0.3 collective-permute-done.11.other_ref
  75.6 6.1 %update.1 = (f32[768,1536]{1,0:T(8,128)}, f32[768,256]{1,0:T(8,128)}, f32[128,256]{1,0:T(8,128)}) custom-call(s32[2]{0:T(128)S(1)} %pad_add_fusion.place_ref, f32[6]{0:T(128)S(1)} %copy-done.2, s32[1,768]{1,0:T(1,128)S(1)} %broadcast_in_dim.49.wfs_ref, f32[768,1536]{1,0:T(8,128)S(1)} %copy-done.1, f32[768,256]{1,0:T(8,128)S(1)} %get-tuple-element.43.t_ref, ...), custom_call_target="tpu_custom_call" | custom-call | flops 2000000000 | bytes 7000000 | tf_op jit(solution)/shard_map/update/pallas_call | solution.py:274
  (23 shorter events, 0.2 us)
Async XLA Ops:
  1.7 15.5 %copy-start.6 = (f32[35]{0:T(128)S(1)}, f32[35]{0:T(128)}, u32[]{:S(2)}) copy-start(f32[35]{0:T(128)} %param.14) | copy-start | bytes 424
  1.7 13.4 %collective-permute-start.2 = (f32[384,128]{1,0:T(8,128)S(1)}, f32[384,128]{1,0:T(8,128)S(1)}, u32[]{:S(2)}, u32[]{:S(2)}) collective-permute-start(f32[384,128]{1,0:T(8,128)S(1)} %get-tuple-element.30), channel_id=1, source_target_pairs={{0,64}} | collective-permute-start | bytes 589832 | tf_op jit(solution)/shard_map/ppermute | solution.py:387
  2.4 12.7 %collective-permute-start.1 = (f32[384,128]{1,0:T(8,128)S(1)}, f32[384,128]{1,0:T(8,128)S(1)}, u32[]{:S(2)}, u32[]{:S(2)}) collective-permute-start(f32[384,128]{1,0:T(8,128)S(1)} %get-tuple-element.30), channel_id=1, source_target_pairs={{0,96}} | collective-permute-start | bytes 589832 | tf_op jit(solution)/shard_map/ppermute | solution.py:387
  3.1 12.0 %collective-permute-start = (f32[384,128]{1,0:T(8,128)S(1)}, f32[384,128]{1,0:T(8,128)S(1)}, u32[]{:S(2)}, u32[]{:S(2)}) collective-permute-start(f32[384,128]{1,0:T(8,128)S(1)} %get-tuple-element.30), channel_id=1, source_target_pairs={{0,32}} | collective-permute-start | bytes 589832 | tf_op jit(solution)/shard_map/ppermute | solution.py:387
  3.7 20.3 %copy-start.5 = (s32[16]{0:T(128)S(1)}, s32[16]{0:T(128)}, u32[]{:S(2)}) copy-start(s32[16]{0:T(128)} %param.15) | copy-start | bytes 196
  3.7 23.4 %copy-start.4 = (f32[35]{0:T(128)S(1)}, f32[35]{0:T(128)}, u32[]{:S(2)}) copy-start(f32[35]{0:T(128)} %param.13) | copy-start | bytes 424
  3.8 24.5 %copy-start.3 = (s32[768]{0:T(1024)S(1)}, s32[768]{0:T(1024)}, u32[]{:S(2)}) copy-start(s32[768]{0:T(1024)} %wfs_ref.1) | copy-start | bytes 9220
  3.8 9.3 %collective-permute-start.3 = (f32[256,128]{1,0:T(8,128)S(1)}, f32[256,128]{1,0:T(8,128)S(1)}, u32[]{:S(2)}, u32[]{:S(2)}) collective-permute-start(f32[256,128]{1,0:T(8,128)S(1)} %get-tuple-element.31), channel_id=1, source_target_pairs={{0,1},{16,17},{32,33},{48,49},{64,65},{80,81},{96,97},{112,113}} | collective-permute-start | bytes 393224 | tf_op jit(solution)/shard_map/ppermute | solution.py:409
  15.1 6.8 %collective-permute-start.6 = (f32[384,128]{1,0:T(8,128)S(1)}, f32[384,128]{1,0:T(8,128)S(1)}, u32[]{:S(2)}, u32[]{:S(2)}) collective-permute-start(f32[384,128]{1,0:T(8,128)S(1)} %add_add_fusion.2), channel_id=1, source_target_pairs={{0,8},{32,40},{64,72},{96,104}} | collective-permute-start | bytes 589832 | tf_op jit(solution)/shard_map/ppermute | solution.py:387
  15.8 6.1 %collective-permute-start.5 = (f32[384,128]{1,0:T(8,128)S(1)}, f32[384,128]{1,0:T(8,128)S(1)}, u32[]{:S(2)}, u32[]{:S(2)}) collective-permute-start(f32[384,128]{1,0:T(8,128)S(1)} %add_add_fusion.2), channel_id=1, source_target_pairs={{0,12},{32,44},{64,76},{96,108}} | collective-permute-start | bytes 589832 | tf_op jit(solution)/shard_map/ppermute | solution.py:387
  16.5 5.5 %collective-permute-start.4 = (f32[384,128]{1,0:T(8,128)S(1)}, f32[384,128]{1,0:T(8,128)S(1)}, u32[]{:S(2)}, u32[]{:S(2)}) collective-permute-start(f32[384,128]{1,0:T(8,128)S(1)} %add_add_fusion.2), channel_id=1, source_target_pairs={{0,4},{32,36},{64,68},{96,100}} | collective-permute-start | bytes 589832 | tf_op jit(solution)/shard_map/ppermute | solution.py:387
  17.3 21.2 %all-to-all-start = ((f32[64,32,128]{2,1,0:T(8,128)}), f32[64,32,128]{2,1,0:T(8,128)S(1)}, u32[]{:S(2)}, u32[]{:S(2)}) async-start(f32[64,32,128]{2,1,0:T(8,128)} %pieces.1), calls=%async_computation | async-start | bytes 2097152 | tf_op jit(solution)/shard_map/all_to_all | solution.py:404
  22.0 6.3 %collective-permute-start.9 = (f32[384,128]{1,0:T(8,128)S(1)}, f32[384,128]{1,0:T(8,128)S(1)}, u32[]{:S(2)}, u32[]{:S(2)}) collective-permute-start(f32[384,128]{1,0:T(8,128)S(1)} %add_add_fusion.1), channel_id=1, source_target_pairs={{0,16},{4,20},{8,24},{12,28},{32,48},{36,52},{40,56},{44,60},{64,8... | collective-permute-start | bytes 589832 | tf_op jit(solution)/shard_map/ppermute | solution.py:387
  22.7 5.6 %collective-permute-start.8 = (f32[384,128]{1,0:T(8,128)S(1)}, f32[384,128]{1,0:T(8,128)S(1)}, u32[]{:S(2)}, u32[]{:S(2)}) collective-permute-start(f32[384,128]{1,0:T(8,128)S(1)} %add_add_fusion.1), channel_id=1, source_target_pairs={{0,18},{4,22},{8,26},{12,30},{32,50},{36,54},{40,58},{44,62},{64,8... | collective-permute-start | bytes 589832 | tf_op jit(solution)/shard_map/ppermute | solution.py:387
  23.4 4.9 %collective-permute-start.7 = (f32[384,128]{1,0:T(8,128)S(1)}, f32[384,128]{1,0:T(8,128)S(1)}, u32[]{:S(2)}, u32[]{:S(2)}) collective-permute-start(f32[384,128]{1,0:T(8,128)S(1)} %add_add_fusion.1), channel_id=1, source_target_pairs={{0,2},{4,6},{8,10},{12,14},{32,34},{36,38},{40,42},{44,46},{64,66}... | collective-permute-start | bytes 589832 | tf_op jit(solution)/shard_map/ppermute | solution.py:387
  40.1 29.7 %all-to-all-start.1 = ((f32[64,56,128]{2,1,0:T(8,128)}), f32[64,56,128]{2,1,0:T(8,128)S(1)}, u32[]{:S(2)}, u32[]{:S(2)}) async-start(f32[64,56,128]{2,1,0:T(8,128)} %bitcast.15), calls=%async_computation.1 | async-start | bytes 3670016 | tf_op jit(solution)/shard_map/all_to_all | solution.py:404
  45.1 28.2 %copy-start.2 = (f32[6]{0:T(128)S(1)}, f32[6]{0:T(128)}, u32[]{:S(2)}) copy-start(f32[6]{0:T(128)} %noise_ref.5) | copy-start | bytes 76
  45.1 8.2 %collective-permute-start.10 = (f32[384,128]{1,0:T(8,128)S(1)}, f32[384,128]{1,0:T(8,128)S(1)}, u32[]{:S(2)}, u32[]{:S(2)}) collective-permute-start(f32[384,128]{1,0:T(8,128)S(1)} %add_add_fusion), channel_id=1, source_target_pairs={{0,1},{2,3},{16,17},{18,19},{4,5},{6,7},{20,21},{22,23},{8,9},{10,... | collective-permute-start | bytes 589832 | tf_op jit(solution)/shard_map/ppermute | solution.py:387
  67.6 2.2 %copy-start = (f32[768,1536]{1,0:T(8,128)}, f32[768,1536]{1,0:T(8,128)S(1)}, u32[]{:S(2)}) copy-start(f32[768,1536]{1,0:T(8,128)S(1)} %get-tuple-element.42.a_ref) | copy-start | bytes 14155780
  69.8 5.8 %copy-start.1 = (f32[768,1536]{1,0:T(8,128)S(1)}, f32[768,1536]{1,0:T(8,128)}, u32[]{:S(2)}) copy-start(f32[768,1536]{1,0:T(8,128)} %copy-done) | copy-start | bytes 14155780
  69.9 5.8 %collective-permute-start.11 = (f32[64,32,128]{2,1,0:T(8,128)S(1)}, f32[64,32,128]{2,1,0:T(8,128)S(1)}, u32[]{:S(2)}, u32[]{:S(2)}) collective-permute-start(f32[64,32,128]{2,1,0:T(8,128)S(1)} %share.1), channel_id=1, source_target_pairs={{0,1},{1,0},{2,3},{3,2},{4,5},{5,4},{6,7},{7,6},{8,9},{9,8},{10,11... | collective-permute-start | bytes 3145736 | tf_op jit(solution)/shard_map/ppermute | solution.py:445
